TPU v7x, 32 devices: a whole 2x2x4 slice. The times are simulated.
32 devices in a mesh: pb: 2 (over core), pa: 16 (over z, y, x).
Axes of the slice: x: 2, y: 2, z: 4, core: 2. Of those that a mesh axis runs over, the one named last changes fastest.
Arguments:
- queries: bfloat16 [16, 256, 1024], P('pa', 'pb'), may hold values from -25 to 25
- passages: bfloat16 [16, 256, 1024], P('pa', 'pb'), may hold values from -17 to 17
- neighbor_lists: int32 [16, 7], P('pa'), may hold values from -1 to 15, as said below
- positives: int32 [16, 256], P('pa'), may hold values from 0 to 255
- weights: float32 [16, 256], P('pa'), may hold values from 2 to 20
Outputs:
- query_grad: float32 [16, 256, 1024], P('pa', 'pb')
- passage_grad: float32 [16, 256, 1024], P('pa', 'pb')
Inputs may be any that keep to these rules, and one draw needn't show every extreme that they name: `neighbor_lists`: row b begins with b; its other entries are distinct blocks within cyclic distance 3 of b, followed by -1 in the remaining slots; some row lists 7 blocks.
All inputs are finite; a program needn't handle non-finite values.
Results may differ from a plain program's by a relative error of at most 0.0045.
Values may be sent and summed in bfloat16 or wider, within the bound.
No kernel may reach another device: no remote copies, remote signals or barrier semaphores. Data moves between devices by JAX's collectives and lax.ppermute only.
A program may use at most 128 MiB of HBM per device.

v0:
```python
import math

import jax
import jax.numpy as jnp
from jax import lax
from jax.sharding import PartitionSpec as P


def from_behind(x, axis, by):
    peers = lax.axis_size(axis)
    return lax.ppermute(x, axis, [(i, (i + by) % peers) for i in range(peers)])


def combined_all(value, axis, join):
    pieces = jax.tree.map(lambda part: lax.all_gather(part, axis), value)
    head = jax.tree.map(lambda part: part[0], pieces)
    tail = jax.tree.map(lambda part: part[1:], pieces)
    running, _ = lax.scan(lambda running, share: (join(running, share), None), head, tail)
    return running


def score_rows(query_rows, block_rows):
    return jnp.einsum("qd,pd->qp", query_rows, block_rows, preferred_element_type=jnp.float32) * (
        1.0 / math.sqrt(query_rows.shape[1])
    )


def empty_rows(query_rows, block_rows):
    return jnp.full((query_rows.shape[0], block_rows.shape[0]), -jnp.inf, jnp.float32)


def multiply_rows(left_side, right_side):
    return jnp.dot(left_side, right_side, preferred_element_type=jnp.float32)


def skip_rows(left_side, right_side):
    return jnp.zeros((left_side.shape[0], right_side.shape[1]), jnp.float32)


def passage_piece(coeff, query_rows):
    return jnp.einsum("qp,qd->pd", coeff, query_rows, preferred_element_type=jnp.float32).astype(
        jnp.bfloat16
    )


def skip_piece(coeff, query_rows):
    return jnp.zeros((coeff.shape[1], query_rows.shape[1]), jnp.bfloat16)


def combine_totals(earlier, later):
    row_max = jnp.maximum(earlier[0], later[0])
    row_total = earlier[1] * jnp.exp(earlier[0] - row_max) + later[1] * jnp.exp(later[0] - row_max)
    return (row_max, row_total)


def body(queries, passages, neighbor_lists, positives, weights):
    feature_count = queries.shape[2]
    score_scale = 1.0 / math.sqrt(feature_count)
    reach_blocks = (neighbor_lists.shape[1] - 1) // 2
    block_count = lax.axis_size("pa")
    home_block = lax.axis_index("pa")
    member_index = lax.axis_index("pb")
    slab_rows = passages.shape[1]
    own_rows = passages[0]
    everyone = lax.all_gather(queries, "pb", axis=1, tiled=True)[0]
    offsets = list(range(-reach_blocks, reach_blocks + 1))
    listed = {}
    for offset in offsets:
        target = (home_block + offset) % block_count
        listed[offset] = jnp.any(neighbor_lists[0] == target)
    fetched = {0: own_rows}
    for offset in offsets:
        if offset != 0:
            fetched[offset] = from_behind(own_rows, "pa", -offset)
    scores = {}
    for offset in offsets:
        scores[offset] = lax.cond(listed[offset], score_rows, empty_rows, everyone, fetched[offset])
    row_max = jnp.max(jnp.stack([jnp.max(scores[offset], axis=1) for offset in offsets]), axis=0)
    row_total = jnp.zeros_like(row_max)
    for offset in offsets:
        row_total = row_total + jnp.sum(jnp.exp(scores[offset] - row_max[:, None]), axis=1)
    group_max, group_total = combined_all((row_max, row_total), "pb", combine_totals)
    log_total = group_max + jnp.log(group_total)
    local_positive = positives[0] - member_index * slab_rows
    onehot = (jnp.arange(slab_rows, dtype=jnp.int32)[None, :] == local_positive[:, None]).astype(
        jnp.float32
    )
    query_weight = weights[0][:, None]
    coeffs = {}
    for offset in offsets:
        probs = jnp.exp(scores[offset] - log_total[:, None])
        if offset == 0:
            probs = probs - onehot
        coeffs[offset] = (query_weight * probs * score_scale).astype(jnp.bfloat16)
    partial_value = jnp.zeros((queries.shape[1] * lax.axis_size("pb"), feature_count), jnp.float32)
    for query_offset in offsets:
        piece = coeffs[query_offset]
        partial_value = partial_value + lax.cond(
            listed[query_offset], multiply_rows, skip_rows, piece, fetched[query_offset]
        )
    query_grad = lax.psum_scatter(partial_value, "pb", scatter_dimension=0, tiled=True)
    terms = {}
    for offset in offsets:
        terms[offset] = lax.cond(
            listed[offset], passage_piece, skip_piece, coeffs[offset], everyone
        )
    passage_grad = terms[0].astype(jnp.float32)
    for offset in offsets:
        if offset != 0:
            arrived = from_behind(terms[offset], "pa", offset)
            passage_grad = passage_grad + arrived.astype(jnp.float32)
    return (query_grad[None], passage_grad[None])


def solution(mesh):
    return jax.shard_map(
        body,
        mesh=mesh,
        in_specs=(
            P("pa", "pb", None),
            P("pa", "pb", None),
            P("pa", None),
            P("pa", None),
            P("pa", None),
        ),
        out_specs=(P("pa", "pb", None), P("pa", "pb", None)),
        check_vma=False,
    )
```

profile of v0, /device:TPU:18, one launch (start us, length us, event | category | flops | bytes accessed | tf_op | source)
XLA Modules:
  0.0 112.7 jit_solution(17374742718329827217)
XLA Ops:
  7.2 1.6 %collective-permute-start = (bf16[128,1024]{1,0:T(8,128)(2,1)}, bf16[128,1024]{1,0:T(8,128)(2,1)S(1)}, u32[]{:S(2)}, u32[]{:S(2)}) collective-permute-start(bf16[128,1024]{1,0:T(8,128)(2,1)} %bitcast.77), channel_id=1, source_target_pairs={{0,3},{1,4},{2,5},{3,6},{4,7},{5,8},{6,9},{7,10},{8,11},{9,12},{10... | collective-permute-start | bytes 786440 | tf_op jit(solution)/shard_map/ppermute | solution.py:11
  8.8 2.3 %collective-permute-start.5 = (bf16[128,1024]{1,0:T(8,128)(2,1)}, bf16[128,1024]{1,0:T(8,128)(2,1)S(1)}, u32[]{:S(2)}, u32[]{:S(2)}) collective-permute-start(bf16[128,1024]{1,0:T(8,128)(2,1)} %bitcast.78), channel_id=1, source_target_pairs={{0,13},{1,14},{2,15},{3,0},{4,1},{5,2},{6,3},{7,4},{8,5},{9,6},{10... | collective-permute-start | bytes 786440 | tf_op jit(solution)/shard_map/ppermute | solution.py:11
  12.1 2.4 %collective-permute-start.2 = (bf16[128,1024]{1,0:T(8,128)(2,1)}, bf16[128,1024]{1,0:T(8,128)(2,1)}, u32[]{:S(2)}, u32[]{:S(2)}) collective-permute-start(bf16[128,1024]{1,0:T(8,128)(2,1)} %bitcast.81), channel_id=1, source_target_pairs={{0,1},{1,2},{2,3},{3,4},{4,5},{5,6},{6,7},{7,8},{8,9},{9,10},{10,1... | collective-permute-start | bytes 786440 | tf_op jit(solution)/shard_map/ppermute | solution.py:11
  14.5 2.5 %all_gather.11 = bf16[1,256,1024]{2,1,0:T(8,128)(2,1)S(1)} all-gather(bf16[1,128,1024]{2,1,0:T(8,128)(2,1)} %param.47), channel_id=1, replica_groups=mesh['pb'=2,'pa'=16] {'pb'}, dimensions={1}, use_global_device_ids=true | all-gather | bytes 786432 | tf_op jit(solution)/shard_map/all_gather | solution.py:65
  17.0 1.8 %collective-permute-done = bf16[128,1024]{1,0:T(8,128)(2,1)S(1)} collective-permute-done((bf16[128,1024]{1,0:T(8,128)(2,1)}, bf16[128,1024]{1,0:T(8,128)(2,1)S(1)}, u32[]{:S(2)}, u32[]{:S(2)}) %collective-permute-start) | collective-permute-done | bytes 262176 | tf_op jit(solution)/shard_map/ppermute | solution.py:11
  18.9 5.8 %collective-permute-start.1 = (bf16[128,1024]{1,0:T(8,128)(2,1)S(1)}, bf16[128,1024]{1,0:T(8,128)(2,1)S(1)}, u32[]{:S(2)}, u32[]{:S(2)}) collective-permute-start(bf16[128,1024]{1,0:T(8,128)(2,1)S(1)} %bitcast.82), channel_id=1, source_target_pairs={{0,2},{1,3},{2,4},{3,5},{4,6},{5,7},{6,8},{7,9},{8,10},{9,11},{10,... | collective-permute-start | bytes 786440 | tf_op jit(solution)/shard_map/ppermute | solution.py:11
  24.7 0.8 compare_reduce_fusion.5
  29.9 1.6 %conditional.24 = (f32[256,128]{0,1:T(8,128)S(1)}, f32[256]{0:T(256)}, f32[1,256]{1,0:T(1,128)S(1)}) conditional(s32[]{:T(128)} %convert_element_type.107, () %tuple.173, (bf16[256,1024]{1,0:T(8,128)(2,1)S(1)}, bf16[128,1024]{1,0:T(8,128)(2,1)S(1)}) %tuple.294), branch_computations={%region_13.14_spmd, %region_14.16_spmd} | conditional | flops 67174144 | bytes 920600 | solution.py:77
  29.9 0.9 fusion.6
  30.8 0.7 copy.50
  31.6 0.7 copy-done.10
  32.3 1.6 %conditional.21 = (f32[256,128]{0,1:T(8,128)S(1)}, f32[256]{0:T(256)}, f32[1,256]{1,0:T(1,128)S(1)}) conditional(s32[]{:T(128)} %convert_element_type.104, () %tuple.167, (bf16[256,1024]{1,0:T(8,128)(2,1)S(1)}, bf16[128,1024]{1,0:T(8,128)(2,1)S(1)}) %tuple.281), branch_computations={%region_1.2_spmd, %region_2.4_spmd} | conditional | flops 67174144 | bytes 920600 | solution.py:77
  32.3 0.9 fusion.3
  33.2 0.7 copy.62
  33.9 4.3 %collective-permute-done.1 = bf16[128,1024]{1,0:T(8,128)(2,1)S(1)} collective-permute-done((bf16[128,1024]{1,0:T(8,128)(2,1)S(1)}, bf16[128,1024]{1,0:T(8,128)(2,1)S(1)}, u32[]{:S(2)}, u32[]{:S(2)}) %collective-permute-start.1) | collective-permute-done | bytes 262176 | tf_op jit(solution)/shard_map/ppermute | solution.py:11
  38.3 1.6 %conditional.22 = (f32[256,128]{0,1:T(8,128)S(1)}, f32[256]{0:T(256)}, f32[1,256]{1,0:T(1,128)S(1)}) conditional(s32[]{:T(128)} %convert_element_type.105, () %tuple.169, (bf16[256,1024]{1,0:T(8,128)(2,1)S(1)}, bf16[128,1024]{1,0:T(8,128)(2,1)S(1)}) %tuple.282), branch_computations={%region_5.6_spmd, %region_6.8_spmd} | conditional | flops 67174144 | bytes 920600 | solution.py:77
  38.3 0.9 fusion.4
  39.1 0.7 copy.26
  42.8 0.8 copy.20
  43.5 0.7 maximum_maximum_fusion
  44.4 1.8 %all-gather.2 = f32[2,1,256]{2,1,0:T(1,128)S(1)} all-gather(f32[1,1,256]{2,1,0:T(1,128)S(1)} %bitcast.90), channel_id=2, replica_groups=mesh['pb'=2,'pa'=16] {'pb'}, dimensions={0}, use_global_device_ids=true | all-gather | bytes 3072 | tf_op jit(solution)/shard_map/all_gather | solution.py:15
  46.2 1.8 %all-gather.1 = f32[2,1,256]{2,1,0:T(1,128)S(1)} all-gather(f32[1,1,256]{2,1,0:T(1,128)S(1)} %maximum_bitcast_fusion), channel_id=1, replica_groups=mesh['pb'=2,'pa'=16] {'pb'}, dimensions={0}, use_global_device_ids=true | all-gather | bytes 3072 | tf_op jit(solution)/shard_map/all_gather | solution.py:15
  48.0 0.7 copy-done.9
  48.7 0.9 multiply_convert_fusion.5
  50.7 1.1 %conditional.32 = (f32[256,1024]{1,0:T(8,128)}) conditional(s32[]{:T(128)} %convert_element_type.108, () %tuple.188, (bf16[256,128]{1,0:T(8,128)(2,1)}, bf16[128,1024]{1,0:T(8,128)(2,1)}) %tuple.189), branch_computations={%region_43.44_spmd, %region_44.45_spmd} | conditional | flops 67108864 | bytes 1376264 | solution.py:98
  50.7 1.1 broadcast.119
  51.8 1.1 conditional.33
  51.8 1.1 broadcast.120
  52.9 1.1 %conditional.34 = (f32[256,1024]{1,0:T(8,128)}) conditional(s32[]{:T(128)} %convert_element_type.110, () %tuple.192, (bf16[256,128]{1,0:T(8,128)(2,1)}, bf16[128,1024]{1,0:T(8,128)(2,1)S(1)}) %tuple.193), branch_computations={%region_47.48_spmd, %region_48.49_spmd} | conditional | flops 67108864 | bytes 1376264 | solution.py:98
  52.9 1.1 broadcast.121
  54.0 1.3 %conditional.28 = (f32[256,1024]{1,0:T(8,128)}) conditional(s32[]{:T(128)} %convert_element_type.104, () %tuple.166, (bf16[256,128]{1,0:T(8,128)(2,1)S(1)}, bf16[128,1024]{1,0:T(8,128)(2,1)S(1)}) %tuple.181), branch_computations={%region_35.36_spmd, %region_36.37_spmd} | conditional | flops 67108864 | bytes 1376264 | solution.py:98
  54.0 1.3 %fusion.12 = f32[256,1024]{1,0:T(8,128)} fusion(bf16[256,128]{1,0:T(8,128)(2,1)S(1)} %get-tuple-element.177, bf16[128,1024]{1,0:T(8,128)(2,1)S(1)} %get-tuple-element.178), kind=kOutput, calls=%fused_computation.56 | convolution fusion | flops 67108864 | bytes 1376256 | tf_op jit(solution)/shard_map/cond/branch_1_fun/dot_general | solution.py:33
  55.3 1.3 %conditional.31 = (f32[256,1024]{1,0:T(8,128)}) conditional(s32[]{:T(128)} %convert_element_type.107, () %tuple.186, (bf16[256,128]{1,0:T(8,128)(2,1)S(1)}, bf16[128,1024]{1,0:T(8,128)(2,1)S(1)}) %tuple.295), branch_computations={%region_41.42_spmd, %region_42.43_spmd} | conditional | flops 67108864 | bytes 1376264 | solution.py:98
  55.3 1.3 %fusion.15 = f32[256,1024]{1,0:T(8,128)} fusion(bf16[256,128]{1,0:T(8,128)(2,1)S(1)} %get-tuple-element.183, bf16[128,1024]{1,0:T(8,128)(2,1)S(1)} %get-tuple-element.184), kind=kOutput, calls=%fused_computation.59 | convolution fusion | flops 67108864 | bytes 1376256 | tf_op jit(solution)/shard_map/cond/branch_1_fun/dot_general | solution.py:33
  56.6 4.3 %add_add_fusion = f32[256,1024]{1,0:T(8,128)} fusion(f32[256,1024]{1,0:T(8,128)} %get-tuple-element.336, f32[256,1024]{1,0:T(8,128)} %get-tuple-element.335, f32[256,1024]{1,0:T(8,128)} %get-tuple-element.334, f32[256,1024]{1,0:T(8,128)} %get-tuple-element.333, f32[256,1024]{1,0:T(8,128)S(1)} %get-tuple-element.332, f32[256,1024]{1,0:T(8,128)} %get-tuple-element.330, ...), kind=kLoop, calls=%fused_computation.15 | loop fusion | flops 1572864 | bytes 8388608 | tf_op jit(solution)/shard_map/add | solution.py:98
  60.9 0.8 copy-done.6
  62.0 6.7 %collective-permute-start.7 = (bf16[128,1024]{1,0:T(8,128)(2,1)S(1)}, bf16[128,1024]{1,0:T(8,128)(2,1)S(1)}, u32[]{:S(2)}, u32[]{:S(2)}) collective-permute-start(bf16[128,1024]{1,0:T(8,128)(2,1)S(1)} %get-tuple-element.339), channel_id=1, source_target_pairs={{0,14},{1,15},{2,0},{3,1},{4,2},{5,3},{6,4},{7,5},{8,6},{9,7},{10,... | collective-permute-start | bytes 786440 | tf_op jit(solution)/shard_map/ppermute | solution.py:11
  68.7 0.8 copy-done.3
  69.6 0.8 copy-done.2
  70.4 2.2 %collective-permute-start.9 = (bf16[128,1024]{1,0:T(8,128)(2,1)S(1)}, bf16[128,1024]{1,0:T(8,128)(2,1)S(1)}, u32[]{:S(2)}, u32[]{:S(2)}) collective-permute-start(bf16[128,1024]{1,0:T(8,128)(2,1)S(1)} %get-tuple-element.341), channel_id=1, source_target_pairs={{0,1},{1,2},{2,3},{3,4},{4,5},{5,6},{6,7},{7,8},{8,9},{9,10},{10,1... | collective-permute-start | bytes 786440 | tf_op jit(solution)/shard_map/ppermute | solution.py:11
  72.6 8.7 %collective-permute-start.10 = (bf16[128,1024]{1,0:T(8,128)(2,1)S(1)}, bf16[128,1024]{1,0:T(8,128)(2,1)S(1)}, u32[]{:S(2)}, u32[]{:S(2)}) collective-permute-start(bf16[128,1024]{1,0:T(8,128)(2,1)S(1)} %get-tuple-element.342), channel_id=1, source_target_pairs={{0,2},{1,3},{2,4},{3,5},{4,6},{5,7},{6,8},{7,9},{8,10},{9,11},{10,... | collective-permute-start | bytes 786440 | tf_op jit(solution)/shard_map/ppermute | solution.py:11
  81.3 0.7 conditional.41
  81.3 0.7 broadcast.128
  82.8 0.7 copy-done.8
  83.5 11.9 %collective-permute-done.7 = bf16[128,1024]{1,0:T(8,128)(2,1)S(1)} collective-permute-done((bf16[128,1024]{1,0:T(8,128)(2,1)S(1)}, bf16[128,1024]{1,0:T(8,128)(2,1)S(1)}, u32[]{:S(2)}, u32[]{:S(2)}) %collective-permute-start.7) | collective-permute-done | bytes 262176 | tf_op jit(solution)/shard_map/ppermute | solution.py:11
  95.7 3.7 %collective-permute-done.10 = bf16[128,1024]{1,0:T(8,128)(2,1)S(1)} collective-permute-done((bf16[128,1024]{1,0:T(8,128)(2,1)S(1)}, bf16[128,1024]{1,0:T(8,128)(2,1)S(1)}, u32[]{:S(2)}, u32[]{:S(2)}) %collective-permute-start.10) | collective-permute-done | bytes 262176 | tf_op jit(solution)/shard_map/ppermute | solution.py:11
  99.4 5.4 %collective-permute-done.6 = bf16[128,1024]{1,0:T(8,128)(2,1)S(1)} collective-permute-done((bf16[128,1024]{1,0:T(8,128)(2,1)}, bf16[128,1024]{1,0:T(8,128)(2,1)S(1)}, u32[]{:S(2)}, u32[]{:S(2)}) %collective-permute-start.6) | collective-permute-done | bytes 262176 | tf_op jit(solution)/shard_map/ppermute | solution.py:11
  104.8 1.1 add_bitcast_fusion
  (78 shorter events, 10.3 us)
Async XLA Ops:
  7.2 98.7 %reduce-scatter.2.cloned.1.call-start = ((), (), s32[]{:S(2)}) async-start(), calls=%async_computation.1 | async-start | bytes 1572864 | tf_op jit(solution)/shard_map/reduce_scatter | solution.py:101
  7.2 11.7 %collective-permute-start = (bf16[128,1024]{1,0:T(8,128)(2,1)}, bf16[128,1024]{1,0:T(8,128)(2,1)S(1)}, u32[]{:S(2)}, u32[]{:S(2)}) collective-permute-start(bf16[128,1024]{1,0:T(8,128)(2,1)} %bitcast.77), channel_id=1, source_target_pairs={{0,3},{1,4},{2,5},{3,6},{4,7},{5,8},{6,9},{7,10},{8,11},{9,12},{10... | collective-permute-start | bytes 786440 | tf_op jit(solution)/shard_map/ppermute | solution.py:11
  8.8 33.3 %collective-permute-start.5 = (bf16[128,1024]{1,0:T(8,128)(2,1)}, bf16[128,1024]{1,0:T(8,128)(2,1)S(1)}, u32[]{:S(2)}, u32[]{:S(2)}) collective-permute-start(bf16[128,1024]{1,0:T(8,128)(2,1)} %bitcast.78), channel_id=1, source_target_pairs={{0,13},{1,14},{2,15},{3,0},{4,1},{5,2},{6,3},{7,4},{8,5},{9,6},{10... | collective-permute-start | bytes 786440 | tf_op jit(solution)/shard_map/ppermute | solution.py:11
  11.1 30.3 %collective-permute-start.4 = (bf16[128,1024]{1,0:T(8,128)(2,1)}, bf16[128,1024]{1,0:T(8,128)(2,1)}, u32[]{:S(2)}, u32[]{:S(2)}) collective-permute-start(bf16[128,1024]{1,0:T(8,128)(2,1)} %bitcast.79), channel_id=1, source_target_pairs={{0,14},{1,15},{2,0},{3,1},{4,2},{5,3},{6,4},{7,5},{8,6},{9,7},{10,... | collective-permute-start | bytes 786440 | tf_op jit(solution)/shard_map/ppermute | solution.py:11
  11.6 29.1 %collective-permute-start.3 = (bf16[128,1024]{1,0:T(8,128)(2,1)}, bf16[128,1024]{1,0:T(8,128)(2,1)}, u32[]{:S(2)}, u32[]{:S(2)}) collective-permute-start(bf16[128,1024]{1,0:T(8,128)(2,1)} %bitcast.80), channel_id=1, source_target_pairs={{0,15},{1,0},{2,1},{3,2},{4,3},{5,4},{6,5},{7,6},{8,7},{9,8},{10,9... | collective-permute-start | bytes 786440 | tf_op jit(solution)/shard_map/ppermute | solution.py:11
  12.1 27.8 %collective-permute-start.2 = (bf16[128,1024]{1,0:T(8,128)(2,1)}, bf16[128,1024]{1,0:T(8,128)(2,1)}, u32[]{:S(2)}, u32[]{:S(2)}) collective-permute-start(bf16[128,1024]{1,0:T(8,128)(2,1)} %bitcast.81), channel_id=1, source_target_pairs={{0,1},{1,2},{2,3},{3,4},{4,5},{5,6},{6,7},{7,8},{8,9},{9,10},{10,1... | collective-permute-start | bytes 786440 | tf_op jit(solution)/shard_map/ppermute | solution.py:11
  14.5 4.4 %copy-start = (bf16[1,128,1024]{2,1,0:T(8,128)(2,1)S(1)}, bf16[1,128,1024]{2,1,0:T(8,128)(2,1)}, u32[]{:S(2)}) copy-start(bf16[1,128,1024]{2,1,0:T(8,128)(2,1)} %param.48) | copy-start | bytes 786436
  14.5 10.2 %copy-start.11 = (s32[1,7]{1,0:T(1,128)S(1)}, s32[1,7]{1,0:T(1,128)}, u32[]{:S(2)}) copy-start(s32[1,7]{1,0:T(1,128)} %param.49) | copy-start | bytes 88
  18.9 19.4 %collective-permute-start.1 = (bf16[128,1024]{1,0:T(8,128)(2,1)S(1)}, bf16[128,1024]{1,0:T(8,128)(2,1)S(1)}, u32[]{:S(2)}, u32[]{:S(2)}) collective-permute-start(bf16[128,1024]{1,0:T(8,128)(2,1)S(1)} %bitcast.82), channel_id=1, source_target_pairs={{0,2},{1,3},{2,4},{3,5},{4,6},{5,7},{6,8},{7,9},{8,10},{9,11},{10,... | collective-permute-start | bytes 786440 | tf_op jit(solution)/shard_map/ppermute | solution.py:11
  31.6 0.7 copy-start.10
  44.2 3.8 %copy-start.7 = (f32[256,128]{1,0:T(8,128)S(1)}, f32[256,128]{1,0:T(8,128)}, u32[]{:S(2)}) copy-start(f32[256,128]{1,0:T(8,128)} %copy.20) | copy-start | bytes 393220
  48.0 0.7 copy-start.9
  49.6 0.6 copy-start.5
  60.9 0.8 copy-start.6
  61.7 7.0 %copy-start.4 = (bf16[256,128]{1,0:T(8,128)(2,1)S(1)}, bf16[256,128]{1,0:T(8,128)(2,1)}, u32[]{:S(2)}) copy-start(bf16[256,128]{1,0:T(8,128)(2,1)} %get-tuple-element.278) | copy-start | bytes 196612
  62.0 33.4 %collective-permute-start.7 = (bf16[128,1024]{1,0:T(8,128)(2,1)S(1)}, bf16[128,1024]{1,0:T(8,128)(2,1)S(1)}, u32[]{:S(2)}, u32[]{:S(2)}) collective-permute-start(bf16[128,1024]{1,0:T(8,128)(2,1)S(1)} %get-tuple-element.339), channel_id=1, source_target_pairs={{0,14},{1,15},{2,0},{3,1},{4,2},{5,3},{6,4},{7,5},{8,6},{9,7},{10,... | collective-permute-start | bytes 786440 | tf_op jit(solution)/shard_map/ppermute | solution.py:11
  68.7 0.8 copy-start.3
  69.5 0.8 copy-start.2
  69.5 26.1 %collective-permute-start.8 = (bf16[128,1024]{1,0:T(8,128)(2,1)S(1)}, bf16[128,1024]{1,0:T(8,128)(2,1)S(1)}, u32[]{:S(2)}, u32[]{:S(2)}) collective-permute-start(bf16[128,1024]{1,0:T(8,128)(2,1)S(1)} %get-tuple-element.340), channel_id=1, source_target_pairs={{0,15},{1,0},{2,1},{3,2},{4,3},{5,4},{6,5},{7,6},{8,7},{9,8},{10,9... | collective-permute-start | bytes 786440 | tf_op jit(solution)/shard_map/ppermute | solution.py:11
  70.4 2.2 %copy-start.1 = (bf16[256,128]{1,0:T(8,128)(2,1)S(1)}, bf16[256,128]{1,0:T(8,128)(2,1)}, u32[]{:S(2)}) copy-start(bf16[256,128]{1,0:T(8,128)(2,1)} %get-tuple-element.282) | copy-start | bytes 196612
  70.4 25.3 %collective-permute-start.9 = (bf16[128,1024]{1,0:T(8,128)(2,1)S(1)}, bf16[128,1024]{1,0:T(8,128)(2,1)S(1)}, u32[]{:S(2)}, u32[]{:S(2)}) collective-permute-start(bf16[128,1024]{1,0:T(8,128)(2,1)S(1)} %get-tuple-element.341), channel_id=1, source_target_pairs={{0,1},{1,2},{2,3},{3,4},{4,5},{5,6},{6,7},{7,8},{8,9},{9,10},{10,1... | collective-permute-start | bytes 786440 | tf_op jit(solution)/shard_map/ppermute | solution.py:11
  72.6 26.7 %collective-permute-start.10 = (bf16[128,1024]{1,0:T(8,128)(2,1)S(1)}, bf16[128,1024]{1,0:T(8,128)(2,1)S(1)}, u32[]{:S(2)}, u32[]{:S(2)}) collective-permute-start(bf16[128,1024]{1,0:T(8,128)(2,1)S(1)} %get-tuple-element.342), channel_id=1, source_target_pairs={{0,2},{1,3},{2,4},{3,5},{4,6},{5,7},{6,8},{7,9},{8,10},{9,11},{10,... | collective-permute-start | bytes 786440 | tf_op jit(solution)/shard_map/ppermute | solution.py:11
  82.0 17.3 %collective-permute-start.11 = (bf16[128,1024]{1,0:T(8,128)(2,1)}, bf16[128,1024]{1,0:T(8,128)(2,1)S(1)}, u32[]{:S(2)}, u32[]{:S(2)}) collective-permute-start(bf16[128,1024]{1,0:T(8,128)(2,1)} %get-tuple-element.343), channel_id=1, source_target_pairs={{0,3},{1,4},{2,5},{3,6},{4,7},{5,8},{6,9},{7,10},{8,11},{9,12},{10... | collective-permute-start | bytes 786440 | tf_op jit(solution)/shard_map/ppermute | solution.py:11
  82.8 0.7 copy-start.8
  95.4 9.4 %collective-permute-start.6 = (bf16[128,1024]{1,0:T(8,128)(2,1)}, bf16[128,1024]{1,0:T(8,128)(2,1)S(1)}, u32[]{:S(2)}, u32[]{:S(2)}) collective-permute-start(bf16[128,1024]{1,0:T(8,128)(2,1)} %copy-done.8), channel_id=1, source_target_pairs={{0,13},{1,14},{2,15},{3,0},{4,1},{5,2},{6,3},{7,4},{8,5},{9,6},{10... | collective-permute-start | bytes 786440 | tf_op jit(solution)/shard_map/ppermute | solution.py:11
Sparse Core Ops, SparseCore 0:
  61.0 20.9 reduce-scatter.1
where the time goes:
time: 114 us; the launch traced here: 113 us
  starting transfers between devices  31.3 us (27%)
  waiting for transfers between devices  27.2 us (24%)
  between operations  18.7 us (16%)
  local copies, waits for them, and re-layouts  15 us (13%)
  other arithmetic  7.95 us (7%)
  matrix products  6.24 us (5%)
  blocking collectives  6.08 us (5%)
    ppermute x12, starting transfers between devices, from_behind(): return lax.ppermute(x, axis, [(i, (i + by) % peers) for i in range(peers)])  31.3 us
    ppermute x12, waiting for transfers between devices, from_behind(): return lax.ppermute(x, axis, [(i, (i + by) % peers) for i in range(peers)])  27.2 us
    unnamed x24, local copies, waits for them, and re-layouts  5.11 us
    another operation x12, local copies, waits for them, and re-layouts  4.28 us
    add x1, other arithmetic, body(): partial_value + lax.cond(listed[query_offset], multiply_rows, skip_rows,...  4.28 us
    all_gather x2, blocking collectives, combined_all(): pieces = jax.tree.map(lambda part: lax.all_gather(part, axis), value)  3.57 us
    dot_general x3, matrix products, multiply_rows(): return jnp.dot(left_side, right_side, preferred_element_type=jnp.float32)  2.81 us
    dot_general x3, matrix products, score_rows(): jnp.einsum('qd,pd->qp', query_rows, block_rows, preferred_element_type=jn...  2.69 us
  transfers between devices with their start and end apart: 13, of which 5 were waited for; matrix products, arithmetic and copies ran while one was open for 9% of the time, Pallas kernels for 0%

commit v1 on v0

v1 whole, which is shorter than its diff:
```python
import math

import jax
import jax.numpy as jnp
from jax import lax
from jax.experimental import pallas as pl
from jax.experimental.pallas import tpu as pltpu
from jax.sharding import PartitionSpec as P

F32 = jnp.float32
BF16 = jnp.bfloat16
WINDOW = 7
LSE_ROW, WEIGHT_ROW, LIST_ROW, STAT_ROWS = 0, 1, 2, 8


def group_shift(i, step, count):
    return (i + step + count) % count


def relay_tables(count):
    every = range(count)
    return {
        "x": [(i, i ^ 1) for i in every],
        "y": [(i, i ^ 2) for i in every],
        "d": [(i, i ^ 3) for i in every],
        "za": [(i, group_shift(i, -4 if i & 2 else 4, count)) for i in every],
        "zb": [(i, group_shift(i, -4 if i & 1 else 4, count)) for i in every],
        "up": [(i, group_shift(i, 4, count)) for i in every],
        "down": [(i, group_shift(i, -4, count)) for i in every],
    }


def window_ids(i, count):
    to_y = jnp.where((i & 2) != 0, 4, -4)
    to_x = jnp.where((i & 1) != 0, 4, -4)
    return [
        i,
        i ^ 1,
        i ^ 2,
        i ^ 3,
        ((i ^ 2) + to_y + count) % count,
        ((i ^ 1) + to_x + count) % count,
        ((i ^ 3) + to_y + count) % count,
    ]


def nt_dot(a, b):
    return lax.dot_general(a, b, (((1,), (1,)), ((), ())), preferred_element_type=F32)


def tn_dot(a, b):
    return lax.dot_general(a, b, (((0,), (0,)), ((), ())), preferred_element_type=F32)


def scores_kernel(count, lists, q_ref, *refs):
    p_refs, (s_ref, ml_ref) = refs[:WINDOW], refs[WINDOW:]
    rows = p_refs[0].shape[0]
    scale = 1.0 / math.sqrt(q_ref.shape[1])
    ids = window_ids(lax.axis_index("pa"), count)
    top = None
    for t in range(WINDOW):
        hit = lists[0, 0] == ids[t]
        for s in range(1, lists.shape[1]):
            hit = jnp.logical_or(hit, lists[0, s] == ids[t])
        bias = jnp.where(hit, 0.0, -jnp.inf).astype(F32)
        part = nt_dot(p_refs[t][...], q_ref[...]) * scale + bias
        s_ref[t * rows : (t + 1) * rows, :] = part
        part_top = jnp.max(part, axis=0, keepdims=True)
        top = part_top if top is None else jnp.maximum(top, part_top)
    total = jnp.zeros_like(top)
    for t in range(WINDOW):
        total += jnp.sum(jnp.exp(s_ref[t * rows : (t + 1) * rows, :] - top), axis=0, keepdims=True)
    ml_ref[...] = jnp.zeros_like(ml_ref)
    ml_ref[0:1, :] = top
    ml_ref[1:2, :] = total


def query_kernel(pb, s_ref, stat_ref, w_ref, pos_ref, *refs):
    p_refs, outs, coeff = refs[:WINDOW], refs[WINDOW:-1], refs[-1]
    rows = p_refs[0].shape[0]
    scale = 1.0 / math.sqrt(p_refs[0].shape[1])
    me = lax.axis_index("pb")
    lse = stat_ref[LSE_ROW : LSE_ROW + 1, :]
    w = w_ref[...]
    row = lax.broadcasted_iota(jnp.int32, (rows, s_ref.shape[1]), 0)
    for t in range(WINDOW):
        prob = jnp.exp(s_ref[t * rows : (t + 1) * rows, :] - lse)
        if t == 0:
            prob = prob - (row == pos_ref[...] - me * rows).astype(F32)
        coeff[t * rows : (t + 1) * rows, :] = (w * prob * scale).astype(BF16)
    for r in range(pb):
        lanes = pl.ds(pl.multiple_of(((me + r) % pb) * rows, rows), rows)
        total = None
        for t in range(WINDOW):
            part = tn_dot(coeff[t * rows : (t + 1) * rows, lanes], p_refs[t][...])
            total = part if total is None else total + part
        outs[r][...] = total.astype(outs[r].dtype)


def cross_kernel(p_ref, *refs):
    q_refs, s_ref = refs[:-1], refs[-1]
    rows = p_ref.shape[0]
    scale = 1.0 / math.sqrt(p_ref.shape[1])
    for n, q_ref in enumerate(q_refs):
        s_ref[:, n * rows : (n + 1) * rows] = nt_dot(p_ref[...], q_ref[...]) * scale


def passage_kernel(pb, s_ref, stat_ref, pos_ref, *refs):
    q_refs, out_ref = refs[:-1], refs[-1]
    rows = out_ref.shape[0]
    scale = 1.0 / math.sqrt(out_ref.shape[1])
    me, home = lax.axis_index("pb"), lax.axis_index("pa").astype(F32)
    row = lax.broadcasted_iota(jnp.int32, (rows, rows), 0)
    total = None
    for t in range(WINDOW):
        lists = stat_ref[t, LIST_ROW : LIST_ROW + 1, :]
        hit = jnp.max(jnp.where(lists == home, 1.0, 0.0), axis=1, keepdims=True) > 0.5
        for r in range(pb):
            n = t * pb + r
            lanes = pl.ds(pl.multiple_of(((me - r + pb) % pb) * rows, rows), rows)
            lse = stat_ref[t, LSE_ROW : LSE_ROW + 1, lanes]
            w = stat_ref[t, WEIGHT_ROW : WEIGHT_ROW + 1, lanes]
            prob = jnp.exp(s_ref[:, n * rows : (n + 1) * rows] - lse)
            if t == 0:
                prob = prob - (row == pos_ref[:, lanes] - me * rows).astype(F32)
            value = jnp.where(hit, w * prob * scale, 0.0).astype(BF16)
            part = jnp.dot(value, q_refs[n][...], preferred_element_type=F32)
            total = part if total is None else total + part
    out_ref[...] = total


VMEM = pl.BlockSpec(memory_space=pltpu.VMEM)
SMEM = pl.BlockSpec(memory_space=pltpu.SMEM)


def call(kernel, outs, specs, args, flops, scratch=()):
    moved = sum(a.size * a.dtype.itemsize for a in (*args, *outs))
    return pl.pallas_call(
        kernel,
        out_shape=outs,
        in_specs=specs,
        out_specs=[VMEM] * len(outs),
        scratch_shapes=list(scratch),
        cost_estimate=pl.CostEstimate(flops=flops, bytes_accessed=moved, transcendentals=0),
        compiler_params=pltpu.CompilerParams(vmem_limit_bytes=32 * 1024 * 1024),
    )(*args)


def body(queries, passages, neighbor_lists, positives, weights):
    pb, count = lax.axis_size("pb"), lax.axis_size("pa")
    own_q, own_p = queries[0], passages[0]
    rows, width = own_p.shape
    q_rows = rows * pb
    tables = relay_tables(count)

    def move(value, name):
        return lax.ppermute(value, "pa", tables[name])

    def from_member(value, by):
        return lax.ppermute(value, "pb", [(i, (i + by) % pb) for i in range(pb)])

    def relay(own):
        x, y = move(own, "x"), move(own, "y")
        za, zb, d = move(y, "za"), move(x, "zb"), move(x, "y")
        return [own, x, y, d, za, zb, move(za, "x")]

    full_q = lax.all_gather(own_q, "pb", axis=0, tiled=True)
    window_p = relay(own_p)
    window_q = relay(own_q)
    flops = 2 * WINDOW * rows * q_rows * width

    def shape(dims, dtype):
        return jax.ShapeDtypeStruct(dims, dtype)

    scores, ml = call(
        lambda *refs: scores_kernel(count, *refs),
        [shape((WINDOW * rows, q_rows), F32), shape((8, q_rows), F32)],
        [SMEM] + [VMEM] * (1 + WINDOW),
        [neighbor_lists, full_q, *window_p],
        flops,
    )
    top, total = ml[0], ml[1]
    for r in range(1, pb):
        other = from_member(ml, r)
        joint = jnp.maximum(top, other[0])
        total = total * jnp.exp(top - joint) + other[1] * jnp.exp(other[0] - joint)
        top = joint
    log_total = top + jnp.log(total)
    lists = jnp.pad(neighbor_lists[0].astype(F32), (0, q_rows - neighbor_lists.shape[1]), constant_values=-1.0)
    stat = jnp.pad(jnp.stack([log_total, weights[0], lists]), ((0, STAT_ROWS - 3), (0, 0)))

    up, down = move(stat, "up"), move(stat, "down")
    trio = jnp.stack([stat, up, down])
    trio_x, trio_y, trio_d = move(trio, "x"), move(trio, "y"), move(trio, "d")
    home = lax.axis_index("pa")
    y_low, x_low = (home & 2) == 0, (home & 1) == 0

    def shifted(trio, low):
        return jnp.where(low, trio[2 - 1], trio[2])

    stats = jnp.stack(
        [stat, trio_x[0], trio_y[0], trio_d[0], shifted(trio_y, y_low), shifted(trio_x, x_low), shifted(trio_d, y_low)]
    )

    parts = call(
        lambda *refs: query_kernel(pb, *refs),
        [shape((rows, width), F32)] + [shape((rows, width), BF16)] * (pb - 1),
        [VMEM] * (4 + WINDOW),
        [scores, stat, weights, positives, *window_p],
        flops,
        [pltpu.VMEM((WINDOW * rows, q_rows), BF16)],
    )
    query_grad = parts[0]
    for r in range(1, pb):
        query_grad = query_grad + from_member(parts[r], r).astype(F32)

    pieces = []
    for block in window_q:
        pieces.append(block)
        for r in range(1, pb):
            pieces.append(from_member(block, r))
    (cross,) = call(
        cross_kernel,
        [shape((rows, WINDOW * q_rows), F32)],
        [VMEM] * (1 + len(pieces)),
        [own_p, *pieces],
        flops,
    )
    (passage_grad,) = call(
        lambda *refs: passage_kernel(pb, *refs),
        [shape((rows, width), F32)],
        [VMEM] * (3 + len(pieces)),
        [cross, stats, positives, *pieces],
        flops,
    )
    return (query_grad[None], passage_grad[None])


def solution(mesh):
    return jax.shard_map(
        body,
        mesh=mesh,
        in_specs=(
            P("pa", "pb", None),
            P("pa", "pb", None),
            P("pa", None),
            P("pa", None),
            P("pa", None),
        ),
        out_specs=(P("pa", "pb", None), P("pa", "pb", None)),
        check_vma=False,
    )
```

time: 114 us -> 71.2 us (0.62)
  the two profiles are of different devices: /device:TPU:18 before, /device:TPU:0 now
where the time goes in v1:
time: 71.2 us; the launch traced here: 71 us
  waiting for transfers between devices  31.6 us (44%)
  starting transfers between devices  26.1 us (37%)
  Pallas kernels  6.31 us (9%)
  local copies, waits for them, and re-layouts  2.81 us (4%)
  blocking collectives  2.51 us (4%)
  other arithmetic  0.9 us (1%)
  between operations  0.77 us (1%)
    ppermute x17, waiting for transfers between devices, move(): return lax.ppermute(value, 'pa', tables[name])  30 us
    ppermute x17, starting transfers between devices, move(): return lax.ppermute(value, 'pa', tables[name])  24.7 us
    pallas_call x4, Pallas kernels, call(): pl.pallas_call(kernel, out_shape=outs, in_specs=specs, out_specs=[VMEM] *...  6.31 us
    unnamed x17, local copies, waits for them, and re-layouts  2.81 us
    all_gather x1, blocking collectives, body(): full_q = lax.all_gather(own_q, 'pb', axis=0, tiled=True)  2.51 us
    ppermute x9, waiting for transfers between devices, from_member(): return lax.ppermute(value, 'pb', [(i, (i + by) % pb) for i in range(pb)])  1.6 us
  transfers between devices with their start and end apart: 26, of which 12 were waited for; matrix products, arithmetic and copies ran while one was open for 0% of the time, Pallas kernels for 9%

profile of v1, /device:TPU:0, one launch (start us, length us, event | category | flops | bytes accessed | tf_op | source)
XLA Modules:
  0.0 71.0 jit_solution(9051601547949195107)
XLA Ops:
  0.6 3.0 %collective-permute-start.1 = (bf16[128,1024]{1,0:T(8,128)(2,1)}, bf16[128,1024]{1,0:T(8,128)(2,1)S(1)}, u32[]{:S(2)}, u32[]{:S(2)}) collective-permute-start(bf16[128,1024]{1,0:T(8,128)(2,1)} %bitcast.14), channel_id=1, source_target_pairs={{0,2},{1,3},{2,0},{3,1},{4,6},{5,7},{6,4},{7,5},{8,10},{9,11},{10,... | collective-permute-start | bytes 786440 | tf_op jit(solution)/shard_map/ppermute | solution.py:157
  3.7 1.5 %collective-permute-start = (bf16[128,1024]{1,0:T(8,128)(2,1)}, bf16[128,1024]{1,0:T(8,128)(2,1)S(1)}, u32[]{:S(2)}, u32[]{:S(2)}) collective-permute-start(bf16[128,1024]{1,0:T(8,128)(2,1)} %bitcast.15), channel_id=1, source_target_pairs={{0,1},{1,0},{2,3},{3,2},{4,5},{5,4},{6,7},{7,6},{8,9},{9,8},{10,11... | collective-permute-start | bytes 786440 | tf_op jit(solution)/shard_map/ppermute | solution.py:157
  5.2 5.0 %collective-permute-done.1.refs_4_.refs_6_ = bf16[128,1024]{1,0:T(8,128)(2,1)S(1)} collective-permute-done((bf16[128,1024]{1,0:T(8,128)(2,1)}, bf16[128,1024]{1,0:T(8,128)(2,1)S(1)}, u32[]{:S(2)}, u32[]{:S(2)}) %collective-permute-start.1) | collective-permute-done | bytes 262176 | tf_op jit(solution)/shard_map/ppermute | solution.py:157
  10.2 1.8 %collective-permute-start.3 = (bf16[128,1024]{1,0:T(8,128)(2,1)S(1)}, bf16[128,1024]{1,0:T(8,128)(2,1)S(1)}, u32[]{:S(2)}, u32[]{:S(2)}) collective-permute-start(bf16[128,1024]{1,0:T(8,128)(2,1)S(1)} %collective-permute-done.1.refs_4_.refs_6_), channel_id=1, source_target_pairs={{0,4},{1,5},{2,14},{3,15},{4,8},{5,9},{6,2},{7,3},{8,12},{9,13},{1... | collective-permute-start | bytes 786440 | tf_op jit(solution)/shard_map/ppermute | solution.py:157
  12.0 0.0 collective-permute-done.refs_3_.refs_5_
  12.0 3.5 %collective-permute-start.2 = (bf16[128,1024]{1,0:T(8,128)(2,1)S(1)}, bf16[128,1024]{1,0:T(8,128)(2,1)S(1)}, u32[]{:S(2)}, u32[]{:S(2)}) collective-permute-start(bf16[128,1024]{1,0:T(8,128)(2,1)S(1)} %collective-permute-done.refs_3_.refs_5_), channel_id=1, source_target_pairs={{0,2},{1,3},{2,0},{3,1},{4,6},{5,7},{6,4},{7,5},{8,10},{9,11},{10,... | collective-permute-start | bytes 786440 | tf_op jit(solution)/shard_map/ppermute | solution.py:157
  15.5 0.0 collective-permute-start.4
  15.5 5.0 %collective-permute-done.3.refs_6_.refs_8_ = bf16[128,1024]{1,0:T(8,128)(2,1)S(1)} collective-permute-done((bf16[128,1024]{1,0:T(8,128)(2,1)S(1)}, bf16[128,1024]{1,0:T(8,128)(2,1)S(1)}, u32[]{:S(2)}, u32[]{:S(2)}) %collective-permute-start.3) | collective-permute-done | bytes 262176 | tf_op jit(solution)/shard_map/ppermute | solution.py:157
  20.5 2.4 %collective-permute-start.5 = (bf16[128,1024]{1,0:T(8,128)(2,1)S(1)}, bf16[128,1024]{1,0:T(8,128)(2,1)S(1)}, u32[]{:S(2)}, u32[]{:S(2)}) collective-permute-start(bf16[128,1024]{1,0:T(8,128)(2,1)S(1)} %collective-permute-done.3.refs_6_.refs_8_), channel_id=1, source_target_pairs={{0,1},{1,0},{2,3},{3,2},{4,5},{5,4},{6,7},{7,6},{8,9},{9,8},{10,11... | collective-permute-start | bytes 786440 | tf_op jit(solution)/shard_map/ppermute | solution.py:157
  23.0 0.1 collective-permute-start.9
  23.1 2.5 %all-gather = bf16[1,256,1024]{2,1,0:T(8,128)(2,1)S(1)} all-gather(bf16[1,128,1024]{2,1,0:T(8,128)(2,1)} %param.5), channel_id=2, replica_groups=mesh['pb'=2,'pa'=16] {'pb'}, dimensions={1}, use_global_device_ids=true | all-gather | bytes 786432 | tf_op jit(solution)/shard_map/all_gather | solution.py:167
  25.6 0.0 collective-permute-done.2.refs_5_.refs_7_
  25.6 1.1 %collective-permute-start.11 = (bf16[128,1024]{1,0:T(8,128)(2,1)S(1)}, bf16[128,1024]{1,0:T(8,128)(2,1)S(1)}, u32[]{:S(2)}, u32[]{:S(2)}) collective-permute-start(bf16[128,1024]{1,0:T(8,128)(2,1)S(1)} %bitcast.21), channel_id=1, source_target_pairs={{0,2},{1,3},{2,0},{3,1},{4,6},{5,7},{6,4},{7,5},{8,10},{9,11},{10,... | collective-permute-start | bytes 786440 | tf_op jit(solution)/shard_map/ppermute | solution.py:157
  26.8 0.0 collective-permute-done.4.refs_7_.refs_9_
  26.8 2.9 %collective-permute-done.5.refs_8_.refs_10_ = bf16[128,1024]{1,0:T(8,128)(2,1)S(1)} collective-permute-done((bf16[128,1024]{1,0:T(8,128)(2,1)S(1)}, bf16[128,1024]{1,0:T(8,128)(2,1)S(1)}, u32[]{:S(2)}, u32[]{:S(2)}) %collective-permute-start.5) | collective-permute-done | bytes 262176 | tf_op jit(solution)/shard_map/ppermute | solution.py:157
  29.6 2.0 %shard_map.68 = (f32[896,256]{1,0:T(8,128)S(1)}, f32[8,256]{1,0:T(8,128)S(1)}) custom-call(s32[1,7]{1,0:T(1,128)S(1)} %copy-done.6, bf16[256,1024]{1,0:T(8,128)(2,1)S(1)} %bitcast.24, bf16[128,1024]{1,0:T(8,128)(2,1)S(1)} %bitcast.16, bf16[128,1024]{1,0:T(8,128)(2,1)S(1)} %collective-permute-done.refs_3_.refs_5_, ...), custom_call_target="tpu_custom_call" | custom-call | flops 469762048 | bytes 3285020 | tf_op jit(solution)/shard_map/pallas_call | solution.py:138
  31.7 0.9 %copy-done.2 = f32[896,256]{1,0:T(8,128)} copy-done((f32[896,256]{1,0:T(8,128)}, f32[896,256]{1,0:T(8,128)S(1)}, u32[]{:S(2)}) %copy-start.2) | copy-done | bytes 917528
  32.6 0.0 collective-permute-start.6
  32.6 0.3 collective-permute-done.9.refs_2_.refs_5_
  32.9 0.2 collective-permute-start.10
  33.2 0.6 collective-permute-done.6
  33.8 0.0 copy-start.4
  33.8 0.7 copy-done.4
  34.5 5.4 %collective-permute-start.22 = (f32[8,256]{1,0:T(8,128)S(1)}, f32[8,256]{1,0:T(8,128)S(1)}, u32[]{:S(2)}, u32[]{:S(2)}) collective-permute-start(f32[8,256]{1,0:T(8,128)S(1)} %get-tuple-element.11.refs_1_), channel_id=1, source_target_pairs={{0,12},{1,13},{2,14},{3,15},{4,0},{5,1},{6,2},{7,3},{8,4},{9,5},{1... | collective-permute-start | bytes 24584 | tf_op jit(solution)/shard_map/ppermute | solution.py:157
  39.9 0.0 collective-permute-done.11.refs_4_.refs_7_
  39.9 0.1 collective-permute-start.13
  40.0 1.3 %collective-permute-done.22 = f32[8,256]{1,0:T(8,128)S(1)} collective-permute-done((f32[8,256]{1,0:T(8,128)S(1)}, f32[8,256]{1,0:T(8,128)S(1)}, u32[]{:S(2)}, u32[]{:S(2)}) %collective-permute-start.22) | collective-permute-done | bytes 8224 | tf_op jit(solution)/shard_map/ppermute | solution.py:157
  41.2 0.0 collective-permute-start.15
  41.2 4.2 %collective-permute-done.21 = f32[8,256]{1,0:T(8,128)S(1)} collective-permute-done((f32[8,256]{1,0:T(8,128)S(1)}, f32[8,256]{1,0:T(8,128)S(1)}, u32[]{:S(2)}, u32[]{:S(2)}) %collective-permute-start.21) | collective-permute-done | bytes 8224 | tf_op jit(solution)/shard_map/ppermute | solution.py:157
  45.4 2.5 %collective-permute-start.23 = (f32[3,8,256]{2,1,0:T(8,128)S(1)}, f32[3,8,256]{2,1,0:T(8,128)S(1)}, u32[]{:S(2)}, u32[]{:S(2)}) collective-permute-start(f32[3,8,256]{2,1,0:T(8,128)S(1)} %pad_maximum_fusion), channel_id=1, source_target_pairs={{0,1},{1,0},{2,3},{3,2},{4,5},{5,4},{6,7},{7,6},{8,9},{9,8},{10,11... | collective-permute-start | bytes 73736 | tf_op jit(solution)/shard_map/ppermute | solution.py:157
  47.9 1.2 %copy-done.3 = f32[896,256]{1,0:T(8,128)S(1)} copy-done((f32[896,256]{1,0:T(8,128)S(1)}, f32[896,256]{1,0:T(8,128)}, u32[]{:S(2)}) %copy-start.3) | copy-done | bytes 917528
  49.1 1.2 %shard_map.69 = (f32[128,1024]{1,0:T(8,128)S(1)}, bf16[128,1024]{1,0:T(8,128)(2,1)S(1)}) custom-call(f32[896,256]{1,0:T(8,128)S(1)} %copy-done.3, f32[8,256]{1,0:T(8,128)S(1)} %get-tuple-element.11.refs_1_, f32[1,256]{1,0:T(1,128)S(1)} %copy-done.4, s32[1,256]{1,0:T(1,128)S(1)} %copy-done.5, bf16[128,1024]{1,0:T(8,128)(2,1)S(1)} %bitcast.17, ...), custom_call_target="tpu_custom_call" | custom-call | flops 469762048 | bytes 3549184 | tf_op jit(solution)/shard_map/pallas_call | solution.py:138
  50.3 0.0 collective-permute-done.23
  50.3 0.5 collective-permute-start.24
  50.8 3.3 %collective-permute-done.24 = f32[3,8,256]{2,1,0:T(8,128)S(1)} collective-permute-done((f32[3,8,256]{2,1,0:T(8,128)S(1)}, f32[3,8,256]{2,1,0:T(8,128)S(1)}, u32[]{:S(2)}, u32[]{:S(2)}) %collective-permute-start.24) | collective-permute-done | bytes 24608 | tf_op jit(solution)/shard_map/ppermute | solution.py:157
  54.2 1.3 %collective-permute-start.25 = (f32[3,8,256]{2,1,0:T(8,128)S(1)}, f32[3,8,256]{2,1,0:T(8,128)S(1)}, u32[]{:S(2)}, u32[]{:S(2)}) collective-permute-start(f32[3,8,256]{2,1,0:T(8,128)S(1)} %pad_maximum_fusion), channel_id=1, source_target_pairs={{0,3},{1,2},{2,1},{3,0},{4,7},{5,6},{6,5},{7,4},{8,11},{9,10},{10,... | collective-permute-start | bytes 73736 | tf_op jit(solution)/shard_map/ppermute | solution.py:157
  55.4 0.0 collective-permute-done.15.refs_8_.refs_11_
  55.5 3.7 %collective-permute-done.25 = f32[3,8,256]{2,1,0:T(8,128)S(1)} collective-permute-done((f32[3,8,256]{2,1,0:T(8,128)S(1)}, f32[3,8,256]{2,1,0:T(8,128)S(1)}, u32[]{:S(2)}, u32[]{:S(2)}) %collective-permute-start.25) | collective-permute-done | bytes 24608 | tf_op jit(solution)/shard_map/ppermute | solution.py:157
  59.1 1.4 %collective-permute-start.19 = (bf16[128,1024]{1,0:T(8,128)(2,1)S(1)}, bf16[128,1024]{1,0:T(8,128)(2,1)S(1)}, u32[]{:S(2)}, u32[]{:S(2)}) collective-permute-start(bf16[128,1024]{1,0:T(8,128)(2,1)S(1)} %collective-permute-done.15.refs_8_.refs_11_), channel_id=1, source_target_pairs={{0,1},{1,0},{2,3},{3,2},{4,5},{5,4},{6,7},{7,6},{8,9},{9,8},{10,11... | collective-permute-start | bytes 786440 | tf_op jit(solution)/shard_map/ppermute | solution.py:157
  60.6 0.5 collective-permute-start.16
  61.1 0.1 collective-permute-start.14
  61.2 2.5 %collective-permute-done.17.refs_10_.refs_13_ = bf16[128,1024]{1,0:T(8,128)(2,1)S(1)} collective-permute-done((bf16[128,1024]{1,0:T(8,128)(2,1)S(1)}, bf16[128,1024]{1,0:T(8,128)(2,1)S(1)}, u32[]{:S(2)}, u32[]{:S(2)}) %collective-permute-start.17) | collective-permute-done | bytes 262176 | tf_op jit(solution)/shard_map/ppermute | solution.py:157
  63.6 1.9 %collective-permute-done.19.refs_12_.refs_15_ = bf16[128,1024]{1,0:T(8,128)(2,1)S(1)} collective-permute-done((bf16[128,1024]{1,0:T(8,128)(2,1)S(1)}, bf16[128,1024]{1,0:T(8,128)(2,1)S(1)}, u32[]{:S(2)}, u32[]{:S(2)}) %collective-permute-start.19) | collective-permute-done | bytes 262176 | tf_op jit(solution)/shard_map/ppermute | solution.py:157
  65.5 0.5 collective-permute-start.7
  66.0 1.0 %collective-permute-done.20.refs_13_.refs_16_ = bf16[128,1024]{1,0:T(8,128)(2,1)S(1)} collective-permute-done((bf16[128,1024]{1,0:T(8,128)(2,1)S(1)}, bf16[128,1024]{1,0:T(8,128)(2,1)S(1)}, u32[]{:S(2)}, u32[]{:S(2)}) %collective-permute-start.20) | collective-permute-done | bytes 262176 | tf_op jit(solution)/shard_map/ppermute | solution.py:160
  67.0 1.1 %shard_map.70.refs_0_ = f32[128,1792]{1,0:T(8,128)S(1)} custom-call(bf16[128,1024]{1,0:T(8,128)(2,1)S(1)} %bitcast.18, bf16[128,1024]{1,0:T(8,128)(2,1)S(1)} %bitcast.22, bf16[128,1024]{1,0:T(8,128)(2,1)S(1)} %collective-permute-done.8.refs_1_.refs_4_, bf16[128,1024]{1,0:T(8,128)(2,1)S(1)} %collective-permute-done.9.refs_2_.refs_5_, ...), custom_call_target="tpu_custom_call" | custom-call | flops 469762048 | bytes 4849664 | tf_op jit(solution)/shard_map/pallas_call | solution.py:138
  68.2 2.0 %shard_map.71 = f32[128,1024]{1,0:T(8,128)} custom-call(f32[128,1792]{1,0:T(8,128)S(1)} %shard_map.70.refs_0_, f32[7,8,256]{2,1,0:T(8,128)S(1)} %constant_dynamic-update-slice_fusion.refs_1_, s32[1,256]{1,0:T(1,128)S(1)} %copy-done.5, bf16[128,1024]{1,0:T(8,128)(2,1)S(1)} %bitcast.23, bf16[128,1024]{1,0:T(8,128)(2,1)S(1)} %collective-permute-done.8.refs_1_.refs_4_, ...), custom_call_target="tpu_custom_call" | custom-call | flops 469762048 | bytes 5170176 | tf_op jit(solution)/shard_map/pallas_call | solution.py:138
  70.1 0.8 %add_bitcast_fusion = f32[1,128,1024]{2,1,0:T(8,128)} fusion(f32[128,1024]{1,0:T(8,128)S(1)} %get-tuple-element.8, bf16[128,1024]{1,0:T(8,128)(2,1)S(1)} %collective-permute-done.7), kind=kLoop, calls=%fused_computation | loop fusion | flops 262144 | bytes 1310720 | tf_op jit(solution)/shard_map/broadcast_in_dim | solution.py:236
  (36 shorter events, 0.1 us)
Async XLA Ops:
  0.6 9.5 %collective-permute-start.1 = (bf16[128,1024]{1,0:T(8,128)(2,1)}, bf16[128,1024]{1,0:T(8,128)(2,1)S(1)}, u32[]{:S(2)}, u32[]{:S(2)}) collective-permute-start(bf16[128,1024]{1,0:T(8,128)(2,1)} %bitcast.14), channel_id=1, source_target_pairs={{0,2},{1,3},{2,0},{3,1},{4,6},{5,7},{6,4},{7,5},{8,10},{9,11},{10,... | collective-permute-start | bytes 786440 | tf_op jit(solution)/shard_map/ppermute | solution.py:157
  3.7 8.3 %collective-permute-start = (bf16[128,1024]{1,0:T(8,128)(2,1)}, bf16[128,1024]{1,0:T(8,128)(2,1)S(1)}, u32[]{:S(2)}, u32[]{:S(2)}) collective-permute-start(bf16[128,1024]{1,0:T(8,128)(2,1)} %bitcast.15), channel_id=1, source_target_pairs={{0,1},{1,0},{2,3},{3,2},{4,5},{5,4},{6,7},{7,6},{8,9},{9,8},{10,11... | collective-permute-start | bytes 786440 | tf_op jit(solution)/shard_map/ppermute | solution.py:157
  10.2 10.4 %collective-permute-start.3 = (bf16[128,1024]{1,0:T(8,128)(2,1)S(1)}, bf16[128,1024]{1,0:T(8,128)(2,1)S(1)}, u32[]{:S(2)}, u32[]{:S(2)}) collective-permute-start(bf16[128,1024]{1,0:T(8,128)(2,1)S(1)} %collective-permute-done.1.refs_4_.refs_6_), channel_id=1, source_target_pairs={{0,4},{1,5},{2,14},{3,15},{4,8},{5,9},{6,2},{7,3},{8,12},{9,13},{1... | collective-permute-start | bytes 786440 | tf_op jit(solution)/shard_map/ppermute | solution.py:157
  12.0 13.6 %collective-permute-start.2 = (bf16[128,1024]{1,0:T(8,128)(2,1)S(1)}, bf16[128,1024]{1,0:T(8,128)(2,1)S(1)}, u32[]{:S(2)}, u32[]{:S(2)}) collective-permute-start(bf16[128,1024]{1,0:T(8,128)(2,1)S(1)} %collective-permute-done.refs_3_.refs_5_), channel_id=1, source_target_pairs={{0,2},{1,3},{2,0},{3,1},{4,6},{5,7},{6,4},{7,5},{8,10},{9,11},{10,... | collective-permute-start | bytes 786440 | tf_op jit(solution)/shard_map/ppermute | solution.py:157
  15.5 11.3 %collective-permute-start.4 = (bf16[128,1024]{1,0:T(8,128)(2,1)S(1)}, bf16[128,1024]{1,0:T(8,128)(2,1)S(1)}, u32[]{:S(2)}, u32[]{:S(2)}) collective-permute-start(bf16[128,1024]{1,0:T(8,128)(2,1)S(1)} %collective-permute-done.refs_3_.refs_5_), channel_id=1, source_target_pairs={{0,4},{1,13},{2,6},{3,15},{4,8},{5,1},{6,10},{7,3},{8,12},{9,5},{1... | collective-permute-start | bytes 786440 | tf_op jit(solution)/shard_map/ppermute | solution.py:157
  20.5 9.1 %collective-permute-start.5 = (bf16[128,1024]{1,0:T(8,128)(2,1)S(1)}, bf16[128,1024]{1,0:T(8,128)(2,1)S(1)}, u32[]{:S(2)}, u32[]{:S(2)}) collective-permute-start(bf16[128,1024]{1,0:T(8,128)(2,1)S(1)} %collective-permute-done.3.refs_6_.refs_8_), channel_id=1, source_target_pairs={{0,1},{1,0},{2,3},{3,2},{4,5},{5,4},{6,7},{7,6},{8,9},{9,8},{10,11... | collective-permute-start | bytes 786440 | tf_op jit(solution)/shard_map/ppermute | solution.py:157
  23.0 2.7 %copy-start.1 = (bf16[1,128,1024]{2,1,0:T(8,128)(2,1)S(1)}, bf16[1,128,1024]{2,1,0:T(8,128)(2,1)}, u32[]{:S(2)}) copy-start(bf16[1,128,1024]{2,1,0:T(8,128)(2,1)} %param.5) | copy-start | bytes 786436
  23.0 6.7 %copy-start = (bf16[1,128,1024]{2,1,0:T(8,128)(2,1)S(1)}, bf16[1,128,1024]{2,1,0:T(8,128)(2,1)}, u32[]{:S(2)}) copy-start(bf16[1,128,1024]{2,1,0:T(8,128)(2,1)} %param.6) | copy-start | bytes 786436
  23.0 37.6 %collective-permute-start.8 = (bf16[128,1024]{1,0:T(8,128)(2,1)}, bf16[128,1024]{1,0:T(8,128)(2,1)S(1)}, u32[]{:S(2)}, u32[]{:S(2)}) collective-permute-start(bf16[128,1024]{1,0:T(8,128)(2,1)} %bitcast.19), channel_id=1, source_target_pairs={{0,16},{16,0},{1,17},{17,1},{2,18},{18,2},{3,19},{19,3},{4,20},{20... | collective-permute-start | bytes 786440 | tf_op jit(solution)/shard_map/ppermute | solution.py:160
  23.0 10.0 %collective-permute-start.9 = (bf16[128,1024]{1,0:T(8,128)(2,1)}, bf16[128,1024]{1,0:T(8,128)(2,1)S(1)}, u32[]{:S(2)}, u32[]{:S(2)}) collective-permute-start(bf16[128,1024]{1,0:T(8,128)(2,1)} %bitcast.20), channel_id=1, source_target_pairs={{0,1},{1,0},{2,3},{3,2},{4,5},{5,4},{6,7},{7,6},{8,9},{9,8},{10,11... | collective-permute-start | bytes 786440 | tf_op jit(solution)/shard_map/ppermute | solution.py:157
  25.6 4.0 %copy-start.6 = (s32[1,7]{1,0:T(1,128)S(1)}, s32[1,7]{1,0:T(1,128)}, u32[]{:S(2)}) copy-start(s32[1,7]{1,0:T(1,128)} %refs_0_.1) | copy-start | bytes 88
  25.6 14.2 %collective-permute-start.11 = (bf16[128,1024]{1,0:T(8,128)(2,1)S(1)}, bf16[128,1024]{1,0:T(8,128)(2,1)S(1)}, u32[]{:S(2)}, u32[]{:S(2)}) collective-permute-start(bf16[128,1024]{1,0:T(8,128)(2,1)S(1)} %bitcast.21), channel_id=1, source_target_pairs={{0,2},{1,3},{2,0},{3,1},{4,6},{5,7},{6,4},{7,5},{8,10},{9,11},{10,... | collective-permute-start | bytes 786440 | tf_op jit(solution)/shard_map/ppermute | solution.py:157
  31.7 0.9 %copy-start.2 = (f32[896,256]{1,0:T(8,128)}, f32[896,256]{1,0:T(8,128)S(1)}, u32[]{:S(2)}) copy-start(f32[896,256]{1,0:T(8,128)S(1)} %get-tuple-element.6.refs_0_) | copy-start | bytes 2752516
  32.6 1.2 %collective-permute-start.6 = (f32[8,256]{1,0:T(8,128)S(1)}, f32[8,256]{1,0:T(8,128)S(1)}, u32[]{:S(2)}, u32[]{:S(2)}) collective-permute-start(f32[8,256]{1,0:T(8,128)S(1)} %get-tuple-element.7), channel_id=1, source_target_pairs={{0,16},{16,0},{1,17},{17,1},{2,18},{18,2},{3,19},{19,3},{4,20},{20... | collective-permute-start | bytes 24584 | tf_op jit(solution)/shard_map/ppermute | solution.py:160
  32.9 27.6 %collective-permute-start.10 = (bf16[128,1024]{1,0:T(8,128)(2,1)S(1)}, bf16[128,1024]{1,0:T(8,128)(2,1)S(1)}, u32[]{:S(2)}, u32[]{:S(2)}) collective-permute-start(bf16[128,1024]{1,0:T(8,128)(2,1)S(1)} %collective-permute-done.9.refs_2_.refs_5_), channel_id=1, source_target_pairs={{0,16},{16,0},{1,17},{17,1},{2,18},{18,2},{3,19},{19,3},{4,20},{20... | collective-permute-start | bytes 786440 | tf_op jit(solution)/shard_map/ppermute | solution.py:160
  33.8 0.7 copy-start.4
  34.5 6.7 %collective-permute-start.22 = (f32[8,256]{1,0:T(8,128)S(1)}, f32[8,256]{1,0:T(8,128)S(1)}, u32[]{:S(2)}, u32[]{:S(2)}) collective-permute-start(f32[8,256]{1,0:T(8,128)S(1)} %get-tuple-element.11.refs_1_), channel_id=1, source_target_pairs={{0,12},{1,13},{2,14},{3,15},{4,0},{5,1},{6,2},{7,3},{8,4},{9,5},{1... | collective-permute-start | bytes 24584 | tf_op jit(solution)/shard_map/ppermute | solution.py:157
  39.8 5.5 %collective-permute-start.21 = (f32[8,256]{1,0:T(8,128)S(1)}, f32[8,256]{1,0:T(8,128)S(1)}, u32[]{:S(2)}, u32[]{:S(2)}) collective-permute-start(f32[8,256]{1,0:T(8,128)S(1)} %get-tuple-element.11.refs_1_), channel_id=1, source_target_pairs={{0,4},{1,5},{2,6},{3,7},{4,8},{5,9},{6,10},{7,11},{8,12},{9,13},{1... | collective-permute-start | bytes 24584 | tf_op jit(solution)/shard_map/ppermute | solution.py:157
  39.9 21.2 %collective-permute-start.13 = (bf16[128,1024]{1,0:T(8,128)(2,1)S(1)}, bf16[128,1024]{1,0:T(8,128)(2,1)S(1)}, u32[]{:S(2)}, u32[]{:S(2)}) collective-permute-start(bf16[128,1024]{1,0:T(8,128)(2,1)S(1)} %collective-permute-done.9.refs_2_.refs_5_), channel_id=1, source_target_pairs={{0,2},{1,3},{2,0},{3,1},{4,6},{5,7},{6,4},{7,5},{8,10},{9,11},{10,... | collective-permute-start | bytes 786440 | tf_op jit(solution)/shard_map/ppermute | solution.py:157
  41.2 14.2 %collective-permute-start.15 = (bf16[128,1024]{1,0:T(8,128)(2,1)S(1)}, bf16[128,1024]{1,0:T(8,128)(2,1)S(1)}, u32[]{:S(2)}, u32[]{:S(2)}) collective-permute-start(bf16[128,1024]{1,0:T(8,128)(2,1)S(1)} %collective-permute-done.11.refs_4_.refs_7_), channel_id=1, source_target_pairs={{0,4},{1,5},{2,14},{3,15},{4,8},{5,9},{6,2},{7,3},{8,12},{9,13},{1... | collective-permute-start | bytes 786440 | tf_op jit(solution)/shard_map/ppermute | solution.py:157
  45.4 2.5 %copy-start.5 = (s32[1,256]{1,0:T(1,128)S(1)}, s32[1,256]{1,0:T(1,128)}, u32[]{:S(2)}) copy-start(s32[1,256]{1,0:T(1,128)} %refs_2_.3) | copy-start | bytes 3076
  45.4 4.9 %collective-permute-start.23 = (f32[3,8,256]{2,1,0:T(8,128)S(1)}, f32[3,8,256]{2,1,0:T(8,128)S(1)}, u32[]{:S(2)}, u32[]{:S(2)}) collective-permute-start(f32[3,8,256]{2,1,0:T(8,128)S(1)} %pad_maximum_fusion), channel_id=1, source_target_pairs={{0,1},{1,0},{2,3},{3,2},{4,5},{5,4},{6,7},{7,6},{8,9},{9,8},{10,11... | collective-permute-start | bytes 73736 | tf_op jit(solution)/shard_map/ppermute | solution.py:157
  47.9 1.2 %copy-start.3 = (f32[896,256]{1,0:T(8,128)S(1)}, f32[896,256]{1,0:T(8,128)}, u32[]{:S(2)}) copy-start(f32[896,256]{1,0:T(8,128)} %copy-done.2) | copy-start | bytes 2752516
  50.3 3.9 %collective-permute-start.24 = (f32[3,8,256]{2,1,0:T(8,128)S(1)}, f32[3,8,256]{2,1,0:T(8,128)S(1)}, u32[]{:S(2)}, u32[]{:S(2)}) collective-permute-start(f32[3,8,256]{2,1,0:T(8,128)S(1)} %pad_maximum_fusion), channel_id=1, source_target_pairs={{0,2},{1,3},{2,0},{3,1},{4,6},{5,7},{6,4},{7,5},{8,10},{9,11},{10,... | collective-permute-start | bytes 73736 | tf_op jit(solution)/shard_map/ppermute | solution.py:157
  54.2 5.0 %collective-permute-start.25 = (f32[3,8,256]{2,1,0:T(8,128)S(1)}, f32[3,8,256]{2,1,0:T(8,128)S(1)}, u32[]{:S(2)}, u32[]{:S(2)}) collective-permute-start(f32[3,8,256]{2,1,0:T(8,128)S(1)} %pad_maximum_fusion), channel_id=1, source_target_pairs={{0,3},{1,2},{2,1},{3,0},{4,7},{5,6},{6,5},{7,4},{8,11},{9,10},{10,... | collective-permute-start | bytes 73736 | tf_op jit(solution)/shard_map/ppermute | solution.py:157
  55.4 8.2 %collective-permute-start.17 = (bf16[128,1024]{1,0:T(8,128)(2,1)S(1)}, bf16[128,1024]{1,0:T(8,128)(2,1)S(1)}, u32[]{:S(2)}, u32[]{:S(2)}) collective-permute-start(bf16[128,1024]{1,0:T(8,128)(2,1)S(1)} %collective-permute-done.9.refs_2_.refs_5_), channel_id=1, source_target_pairs={{0,4},{1,13},{2,6},{3,15},{4,8},{5,1},{6,10},{7,3},{8,12},{9,5},{1... | collective-permute-start | bytes 786440 | tf_op jit(solution)/shard_map/ppermute | solution.py:157
  59.1 6.4 %collective-permute-start.19 = (bf16[128,1024]{1,0:T(8,128)(2,1)S(1)}, bf16[128,1024]{1,0:T(8,128)(2,1)S(1)}, u32[]{:S(2)}, u32[]{:S(2)}) collective-permute-start(bf16[128,1024]{1,0:T(8,128)(2,1)S(1)} %collective-permute-done.15.refs_8_.refs_11_), channel_id=1, source_target_pairs={{0,1},{1,0},{2,3},{3,2},{4,5},{5,4},{6,7},{7,6},{8,9},{9,8},{10,11... | collective-permute-start | bytes 786440 | tf_op jit(solution)/shard_map/ppermute | solution.py:157
  60.6 5.0 %collective-permute-start.12 = (bf16[128,1024]{1,0:T(8,128)(2,1)S(1)}, bf16[128,1024]{1,0:T(8,128)(2,1)S(1)}, u32[]{:S(2)}, u32[]{:S(2)}) collective-permute-start(bf16[128,1024]{1,0:T(8,128)(2,1)S(1)} %collective-permute-done.11.refs_4_.refs_7_), channel_id=1, source_target_pairs={{0,16},{16,0},{1,17},{17,1},{2,18},{18,2},{3,19},{19,3},{4,20},{20... | collective-permute-start | bytes 786440 | tf_op jit(solution)/shard_map/ppermute | solution.py:160
  60.6 5.4 %collective-permute-start.16 = (bf16[128,1024]{1,0:T(8,128)(2,1)S(1)}, bf16[128,1024]{1,0:T(8,128)(2,1)S(1)}, u32[]{:S(2)}, u32[]{:S(2)}) collective-permute-start(bf16[128,1024]{1,0:T(8,128)(2,1)S(1)} %collective-permute-done.15.refs_8_.refs_11_), channel_id=1, source_target_pairs={{0,16},{16,0},{1,17},{17,1},{2,18},{18,2},{3,19},{19,3},{4,20},{20... | collective-permute-start | bytes 786440 | tf_op jit(solution)/shard_map/ppermute | solution.py:160
  61.1 4.9 %collective-permute-start.14 = (bf16[128,1024]{1,0:T(8,128)(2,1)S(1)}, bf16[128,1024]{1,0:T(8,128)(2,1)S(1)}, u32[]{:S(2)}, u32[]{:S(2)}) collective-permute-start(bf16[128,1024]{1,0:T(8,128)(2,1)S(1)} %collective-permute-done.13.refs_6_.refs_9_), channel_id=1, source_target_pairs={{0,16},{16,0},{1,17},{17,1},{2,18},{18,2},{3,19},{19,3},{4,20},{20... | collective-permute-start | bytes 786440 | tf_op jit(solution)/shard_map/ppermute | solution.py:160
  63.6 2.4 %collective-permute-start.18 = (bf16[128,1024]{1,0:T(8,128)(2,1)S(1)}, bf16[128,1024]{1,0:T(8,128)(2,1)S(1)}, u32[]{:S(2)}, u32[]{:S(2)}) collective-permute-start(bf16[128,1024]{1,0:T(8,128)(2,1)S(1)} %collective-permute-done.17.refs_10_.refs_13_), channel_id=1, source_target_pairs={{0,16},{16,0},{1,17},{17,1},{2,18},{18,2},{3,19},{19,3},{4,20},{20... | collective-permute-start | bytes 786440 | tf_op jit(solution)/shard_map/ppermute | solution.py:160
  65.5 1.5 %collective-permute-start.20 = (bf16[128,1024]{1,0:T(8,128)(2,1)S(1)}, bf16[128,1024]{1,0:T(8,128)(2,1)S(1)}, u32[]{:S(2)}, u32[]{:S(2)}) collective-permute-start(bf16[128,1024]{1,0:T(8,128)(2,1)S(1)} %collective-permute-done.19.refs_12_.refs_15_), channel_id=1, source_target_pairs={{0,16},{16,0},{1,17},{17,1},{2,18},{18,2},{3,19},{19,3},{4,20},{20... | collective-permute-start | bytes 786440 | tf_op jit(solution)/shard_map/ppermute | solution.py:160
  65.5 4.6 %collective-permute-start.7 = (bf16[128,1024]{1,0:T(8,128)(2,1)S(1)}, bf16[128,1024]{1,0:T(8,128)(2,1)S(1)}, u32[]{:S(2)}, u32[]{:S(2)}) collective-permute-start(bf16[128,1024]{1,0:T(8,128)(2,1)S(1)} %get-tuple-element.9), channel_id=1, source_target_pairs={{0,16},{16,0},{1,17},{17,1},{2,18},{18,2},{3,19},{19,3},{4,20},{20... | collective-permute-start | bytes 786440 | tf_op jit(solution)/shard_map/ppermute | solution.py:160

commit v2 on v1

v2 whole, which is shorter than its diff:
```python
import math

import jax
import jax.numpy as jnp
from jax import lax
from jax.experimental import pallas as pl
from jax.experimental.pallas import tpu as pltpu
from jax.sharding import PartitionSpec as P

F32 = jnp.float32
BF16 = jnp.bfloat16
WINDOW = 7
LAST = WINDOW - 1


def group_shift(i, step, count):
    return (i + step + count) % count


def relay_tables(count):
    every = range(count)
    return {
        "x": [(i, i ^ 1) for i in every],
        "y": [(i, i ^ 2) for i in every],
        "d": [(i, i ^ 3) for i in every],
        "za": [(i, group_shift(i, -4 if i & 2 else 4, count)) for i in every],
        "zb": [(i, group_shift(i, -4 if i & 1 else 4, count)) for i in every],
        "up": [(i, group_shift(i, 4, count)) for i in every],
        "down": [(i, group_shift(i, -4, count)) for i in every],
    }


def window_ids(i, count):
    to_y = jnp.where((i & 2) != 0, 4, -4)
    to_x = jnp.where((i & 1) != 0, 4, -4)
    return [
        i,
        i ^ 1,
        i ^ 2,
        i ^ 3,
        ((i ^ 2) + to_y + count) % count,
        ((i ^ 1) + to_x + count) % count,
        ((i ^ 3) + to_y + count) % count,
    ]


def nt_dot(a, b):
    return lax.dot_general(a, b, (((1,), (1,)), ((), ())), preferred_element_type=F32)


def tn_dot(a, b):
    return lax.dot_general(a, b, (((0,), (0,)), ((), ())), preferred_element_type=F32)


def member_slice(member, rows):
    return pl.ds(pl.multiple_of(member * rows, rows), rows)


def fold(part, top, total):
    new_top = jnp.max(part, axis=0, keepdims=True)
    if top is None:
        return new_top, jnp.sum(jnp.exp(part - new_top), axis=0, keepdims=True)
    new_top = jnp.maximum(top, new_top)
    return new_top, total * jnp.exp(top - new_top) + jnp.sum(jnp.exp(part - new_top), axis=0, keepdims=True)


def joined(pairs):
    top = pairs[0][0]
    for other, _ in pairs[1:]:
        top = jnp.maximum(top, other)
    total = jnp.zeros_like(top)
    for other, part in pairs:
        total += part * jnp.exp(other - top)
    return top + jnp.log(total)


def own_kernel(count, pb, lists, w_ref, pos_ref, p_ref, *refs):
    q_refs, (s_ref, ml_ref, full_ref, own_ref, side_ref, where_ref) = refs[:pb], refs[pb:]
    rows, width = p_ref.shape
    scale = 1.0 / math.sqrt(width)
    ids = window_ids(lax.axis_index("pa"), count)
    me = lax.axis_index("pb")
    for r in range(pb):
        full_ref[member_slice((me - r + pb) % pb, rows), :] = q_refs[r][...]
    own_ref[...] = p_ref[...]
    where_ref[...] = pos_ref[...]
    side_ref[...] = jnp.zeros_like(side_ref)
    for t in range(WINDOW):
        hit = lists[0, 0] == ids[t]
        for s in range(1, lists.shape[1]):
            hit = jnp.logical_or(hit, lists[0, s] == ids[t])
        bias = jnp.where(hit, 0.0, -jnp.inf).astype(F32)
        side_ref[t : t + 1, :] = jnp.full((1, side_ref.shape[1]), bias, F32)
    lane = lax.broadcasted_iota(jnp.int32, (1, side_ref.shape[1]), 1)
    listed = jnp.full((1, side_ref.shape[1]), -1.0, F32)
    for s in range(lists.shape[1]):
        listed = jnp.where(lane == s, lists[0, s].astype(F32), listed)
    side_ref[WINDOW : WINDOW + 1, :] = listed
    side_ref[WINDOW + 1 : WINDOW + 2, :] = w_ref[...]
    part = nt_dot(own_ref[...], full_ref[...]) * scale + side_ref[0:1, :]
    s_ref[...] = part
    ml_ref[...] = jnp.zeros_like(ml_ref)
    ml_ref[0:1, :], ml_ref[1:2, :] = fold(part, None, None)


def score_parts(full_ref, side_ref, before_ref, p_refs, s_ref, first):
    rows, width = p_refs[0].shape
    scale = 1.0 / math.sqrt(width)
    before, total = before_ref[0:1, :], before_ref[1:2, :]
    top = before
    for n, p_ref in enumerate(p_refs):
        part = nt_dot(p_ref[...], full_ref[...]) * scale + side_ref[first + n : first + n + 1, :]
        s_ref[n * rows : (n + 1) * rows, :] = part
        top = jnp.maximum(top, jnp.max(part, axis=0, keepdims=True))
    total = total * jnp.exp(before - top)
    for n in range(len(p_refs)):
        total += jnp.sum(jnp.exp(s_ref[n * rows : (n + 1) * rows, :] - top), axis=0, keepdims=True)
    return top, total


def middle_kernel(full_ref, side_ref, before_ref, *refs):
    p_refs, (s_ref, ml_ref) = refs[:-2], refs[-2:]
    ml_ref[...] = jnp.zeros_like(ml_ref)
    ml_ref[0:1, :], ml_ref[1:2, :] = score_parts(full_ref, side_ref, before_ref, p_refs, s_ref, 1)


def last_kernel(pb, full_ref, side_ref, before_ref, p_ref, s_ref, ml_ref, stat_ref):
    top, total = score_parts(full_ref, side_ref, before_ref, [p_ref], s_ref, LAST)
    rows = p_ref.shape[0]
    ml_ref[...] = jnp.zeros_like(ml_ref)
    ml_ref[0:1, :] = top
    ml_ref[1:2, :] = total
    pieces = []
    for value in (top, total, side_ref[WINDOW + 1 : WINDOW + 2, :]):
        pieces += [value[:, c * rows : (c + 1) * rows] for c in range(pb)]
    pieces.append(side_ref[WINDOW : WINDOW + 1, 0:rows])
    stat_ref[...] = jnp.zeros_like(stat_ref)
    stat_ref[0 : len(pieces), :] = jnp.concatenate(pieces, axis=0)


def query_kernel(pb, so_ref, sm_ref, sl_ref, side_ref, pos_ref, *refs):
    ml_refs, p_refs, outs, coeff = refs[:pb], refs[pb : pb + WINDOW], refs[pb + WINDOW : -1], refs[-1]
    rows, width = p_refs[0].shape
    scale = 1.0 / math.sqrt(width)
    me = lax.axis_index("pb")
    lse = joined([(ml[0:1, :], ml[1:2, :]) for ml in ml_refs])
    w = side_ref[WINDOW + 1 : WINDOW + 2, :]
    row = lax.broadcasted_iota(jnp.int32, (rows, w.shape[1]), 0)
    for t in range(WINDOW):
        if t == 0:
            prob = jnp.exp(so_ref[...] - lse) - (row == pos_ref[...] - me * rows).astype(F32)
        elif t == LAST:
            prob = jnp.exp(sl_ref[...] - lse)
        else:
            prob = jnp.exp(sm_ref[(t - 1) * rows : t * rows, :] - lse)
        coeff[t * rows : (t + 1) * rows, :] = (w * prob * scale).astype(BF16)
    for r in range(pb):
        lanes = member_slice((me + r) % pb, rows)
        total = None
        for t in range(WINDOW):
            part = tn_dot(coeff[t * rows : (t + 1) * rows, lanes], p_refs[t][...])
            total = part if total is None else total + part
        outs[r][...] = total.astype(outs[r].dtype)


def cross_kernel(p_ref, *refs):
    q_refs, s_ref = refs[:-1], refs[-1]
    scale = 1.0 / math.sqrt(p_ref.shape[1])
    at = 0
    for q_ref in q_refs:
        s_ref[:, at : at + q_ref.shape[0]] = nt_dot(p_ref[...], q_ref[...]) * scale
        at += q_ref.shape[0]


def passage_kernel(pb, se_ref, sl_ref, pos_ref, *refs):
    grad_refs, stat_refs, refs = refs[:pb], refs[pb : 4 * pb], refs[4 * pb :]
    full_ref, q_refs = refs[0], refs[1 : 1 + pb * LAST]
    out_ref, query_ref, lse_ref, weight_ref = refs[-4:]
    four, up, down = (stat_refs[k * pb : (k + 1) * pb] for k in range(3))
    rows, width = out_ref.shape
    scale = 1.0 / math.sqrt(width)
    grad = grad_refs[0][...]
    for ref in grad_refs[1:]:
        grad = grad + ref[...].astype(F32)
    query_ref[...] = grad
    home, me = lax.axis_index("pa"), lax.axis_index("pb")
    y_low, x_low = (home & 2) == 0, (home & 1) == 0
    row = lax.broadcasted_iota(jnp.int32, (rows, rows), 0)

    def stat(t, c):
        if t < 4:
            return four[c][t]
        k, low = {4: (2, y_low), 5: (1, x_low), 6: (3, y_low)}[t]
        return jnp.where(low, up[c][k], down[c][k])

    total = None
    for t in range(WINDOW):
        mine = [stat(t, c) for c in range(pb)]
        lse_all = joined([(s[0:pb, :], s[pb : 2 * pb, :]) for s in mine])
        w_all = mine[0][2 * pb : 3 * pb, :]
        if t > 0:
            lse_ref[...] = lse_all
            weight_ref[...] = w_all
        hit = jnp.max(jnp.where(mine[0][3 * pb : 3 * pb + 1, :] == home.astype(F32), 1.0, 0.0), axis=1, keepdims=True) > 0.5
        for r in range(pb):
            n = t * pb + r
            if t == 0:
                lse, w, q_block = lse_all[r : r + 1, :], w_all[r : r + 1, :], full_ref[r * rows : (r + 1) * rows, :]
            else:
                member = pl.ds((me - r + pb) % pb, 1)
                lse, w, q_block = lse_ref[member, :], weight_ref[member, :], q_refs[n - pb][...]
            score = se_ref[:, n * rows : (n + 1) * rows] if t < LAST else sl_ref[:, r * rows : (r + 1) * rows]
            prob = jnp.exp(score - lse)
            if t == 0:
                prob = prob - (row == pos_ref[:, r * rows : (r + 1) * rows] - me * rows).astype(F32)
            value = jnp.where(hit, w * prob * scale, 0.0).astype(BF16)
            part = jnp.dot(value, q_block, preferred_element_type=F32)
            total = part if total is None else total + part
    out_ref[...] = total


VMEM = pl.BlockSpec(memory_space=pltpu.VMEM)
SMEM = pl.BlockSpec(memory_space=pltpu.SMEM)


def call(kernel, outs, args, flops, smem=0, scratch=()):
    moved = sum(a.size * a.dtype.itemsize for a in (*args, *outs))
    return pl.pallas_call(
        kernel,
        out_shape=outs,
        in_specs=[SMEM] * smem + [VMEM] * (len(args) - smem),
        out_specs=[VMEM] * len(outs),
        scratch_shapes=list(scratch),
        cost_estimate=pl.CostEstimate(flops=flops, bytes_accessed=moved, transcendentals=0),
        compiler_params=pltpu.CompilerParams(vmem_limit_bytes=24 * 1024 * 1024),
    )(*args)


def shape(dims, dtype):
    return jax.ShapeDtypeStruct(dims, dtype)


def after(value, *others):
    return lax.optimization_barrier((value, *others))[0]


def body(queries, passages, neighbor_lists, positives, weights):
    pb, count = lax.axis_size("pb"), lax.axis_size("pa")
    rows, width = passages.shape[1:]
    q_rows = rows * pb
    tables = relay_tables(count)
    flops = 2 * rows * q_rows * width

    def move(value, name):
        return lax.ppermute(value, "pa", tables[name])

    def from_member(value, r):
        return lax.ppermute(value, "pb", [(i, (i + r) % pb) for i in range(pb)])

    def others(value):
        return [from_member(value, r) for r in range(1, pb)]

    yp, xp = move(passages[0], "y"), move(passages[0], "x")
    yq, xq = move(queries[0], "y"), move(queries[0], "x")
    own_score, own_ml, full_q, own_p, side, where = call(
        lambda *refs: own_kernel(count, pb, *refs),
        [
            shape((rows, q_rows), F32),
            shape((8, q_rows), F32),
            shape((q_rows, width), BF16),
            shape((rows, width), BF16),
            shape((16, q_rows), F32),
            shape((1, q_rows), jnp.int32),
        ],
        [neighbor_lists, weights, positives, passages[0], queries[0], *others(queries[0])],
        flops,
        smem=1,
    )
    zap, zbp, dp = move(yp, "za"), move(xp, "zb"), move(xp, "y")
    xzp = move(after(zap, xq, yq, own_ml), "x")
    middle, middle_ml = call(
        middle_kernel,
        [shape(((LAST - 1) * rows, q_rows), F32), shape((8, q_rows), F32)],
        [full_q, side, own_ml, xp, yp, dp, zap, zbp],
        (LAST - 1) * flops,
    )
    yq2, xq2 = after(yq, zbp), after(xq, zbp)
    zaq, zbq, dq = move(yq2, "za"), move(xq2, "zb"), move(xq2, "y")
    xzq = move(zaq, "x")
    stat_rows = -(-(3 * pb + 1) // 8) * 8
    last, ml, stat = call(
        lambda *refs: last_kernel(pb, *refs),
        [shape((rows, q_rows), F32), shape((8, q_rows), F32), shape((stat_rows, rows), F32)],
        [full_q, side, middle_ml, xzp],
        flops,
    )
    four = jnp.stack([stat, move(stat, "x"), move(stat, "y"), move(stat, "d")])
    up, down = move(four, "up"), move(four, "down")
    parts = call(
        lambda *refs: query_kernel(pb, *refs),
        [shape((rows, width), F32)] + [shape((rows, width), BF16)] * (pb - 1),
        [own_score, middle, last, side, where, ml, *others(ml), own_p, xp, yp, dp, zap, zbp, xzp],
        WINDOW * flops,
        scratch=[pltpu.VMEM((WINDOW * rows, q_rows), BF16)],
    )
    arrived = [from_member(parts[r], r) for r in range(1, pb)]

    pieces = []
    for block in (xq, yq, dq, zaq, zbq, xzq):
        pieces += [block, *others(block)]
    split = (LAST - 1) * pb
    (early_cross,) = call(
        cross_kernel, [shape((rows, LAST * q_rows), F32)], [own_p, full_q, *pieces[:split]], LAST * flops
    )
    (late_cross,) = call(cross_kernel, [shape((rows, q_rows), F32)], [own_p, *pieces[split:]], flops)
    stats = [four, *others(four), up, *others(up), down, *others(down)]
    passage_grad, query_grad = call(
        lambda *refs: passage_kernel(pb, *refs),
        [shape((rows, width), F32)] * 2,
        [early_cross, late_cross, where, parts[0], *arrived, *stats, full_q, *pieces],
        WINDOW * flops,
        scratch=[pltpu.VMEM((pb, rows), F32)] * 2,
    )
    return (query_grad[None], passage_grad[None])


def solution(mesh):
    return jax.shard_map(
        body,
        mesh=mesh,
        in_specs=(
            P("pa", "pb", None),
            P("pa", "pb", None),
            P("pa", None),
            P("pa", None),
            P("pa", None),
        ),
        out_specs=(P("pa", "pb", None), P("pa", "pb", None)),
        check_vma=False,
    )
```

time: 71.2 us -> 54 us (0.76)
  waiting for transfers between devices: 31.6 us -> 19 us
  blocking collectives: 2.51 us -> 0 us
  starting transfers between devices: 26.1 us -> 25 us
  local copies, waits for them, and re-layouts: 2.81 us -> 1.91 us
  other arithmetic: 0.9 us -> 0.01 us
  Pallas kernels: 6.31 us -> 7.1 us
    ppermute x17, waiting for transfers between devices: 30 us -> 18.9 us  [move(): return lax.ppermute(value, 'pa', tables[name])]
    all_gather x1 -> x0, blocking collectives: 2.51 us -> none  [body(): full_q = lax.all_gather(own_q, 'pb', axis=0, tiled=True)]
    ppermute x17, starting transfers between devices: 24.7 us -> 22.7 us  [move(): return lax.ppermute(value, 'pa', tables[name])]
    ppermute x9 -> x12, waiting for transfers between devices: 1.6 us -> 0.03 us  [from_member(): return lax.ppermute(value, 'pb', [(i, (i + r) % pb) for i in range(pb)])]
    ppermute x9 -> x12, starting transfers between devices: 1.33 us -> 2.35 us  [from_member(): return lax.ppermute(value, 'pb', [(i, (i + r) % pb) for i in range(pb)])]
    unnamed x17 -> x10, local copies, waits for them, and re-layouts: 2.81 us -> 1.91 us
    broadcast_in_dim x1 -> x0, other arithmetic: 0.85 us -> none  [body(): return (query_grad[None], passage_grad[None])]
    pallas_call x4 -> x7, Pallas kernels: 6.31 us -> 7.1 us  [call(): pl.pallas_call(kernel, out_shape=outs, in_specs=[SMEM] * smem + [VMEM] *...]
  transfers between devices with their start and end apart: 26 -> 29, of which waited for: 12 -> 9; matrix products, arithmetic and copies ran while one was open for 0% -> 0% of each run, Pallas kernels for 9% -> 9%
where the time goes in v2:
time: 54 us; the launch traced here: 53.8 us
  starting transfers between devices  25 us (46%)
  waiting for transfers between devices  19 us (35%)
  Pallas kernels  7.1 us (13%)
  local copies, waits for them, and re-layouts  1.91 us (4%)
  between operations  0.8 us (1%)
    ppermute x17, starting transfers between devices, move(): return lax.ppermute(value, 'pa', tables[name])  22.7 us
    ppermute x17, waiting for transfers between devices, move(): return lax.ppermute(value, 'pa', tables[name])  18.9 us
    pallas_call x7, Pallas kernels, call(): pl.pallas_call(kernel, out_shape=outs, in_specs=[SMEM] * smem + [VMEM] *...  7.1 us
    ppermute x12, starting transfers between devices, from_member(): return lax.ppermute(value, 'pb', [(i, (i + r) % pb) for i in range(pb)])  2.35 us
    unnamed x10, local copies, waits for them, and re-layouts  1.91 us
  transfers between devices with their start and end apart: 29, of which 9 were waited for; matrix products, arithmetic and copies ran while one was open for 0% of the time, Pallas kernels for 9%

profile of v2, /device:TPU:0, one launch (start us, length us, event | category | flops | bytes accessed | tf_op | source)
XLA Modules:
  0.0 53.8 jit_solution(9132736164926677435)
XLA Ops:
  0.7 3.0 %collective-permute-start.15 = (bf16[128,1024]{1,0:T(8,128)(2,1)}, bf16[128,1024]{1,0:T(8,128)(2,1)S(1)}, u32[]{:S(2)}, u32[]{:S(2)}) collective-permute-start(bf16[128,1024]{1,0:T(8,128)(2,1)} %bitcast.8), channel_id=1, source_target_pairs={{0,2},{1,3},{2,0},{3,1},{4,6},{5,7},{6,4},{7,5},{8,10},{9,11},{10,... | collective-permute-start | bytes 786440 | tf_op jit(solution)/shard_map/ppermute | solution.py:255
  3.7 1.5 %collective-permute-start.5 = (bf16[128,1024]{1,0:T(8,128)(2,1)}, bf16[128,1024]{1,0:T(8,128)(2,1)S(1)}, u32[]{:S(2)}, u32[]{:S(2)}) collective-permute-start(bf16[128,1024]{1,0:T(8,128)(2,1)} %bitcast.9), channel_id=1, source_target_pairs={{0,1},{1,0},{2,3},{3,2},{4,5},{5,4},{6,7},{7,6},{8,9},{9,8},{10,11... | collective-permute-start | bytes 786440 | tf_op jit(solution)/shard_map/ppermute | solution.py:255
  5.2 0.5 collective-permute-start.1
  5.7 0.1 collective-permute-start.3
  5.8 5.2 %collective-permute-done.15.refs_1_.refs_9_ = bf16[128,1024]{1,0:T(8,128)(2,1)S(1)} collective-permute-done((bf16[128,1024]{1,0:T(8,128)(2,1)}, bf16[128,1024]{1,0:T(8,128)(2,1)S(1)}, u32[]{:S(2)}, u32[]{:S(2)}) %collective-permute-start.15) | collective-permute-done | bytes 262176 | tf_op jit(solution)/shard_map/ppermute | solution.py:255
  11.0 2.1 %collective-permute-start.17 = (bf16[128,1024]{1,0:T(8,128)(2,1)S(1)}, bf16[128,1024]{1,0:T(8,128)(2,1)S(1)}, u32[]{:S(2)}, u32[]{:S(2)}) collective-permute-start(bf16[128,1024]{1,0:T(8,128)(2,1)S(1)} %collective-permute-done.15.refs_1_.refs_9_), channel_id=1, source_target_pairs={{0,4},{1,5},{2,14},{3,15},{4,8},{5,9},{6,2},{7,3},{8,12},{9,13},{1... | collective-permute-start | bytes 786440 | tf_op jit(solution)/shard_map/ppermute | solution.py:255
  13.2 0.0 collective-permute-done.5.refs_0_.refs_8_
  13.2 1.6 %collective-permute-start.6 = (bf16[128,1024]{1,0:T(8,128)(2,1)S(1)}, bf16[128,1024]{1,0:T(8,128)(2,1)S(1)}, u32[]{:S(2)}, u32[]{:S(2)}) collective-permute-start(bf16[128,1024]{1,0:T(8,128)(2,1)S(1)} %collective-permute-done.5.refs_0_.refs_8_), channel_id=1, source_target_pairs={{0,4},{1,13},{2,6},{3,15},{4,8},{5,1},{6,10},{7,3},{8,12},{9,5},{1... | collective-permute-start | bytes 786440 | tf_op jit(solution)/shard_map/ppermute | solution.py:255
  14.7 0.0 collective-permute-done.refs_5_
  14.7 2.0 %collective-permute-start.16 = (bf16[128,1024]{1,0:T(8,128)(2,1)S(1)}, bf16[128,1024]{1,0:T(8,128)(2,1)S(1)}, u32[]{:S(2)}, u32[]{:S(2)}) collective-permute-start(bf16[128,1024]{1,0:T(8,128)(2,1)S(1)} %collective-permute-done.5.refs_0_.refs_8_), channel_id=1, source_target_pairs={{0,2},{1,3},{2,0},{3,1},{4,6},{5,7},{6,4},{7,5},{8,10},{9,11},{10,... | collective-permute-start | bytes 786440 | tf_op jit(solution)/shard_map/ppermute | solution.py:255
  16.8 0.9 %copy-done = bf16[1,128,1024]{2,1,0:T(8,128)(2,1)S(1)} copy-done((bf16[1,128,1024]{2,1,0:T(8,128)(2,1)S(1)}, bf16[1,128,1024]{2,1,0:T(8,128)(2,1)}, u32[]{:S(2)}) %copy-start) | copy-done | bytes 262168
  17.7 0.9 %copy-done.1 = bf16[1,128,1024]{2,1,0:T(8,128)(2,1)S(1)} copy-done((bf16[1,128,1024]{2,1,0:T(8,128)(2,1)S(1)}, bf16[1,128,1024]{2,1,0:T(8,128)(2,1)}, u32[]{:S(2)}) %copy-start.1) | copy-done | bytes 262168
  18.7 1.0 %shard_map.68 = (f32[128,256]{1,0:T(8,128)S(1)}, f32[8,256]{1,0:T(8,128)S(1)}, bf16[256,1024]{1,0:T(8,128)(2,1)S(1)}, bf16[128,1024]{1,0:T(8,128)(2,1)S(1)}, f32...) custom-call(s32[1,7]{1,0:T(1,128)S(1)} %copy-done.4, f32[1,256]{1,0:T(1,128)S(1)} %copy-done.2, s32[1,256]{1,0:T(1,128)S(1)} %copy-done.3, ...), custom_call_target="tpu_custom_call" | custom-call | flops 67108864 | bytes 1731612 | tf_op jit(solution)/shard_map/pallas_call | solution.py:228
  19.7 2.6 %collective-permute-done.17.refs_3_.refs_11_ = bf16[128,1024]{1,0:T(8,128)(2,1)S(1)} collective-permute-done((bf16[128,1024]{1,0:T(8,128)(2,1)S(1)}, bf16[128,1024]{1,0:T(8,128)(2,1)S(1)}, u32[]{:S(2)}, u32[]{:S(2)}) %collective-permute-start.17) | collective-permute-done | bytes 262176 | tf_op jit(solution)/shard_map/ppermute | solution.py:255
  22.3 1.5 %collective-permute-start.18 = (bf16[128,1024]{1,0:T(8,128)(2,1)S(1)}, bf16[128,1024]{1,0:T(8,128)(2,1)S(1)}, u32[]{:S(2)}, u32[]{:S(2)}) collective-permute-start(bf16[128,1024]{1,0:T(8,128)(2,1)S(1)} %collective-permute-done.17.refs_3_.refs_11_), channel_id=1, source_target_pairs={{0,1},{1,0},{2,3},{3,2},{4,5},{5,4},{6,7},{7,6},{8,9},{9,8},{10,11... | collective-permute-start | bytes 786440 | tf_op jit(solution)/shard_map/ppermute | solution.py:255
  23.8 1.3 %collective-permute-done.6.refs_4_.refs_12_ = bf16[128,1024]{1,0:T(8,128)(2,1)S(1)} collective-permute-done((bf16[128,1024]{1,0:T(8,128)(2,1)S(1)}, bf16[128,1024]{1,0:T(8,128)(2,1)S(1)}, u32[]{:S(2)}, u32[]{:S(2)}) %collective-permute-start.6) | collective-permute-done | bytes 262176 | tf_op jit(solution)/shard_map/ppermute | solution.py:255
  25.1 0.0 collective-permute-start.2
  25.1 0.5 collective-permute-start.4
  25.6 0.0 collective-permute-done.16.refs_2_.refs_10_
  25.6 1.1 %shard_map.71 = (f32[640,256]{1,0:T(8,128)S(1)}, f32[8,256]{1,0:T(8,128)S(1)}) custom-call(bf16[256,1024]{1,0:T(8,128)(2,1)S(1)} %get-tuple-element.21.refs_0_.full_ref.refs_11_, f32[16,256]{1,0:T(8,128)S(1)} %get-tuple-element.26.side_ref.refs_1_.refs_3_, f32[8,256]{1,0:T(8,128)S(1)} %get-tuple-element.27.before_ref, ...), custom_call_target="tpu_custom_call" | custom-call | flops 335544320 | bytes 2523136 | tf_op jit(solution)/shard_map/pallas_call | solution.py:228
  26.8 1.9 %collective-permute-done.18.refs_3_.refs_13_ = bf16[128,1024]{1,0:T(8,128)(2,1)S(1)} collective-permute-done((bf16[128,1024]{1,0:T(8,128)(2,1)S(1)}, bf16[128,1024]{1,0:T(8,128)(2,1)S(1)}, u32[]{:S(2)}, u32[]{:S(2)}) %collective-permute-start.18) | collective-permute-done | bytes 262176 | tf_op jit(solution)/shard_map/ppermute | solution.py:255
  28.7 0.4 shard_map.72
  29.0 1.6 %collective-permute-start.21 = (f32[8,128]{1,0:T(8,128)S(1)}, f32[8,128]{1,0:T(8,128)S(1)}, u32[]{:S(2)}, u32[]{:S(2)}) collective-permute-start(f32[8,128]{1,0:T(8,128)S(1)} %get-tuple-element.35), channel_id=1, source_target_pairs={{0,1},{1,0},{2,3},{3,2},{4,5},{5,4},{6,7},{7,6},{8,9},{9,8},{10,11... | collective-permute-start | bytes 12296 | tf_op jit(solution)/shard_map/ppermute | solution.py:255
  30.6 3.1 %collective-permute-start.22 = (f32[8,128]{1,0:T(8,128)S(1)}, f32[8,128]{1,0:T(8,128)S(1)}, u32[]{:S(2)}, u32[]{:S(2)}) collective-permute-start(f32[8,128]{1,0:T(8,128)S(1)} %get-tuple-element.35), channel_id=1, source_target_pairs={{0,2},{1,3},{2,0},{3,1},{4,6},{5,7},{6,4},{7,5},{8,10},{9,11},{10,... | collective-permute-start | bytes 12296 | tf_op jit(solution)/shard_map/ppermute | solution.py:255
  33.7 1.3 %collective-permute-start.23 = (f32[8,128]{1,0:T(8,128)S(1)}, f32[8,128]{1,0:T(8,128)S(1)}, u32[]{:S(2)}, u32[]{:S(2)}) collective-permute-start(f32[8,128]{1,0:T(8,128)S(1)} %get-tuple-element.35), channel_id=1, source_target_pairs={{0,3},{1,2},{2,1},{3,0},{4,7},{5,6},{6,5},{7,4},{8,11},{9,10},{10,... | collective-permute-start | bytes 12296 | tf_op jit(solution)/shard_map/ppermute | solution.py:255
  35.0 0.0 collective-permute-done.21
  35.0 0.0 collective-permute-start.11
  35.0 0.3 collective-permute-done.22
  35.3 2.0 %collective-permute-start.7 = (bf16[128,1024]{1,0:T(8,128)(2,1)S(1)}, bf16[128,1024]{1,0:T(8,128)(2,1)S(1)}, u32[]{:S(2)}, u32[]{:S(2)}) collective-permute-start(bf16[128,1024]{1,0:T(8,128)(2,1)S(1)} %collective-permute-done.1.refs_1_.refs_12_), channel_id=1, source_target_pairs={{0,2},{1,3},{2,0},{3,1},{4,6},{5,7},{6,4},{7,5},{8,10},{9,11},{10,... | collective-permute-start | bytes 786440 | tf_op jit(solution)/shard_map/ppermute | solution.py:255
  37.3 1.0 %collective-permute-done.23 = f32[8,128]{1,0:T(8,128)S(1)} collective-permute-done((f32[8,128]{1,0:T(8,128)S(1)}, f32[8,128]{1,0:T(8,128)S(1)}, u32[]{:S(2)}, u32[]{:S(2)}) %collective-permute-start.23) | collective-permute-done | bytes 4128 | tf_op jit(solution)/shard_map/ppermute | solution.py:255
  38.3 1.7 %collective-permute-start.13 = (bf16[128,1024]{1,0:T(8,128)(2,1)S(1)}, bf16[128,1024]{1,0:T(8,128)(2,1)S(1)}, u32[]{:S(2)}, u32[]{:S(2)}) collective-permute-start(bf16[128,1024]{1,0:T(8,128)(2,1)S(1)} %collective-permute-done.9.refs_7_.refs_18_), channel_id=1, source_target_pairs={{0,1},{1,0},{2,3},{3,2},{4,5},{5,4},{6,7},{7,6},{8,9},{9,8},{10,11... | collective-permute-start | bytes 786440 | tf_op jit(solution)/shard_map/ppermute | solution.py:255
  40.0 0.0 collective-permute-done.2.refs_2_.refs_13_
  40.0 0.0 collective-permute-done.4.refs_4_.refs_15_
  40.0 0.1 collective-permute-start.19
  40.1 3.7 %collective-permute-done.11.refs_9_.refs_20_ = bf16[128,1024]{1,0:T(8,128)(2,1)S(1)} collective-permute-done((bf16[128,1024]{1,0:T(8,128)(2,1)S(1)}, bf16[128,1024]{1,0:T(8,128)(2,1)S(1)}, u32[]{:S(2)}, u32[]{:S(2)}) %collective-permute-start.11) | collective-permute-done | bytes 262176 | tf_op jit(solution)/shard_map/ppermute | solution.py:255
  43.8 0.5 collective-permute-start.12
  44.3 0.1 collective-permute-start.8
  44.4 1.2 %collective-permute-done.25.refs_7_ = f32[4,8,128]{2,1,0:T(8,128)S(1)} collective-permute-done((f32[4,8,128]{2,1,0:T(8,128)S(1)}, f32[4,8,128]{2,1,0:T(8,128)S(1)}, u32[]{:S(2)}, u32[]{:S(2)}) %collective-permute-start.25) | collective-permute-done | bytes 16416 | tf_op jit(solution)/shard_map/ppermute | solution.py:255
  45.5 0.7 %collective-permute-start.27 = (f32[4,8,128]{2,1,0:T(8,128)S(1)}, f32[4,8,128]{2,1,0:T(8,128)S(1)}, u32[]{:S(2)}, u32[]{:S(2)}) collective-permute-start(f32[4,8,128]{2,1,0:T(8,128)S(1)} %pad_maximum_fusion.refs_5_), channel_id=1, source_target_pairs={{0,12},{1,13},{2,14},{3,15},{4,0},{5,1},{6,2},{7,3},{8,4},{9,5},{1... | collective-permute-start | bytes 49160 | tf_op jit(solution)/shard_map/ppermute | solution.py:255
  46.2 0.2 collective-permute-start.14
  46.4 1.2 %shard_map.73 = (f32[128,1024]{1,0:T(8,128)S(1)}, bf16[128,1024]{1,0:T(8,128)(2,1)S(1)}) custom-call(f32[128,256]{1,0:T(8,128)S(1)} %get-tuple-element.25.refs_0_, f32[640,256]{1,0:T(8,128)S(1)} %get-tuple-element.28.refs_1_, f32[128,256]{1,0:T(8,128)S(1)} %get-tuple-element.31.refs_2_, f32[16,256]{1,0:T(8,128)S(1)} %get-tuple-element.26.side_ref.refs_1_.refs_3_, ...), custom_call_target="tpu_custom_call" | custom-call | flops 469762048 | bytes 3572736 | tf_op jit(solution)/shard_map/pallas_call | solution.py:228
  47.6 1.7 %collective-permute-done.27.refs_9_ = f32[4,8,128]{2,1,0:T(8,128)S(1)} collective-permute-done((f32[4,8,128]{2,1,0:T(8,128)S(1)}, f32[4,8,128]{2,1,0:T(8,128)S(1)}, u32[]{:S(2)}, u32[]{:S(2)}) %collective-permute-start.27) | collective-permute-done | bytes 16416 | tf_op jit(solution)/shard_map/ppermute | solution.py:255
  49.3 0.5 collective-permute-start.24
  49.8 0.1 collective-permute-start.26
  49.9 0.4 collective-permute-start.28
  50.3 1.0 %shard_map.69.refs_0_ = f32[128,1536]{1,0:T(8,128)S(1)} custom-call(bf16[128,1024]{1,0:T(8,128)(2,1)S(1)} %get-tuple-element.20.p_ref.refs_7_, bf16[256,1024]{1,0:T(8,128)(2,1)S(1)} %get-tuple-element.21.refs_0_.full_ref.refs_11_, bf16[128,1024]{1,0:T(8,128)(2,1)S(1)} %collective-permute-done.1.refs_1_.refs_12_, ...), custom_call_target="tpu_custom_call" | custom-call | flops 402653184 | bytes 4194304 | tf_op jit(solution)/shard_map/pallas_call | solution.py:228
  51.3 0.3 shard_map.70.refs_1_
  51.7 2.2 %shard_map.74 = (f32[128,1024]{1,0:T(8,128)}, f32[128,1024]{1,0:T(8,128)}) custom-call(f32[128,1536]{1,0:T(8,128)S(1)} %shard_map.69.refs_0_, f32[128,256]{1,0:T(8,128)S(1)} %shard_map.70.refs_1_, s32[1,256]{1,0:T(1,128)S(1)} %get-tuple-element.24.refs_4_.refs_2_, f32[128,1024]{1,0:T(8,128)S(1)} %get-tuple-element.33.refs_3_, ...), custom_call_target="tpu_custom_call" | custom-call | flops 469762048 | bytes 6521856 | tf_op jit(solution)/shard_map/pallas_call | solution.py:228
  (28 shorter events, 0.1 us)
Async XLA Ops:
  0.6 16.1 %copy-start.3 = (s32[1,256]{1,0:T(1,128)S(1)}, s32[1,256]{1,0:T(1,128)}, u32[]{:S(2)}) copy-start(s32[1,256]{1,0:T(1,128)} %refs_2_.1) | copy-start | bytes 3076
  0.6 16.1 %copy-start.2 = (f32[1,256]{1,0:T(1,128)S(1)}, f32[1,256]{1,0:T(1,128)}, u32[]{:S(2)}) copy-start(f32[1,256]{1,0:T(1,128)} %refs_1_.1) | copy-start | bytes 3076
  0.7 16.1 %copy-start.4 = (s32[1,7]{1,0:T(1,128)S(1)}, s32[1,7]{1,0:T(1,128)}, u32[]{:S(2)}) copy-start(s32[1,7]{1,0:T(1,128)} %refs_0_.1) | copy-start | bytes 88
  0.7 10.4 %collective-permute-start.15 = (bf16[128,1024]{1,0:T(8,128)(2,1)}, bf16[128,1024]{1,0:T(8,128)(2,1)S(1)}, u32[]{:S(2)}, u32[]{:S(2)}) collective-permute-start(bf16[128,1024]{1,0:T(8,128)(2,1)} %bitcast.8), channel_id=1, source_target_pairs={{0,2},{1,3},{2,0},{3,1},{4,6},{5,7},{6,4},{7,5},{8,10},{9,11},{10,... | collective-permute-start | bytes 786440 | tf_op jit(solution)/shard_map/ppermute | solution.py:255
  3.7 9.5 %collective-permute-start.5 = (bf16[128,1024]{1,0:T(8,128)(2,1)}, bf16[128,1024]{1,0:T(8,128)(2,1)S(1)}, u32[]{:S(2)}, u32[]{:S(2)}) collective-permute-start(bf16[128,1024]{1,0:T(8,128)(2,1)} %bitcast.9), channel_id=1, source_target_pairs={{0,1},{1,0},{2,3},{3,2},{4,5},{5,4},{6,7},{7,6},{8,9},{9,8},{10,11... | collective-permute-start | bytes 786440 | tf_op jit(solution)/shard_map/ppermute | solution.py:255
  5.2 9.6 %collective-permute-start = (bf16[128,1024]{1,0:T(8,128)(2,1)}, bf16[128,1024]{1,0:T(8,128)(2,1)S(1)}, u32[]{:S(2)}, u32[]{:S(2)}) collective-permute-start(bf16[128,1024]{1,0:T(8,128)(2,1)} %bitcast.11), channel_id=1, source_target_pairs={{0,16},{16,0},{1,17},{17,1},{2,18},{18,2},{3,19},{19,3},{4,20},{20... | collective-permute-start | bytes 786440 | tf_op jit(solution)/shard_map/ppermute | solution.py:258
  5.2 14.5 %collective-permute-start.1 = (bf16[128,1024]{1,0:T(8,128)(2,1)}, bf16[128,1024]{1,0:T(8,128)(2,1)S(1)}, u32[]{:S(2)}, u32[]{:S(2)}) collective-permute-start(bf16[128,1024]{1,0:T(8,128)(2,1)} %bitcast.12), channel_id=1, source_target_pairs={{0,1},{1,0},{2,3},{3,2},{4,5},{5,4},{6,7},{7,6},{8,9},{9,8},{10,11... | collective-permute-start | bytes 786440 | tf_op jit(solution)/shard_map/ppermute | solution.py:255
  5.7 13.9 %collective-permute-start.3 = (bf16[128,1024]{1,0:T(8,128)(2,1)}, bf16[128,1024]{1,0:T(8,128)(2,1)S(1)}, u32[]{:S(2)}, u32[]{:S(2)}) collective-permute-start(bf16[128,1024]{1,0:T(8,128)(2,1)} %bitcast.13), channel_id=1, source_target_pairs={{0,2},{1,3},{2,0},{3,1},{4,6},{5,7},{6,4},{7,5},{8,10},{9,11},{10,... | collective-permute-start | bytes 786440 | tf_op jit(solution)/shard_map/ppermute | solution.py:255
  11.0 11.3 %collective-permute-start.17 = (bf16[128,1024]{1,0:T(8,128)(2,1)S(1)}, bf16[128,1024]{1,0:T(8,128)(2,1)S(1)}, u32[]{:S(2)}, u32[]{:S(2)}) collective-permute-start(bf16[128,1024]{1,0:T(8,128)(2,1)S(1)} %collective-permute-done.15.refs_1_.refs_9_), channel_id=1, source_target_pairs={{0,4},{1,5},{2,14},{3,15},{4,8},{5,9},{6,2},{7,3},{8,12},{9,13},{1... | collective-permute-start | bytes 786440 | tf_op jit(solution)/shard_map/ppermute | solution.py:255
  13.2 12.0 %collective-permute-start.6 = (bf16[128,1024]{1,0:T(8,128)(2,1)S(1)}, bf16[128,1024]{1,0:T(8,128)(2,1)S(1)}, u32[]{:S(2)}, u32[]{:S(2)}) collective-permute-start(bf16[128,1024]{1,0:T(8,128)(2,1)S(1)} %collective-permute-done.5.refs_0_.refs_8_), channel_id=1, source_target_pairs={{0,4},{1,13},{2,6},{3,15},{4,8},{5,1},{6,10},{7,3},{8,12},{9,5},{1... | collective-permute-start | bytes 786440 | tf_op jit(solution)/shard_map/ppermute | solution.py:255
  14.7 10.9 %collective-permute-start.16 = (bf16[128,1024]{1,0:T(8,128)(2,1)S(1)}, bf16[128,1024]{1,0:T(8,128)(2,1)S(1)}, u32[]{:S(2)}, u32[]{:S(2)}) collective-permute-start(bf16[128,1024]{1,0:T(8,128)(2,1)S(1)} %collective-permute-done.5.refs_0_.refs_8_), channel_id=1, source_target_pairs={{0,2},{1,3},{2,0},{3,1},{4,6},{5,7},{6,4},{7,5},{8,10},{9,11},{10,... | collective-permute-start | bytes 786440 | tf_op jit(solution)/shard_map/ppermute | solution.py:255
  16.8 1.0 %copy-start = (bf16[1,128,1024]{2,1,0:T(8,128)(2,1)S(1)}, bf16[1,128,1024]{2,1,0:T(8,128)(2,1)}, u32[]{:S(2)}) copy-start(bf16[1,128,1024]{2,1,0:T(8,128)(2,1)} %param.6) | copy-start | bytes 786436
  17.7 0.9 %copy-start.1 = (bf16[1,128,1024]{2,1,0:T(8,128)(2,1)S(1)}, bf16[1,128,1024]{2,1,0:T(8,128)(2,1)}, u32[]{:S(2)}) copy-start(bf16[1,128,1024]{2,1,0:T(8,128)(2,1)} %param.5) | copy-start | bytes 786436
  22.3 6.4 %collective-permute-start.18 = (bf16[128,1024]{1,0:T(8,128)(2,1)S(1)}, bf16[128,1024]{1,0:T(8,128)(2,1)S(1)}, u32[]{:S(2)}, u32[]{:S(2)}) collective-permute-start(bf16[128,1024]{1,0:T(8,128)(2,1)S(1)} %collective-permute-done.17.refs_3_.refs_11_), channel_id=1, source_target_pairs={{0,1},{1,0},{2,3},{3,2},{4,5},{5,4},{6,7},{7,6},{8,9},{9,8},{10,11... | collective-permute-start | bytes 786440 | tf_op jit(solution)/shard_map/ppermute | solution.py:255
  25.1 8.6 %collective-permute-start.9 = (bf16[128,1024]{1,0:T(8,128)(2,1)S(1)}, bf16[128,1024]{1,0:T(8,128)(2,1)S(1)}, u32[]{:S(2)}, u32[]{:S(2)}) collective-permute-start(bf16[128,1024]{1,0:T(8,128)(2,1)S(1)} %collective-permute-done.3.refs_3_.refs_14_), channel_id=1, source_target_pairs={{0,4},{1,5},{2,14},{3,15},{4,8},{5,9},{6,2},{7,3},{8,12},{9,13},{1... | collective-permute-start | bytes 786440 | tf_op jit(solution)/shard_map/ppermute | solution.py:255
  25.1 14.9 %collective-permute-start.2 = (bf16[128,1024]{1,0:T(8,128)(2,1)S(1)}, bf16[128,1024]{1,0:T(8,128)(2,1)S(1)}, u32[]{:S(2)}, u32[]{:S(2)}) collective-permute-start(bf16[128,1024]{1,0:T(8,128)(2,1)S(1)} %collective-permute-done.1.refs_1_.refs_12_), channel_id=1, source_target_pairs={{0,16},{16,0},{1,17},{17,1},{2,18},{18,2},{3,19},{19,3},{4,20},{20... | collective-permute-start | bytes 786440 | tf_op jit(solution)/shard_map/ppermute | solution.py:258
  25.1 14.9 %collective-permute-start.4 = (bf16[128,1024]{1,0:T(8,128)(2,1)S(1)}, bf16[128,1024]{1,0:T(8,128)(2,1)S(1)}, u32[]{:S(2)}, u32[]{:S(2)}) collective-permute-start(bf16[128,1024]{1,0:T(8,128)(2,1)S(1)} %collective-permute-done.3.refs_3_.refs_14_), channel_id=1, source_target_pairs={{0,16},{16,0},{1,17},{17,1},{2,18},{18,2},{3,19},{19,3},{4,20},{20... | collective-permute-start | bytes 786440 | tf_op jit(solution)/shard_map/ppermute | solution.py:258
  29.0 5.9 %collective-permute-start.21 = (f32[8,128]{1,0:T(8,128)S(1)}, f32[8,128]{1,0:T(8,128)S(1)}, u32[]{:S(2)}, u32[]{:S(2)}) collective-permute-start(f32[8,128]{1,0:T(8,128)S(1)} %get-tuple-element.35), channel_id=1, source_target_pairs={{0,1},{1,0},{2,3},{3,2},{4,5},{5,4},{6,7},{7,6},{8,9},{9,8},{10,11... | collective-permute-start | bytes 12296 | tf_op jit(solution)/shard_map/ppermute | solution.py:255
  30.6 4.6 %collective-permute-start.22 = (f32[8,128]{1,0:T(8,128)S(1)}, f32[8,128]{1,0:T(8,128)S(1)}, u32[]{:S(2)}, u32[]{:S(2)}) collective-permute-start(f32[8,128]{1,0:T(8,128)S(1)} %get-tuple-element.35), channel_id=1, source_target_pairs={{0,2},{1,3},{2,0},{3,1},{4,6},{5,7},{6,4},{7,5},{8,10},{9,11},{10,... | collective-permute-start | bytes 12296 | tf_op jit(solution)/shard_map/ppermute | solution.py:255
  33.7 4.6 %collective-permute-start.23 = (f32[8,128]{1,0:T(8,128)S(1)}, f32[8,128]{1,0:T(8,128)S(1)}, u32[]{:S(2)}, u32[]{:S(2)}) collective-permute-start(f32[8,128]{1,0:T(8,128)S(1)} %get-tuple-element.35), channel_id=1, source_target_pairs={{0,3},{1,2},{2,1},{3,0},{4,7},{5,6},{6,5},{7,4},{8,11},{9,10},{10,... | collective-permute-start | bytes 12296 | tf_op jit(solution)/shard_map/ppermute | solution.py:255
  35.0 8.8 %collective-permute-start.11 = (bf16[128,1024]{1,0:T(8,128)(2,1)S(1)}, bf16[128,1024]{1,0:T(8,128)(2,1)S(1)}, u32[]{:S(2)}, u32[]{:S(2)}) collective-permute-start(bf16[128,1024]{1,0:T(8,128)(2,1)S(1)} %collective-permute-done.1.refs_1_.refs_12_), channel_id=1, source_target_pairs={{0,4},{1,13},{2,6},{3,15},{4,8},{5,1},{6,10},{7,3},{8,12},{9,5},{1... | collective-permute-start | bytes 786440 | tf_op jit(solution)/shard_map/ppermute | solution.py:255
  35.3 8.5 %collective-permute-start.7 = (bf16[128,1024]{1,0:T(8,128)(2,1)S(1)}, bf16[128,1024]{1,0:T(8,128)(2,1)S(1)}, u32[]{:S(2)}, u32[]{:S(2)}) collective-permute-start(bf16[128,1024]{1,0:T(8,128)(2,1)S(1)} %collective-permute-done.1.refs_1_.refs_12_), channel_id=1, source_target_pairs={{0,2},{1,3},{2,0},{3,1},{4,6},{5,7},{6,4},{7,5},{8,10},{9,11},{10,... | collective-permute-start | bytes 786440 | tf_op jit(solution)/shard_map/ppermute | solution.py:255
  38.3 7.9 %collective-permute-start.13 = (bf16[128,1024]{1,0:T(8,128)(2,1)S(1)}, bf16[128,1024]{1,0:T(8,128)(2,1)S(1)}, u32[]{:S(2)}, u32[]{:S(2)}) collective-permute-start(bf16[128,1024]{1,0:T(8,128)(2,1)S(1)} %collective-permute-done.9.refs_7_.refs_18_), channel_id=1, source_target_pairs={{0,1},{1,0},{2,3},{3,2},{4,5},{5,4},{6,7},{7,6},{8,9},{9,8},{10,11... | collective-permute-start | bytes 786440 | tf_op jit(solution)/shard_map/ppermute | solution.py:255
  40.0 5.5 %collective-permute-start.25 = (f32[4,8,128]{2,1,0:T(8,128)S(1)}, f32[4,8,128]{2,1,0:T(8,128)S(1)}, u32[]{:S(2)}, u32[]{:S(2)}) collective-permute-start(f32[4,8,128]{2,1,0:T(8,128)S(1)} %pad_maximum_fusion.refs_5_), channel_id=1, source_target_pairs={{0,4},{1,5},{2,6},{3,7},{4,8},{5,9},{6,10},{7,11},{8,12},{9,13},{1... | collective-permute-start | bytes 49160 | tf_op jit(solution)/shard_map/ppermute | solution.py:255
  40.0 4.3 %collective-permute-start.19 = (f32[8,256]{1,0:T(8,128)S(1)}, f32[8,256]{1,0:T(8,128)S(1)}, u32[]{:S(2)}, u32[]{:S(2)}) collective-permute-start(f32[8,256]{1,0:T(8,128)S(1)} %get-tuple-element.32.refs_5_), channel_id=1, source_target_pairs={{0,16},{16,0},{1,17},{17,1},{2,18},{18,2},{3,19},{19,3},{4,20},{20... | collective-permute-start | bytes 24584 | tf_op jit(solution)/shard_map/ppermute | solution.py:258
  43.8 5.5 %collective-permute-start.10 = (bf16[128,1024]{1,0:T(8,128)(2,1)S(1)}, bf16[128,1024]{1,0:T(8,128)(2,1)S(1)}, u32[]{:S(2)}, u32[]{:S(2)}) collective-permute-start(bf16[128,1024]{1,0:T(8,128)(2,1)S(1)} %collective-permute-done.9.refs_7_.refs_18_), channel_id=1, source_target_pairs={{0,16},{16,0},{1,17},{17,1},{2,18},{18,2},{3,19},{19,3},{4,20},{20... | collective-permute-start | bytes 786440 | tf_op jit(solution)/shard_map/ppermute | solution.py:258
  43.8 6.0 %collective-permute-start.12 = (bf16[128,1024]{1,0:T(8,128)(2,1)S(1)}, bf16[128,1024]{1,0:T(8,128)(2,1)S(1)}, u32[]{:S(2)}, u32[]{:S(2)}) collective-permute-start(bf16[128,1024]{1,0:T(8,128)(2,1)S(1)} %collective-permute-done.11.refs_9_.refs_20_), channel_id=1, source_target_pairs={{0,16},{16,0},{1,17},{17,1},{2,18},{18,2},{3,19},{19,3},{4,20},{20... | collective-permute-start | bytes 786440 | tf_op jit(solution)/shard_map/ppermute | solution.py:258
  44.3 5.6 %collective-permute-start.8 = (bf16[128,1024]{1,0:T(8,128)(2,1)S(1)}, bf16[128,1024]{1,0:T(8,128)(2,1)S(1)}, u32[]{:S(2)}, u32[]{:S(2)}) collective-permute-start(bf16[128,1024]{1,0:T(8,128)(2,1)S(1)} %collective-permute-done.7.refs_5_.refs_16_), channel_id=1, source_target_pairs={{0,16},{16,0},{1,17},{17,1},{2,18},{18,2},{3,19},{19,3},{4,20},{20... | collective-permute-start | bytes 786440 | tf_op jit(solution)/shard_map/ppermute | solution.py:258
  45.5 3.7 %collective-permute-start.27 = (f32[4,8,128]{2,1,0:T(8,128)S(1)}, f32[4,8,128]{2,1,0:T(8,128)S(1)}, u32[]{:S(2)}, u32[]{:S(2)}) collective-permute-start(f32[4,8,128]{2,1,0:T(8,128)S(1)} %pad_maximum_fusion.refs_5_), channel_id=1, source_target_pairs={{0,12},{1,13},{2,14},{3,15},{4,0},{5,1},{6,2},{7,3},{8,4},{9,5},{1... | collective-permute-start | bytes 49160 | tf_op jit(solution)/shard_map/ppermute | solution.py:255
  46.2 5.1 %collective-permute-start.14 = (bf16[128,1024]{1,0:T(8,128)(2,1)S(1)}, bf16[128,1024]{1,0:T(8,128)(2,1)S(1)}, u32[]{:S(2)}, u32[]{:S(2)}) collective-permute-start(bf16[128,1024]{1,0:T(8,128)(2,1)S(1)} %collective-permute-done.13.refs_0_.refs_22_), channel_id=1, source_target_pairs={{0,16},{16,0},{1,17},{17,1},{2,18},{18,2},{3,19},{19,3},{4,20},{20... | collective-permute-start | bytes 786440 | tf_op jit(solution)/shard_map/ppermute | solution.py:258
  49.3 2.4 %collective-permute-start.20 = (bf16[128,1024]{1,0:T(8,128)(2,1)S(1)}, bf16[128,1024]{1,0:T(8,128)(2,1)S(1)}, u32[]{:S(2)}, u32[]{:S(2)}) collective-permute-start(bf16[128,1024]{1,0:T(8,128)(2,1)S(1)} %get-tuple-element.34), channel_id=1, source_target_pairs={{0,16},{16,0},{1,17},{17,1},{2,18},{18,2},{3,19},{19,3},{4,20},{20... | collective-permute-start | bytes 786440 | tf_op jit(solution)/shard_map/ppermute | solution.py:258
  49.3 2.3 %collective-permute-start.24 = (f32[4,8,128]{2,1,0:T(8,128)S(1)}, f32[4,8,128]{2,1,0:T(8,128)S(1)}, u32[]{:S(2)}, u32[]{:S(2)}) collective-permute-start(f32[4,8,128]{2,1,0:T(8,128)S(1)} %pad_maximum_fusion.refs_5_), channel_id=1, source_target_pairs={{0,16},{16,0},{1,17},{17,1},{2,18},{18,2},{3,19},{19,3},{4,20},{20... | collective-permute-start | bytes 49160 | tf_op jit(solution)/shard_map/ppermute | solution.py:258
  49.8 1.8 %collective-permute-start.26 = (f32[4,8,128]{2,1,0:T(8,128)S(1)}, f32[4,8,128]{2,1,0:T(8,128)S(1)}, u32[]{:S(2)}, u32[]{:S(2)}) collective-permute-start(f32[4,8,128]{2,1,0:T(8,128)S(1)} %collective-permute-done.25.refs_7_), channel_id=1, source_target_pairs={{0,16},{16,0},{1,17},{17,1},{2,18},{18,2},{3,19},{19,3},{4,20},{20... | collective-permute-start | bytes 49160 | tf_op jit(solution)/shard_map/ppermute | solution.py:258
  49.9 1.8 %collective-permute-start.28 = (f32[4,8,128]{2,1,0:T(8,128)S(1)}, f32[4,8,128]{2,1,0:T(8,128)S(1)}, u32[]{:S(2)}, u32[]{:S(2)}) collective-permute-start(f32[4,8,128]{2,1,0:T(8,128)S(1)} %collective-permute-done.27.refs_9_), channel_id=1, source_target_pairs={{0,16},{16,0},{1,17},{17,1},{2,18},{18,2},{3,19},{19,3},{4,20},{20... | collective-permute-start | bytes 49160 | tf_op jit(solution)/shard_map/ppermute | solution.py:258

commit v3 on v2

v3 whole, which is shorter than its diff:
```python
import math

import jax
import jax.numpy as jnp
from jax import lax
from jax.experimental import pallas as pl
from jax.experimental.pallas import tpu as pltpu
from jax.sharding import PartitionSpec as P

F32 = jnp.float32
BF16 = jnp.bfloat16
WINDOW = 7
LAST = WINDOW - 1

def group_shift(i, step, count):
    return (i + step + count) % count

def relay_tables(count):
    every = range(count)
    return {
        "x": [(i, i ^ 1) for i in every],
        "y": [(i, i ^ 2) for i in every],
        "d": [(i, i ^ 3) for i in every],
        "za": [(i, group_shift(i, -4 if i & 2 else 4, count)) for i in every],
        "zb": [(i, group_shift(i, -4 if i & 1 else 4, count)) for i in every],
        "up": [(i, group_shift(i, 4, count)) for i in every],
        "down": [(i, group_shift(i, -4, count)) for i in every],
    }

def window_ids(i, count):
    to_y = jnp.where((i & 2) != 0, 4, -4)
    to_x = jnp.where((i & 1) != 0, 4, -4)
    return [
        i,
        i ^ 1,
        i ^ 2,
        i ^ 3,
        ((i ^ 2) + to_y + count) % count,
        ((i ^ 1) + to_x + count) % count,
        ((i ^ 3) + to_y + count) % count,
    ]

def nt_dot(a, b):
    return lax.dot_general(a, b, (((1,), (1,)), ((), ())), preferred_element_type=F32)

def tn_dot(a, b):
    return lax.dot_general(a, b, (((0,), (0,)), ((), ())), preferred_element_type=F32)

def member_slice(member, rows):
    return pl.ds(pl.multiple_of(member * rows, rows), rows)

def fold(part, top, total):
    new_top = jnp.max(part, axis=0, keepdims=True)
    if top is None:
        return new_top, jnp.sum(jnp.exp(part - new_top), axis=0, keepdims=True)
    new_top = jnp.maximum(top, new_top)
    return new_top, total * jnp.exp(top - new_top) + jnp.sum(jnp.exp(part - new_top), axis=0, keepdims=True)

def joined(pairs):
    top = pairs[0][0]
    for other, _ in pairs[1:]:
        top = jnp.maximum(top, other)
    total = jnp.zeros_like(top)
    for other, part in pairs:
        total += part * jnp.exp(other - top)
    return top + jnp.log(total)

def own_kernel(count, pb, lists, w_ref, pos_ref, p_ref, *refs):
    q_refs, (s_ref, ml_ref, full_ref, own_ref, side_ref, where_ref) = refs[:pb], refs[pb:]
    rows, width = p_ref.shape
    scale = 1.0 / math.sqrt(width)
    ids = window_ids(lax.axis_index("pa"), count)
    me = lax.axis_index("pb")
    for r in range(pb):
        full_ref[member_slice((me - r + pb) % pb, rows), :] = q_refs[r][...]
    own_ref[...] = p_ref[...]
    where_ref[...] = pos_ref[...]
    side_ref[...] = jnp.zeros_like(side_ref)
    for t in range(WINDOW):
        hit = lists[0, 0] == ids[t]
        for s in range(1, lists.shape[1]):
            hit = jnp.logical_or(hit, lists[0, s] == ids[t])
        bias = jnp.where(hit, 0.0, -jnp.inf).astype(F32)
        side_ref[t : t + 1, :] = jnp.full((1, side_ref.shape[1]), bias, F32)
    lane = lax.broadcasted_iota(jnp.int32, (1, side_ref.shape[1]), 1)
    listed = jnp.full((1, side_ref.shape[1]), -1.0, F32)
    for s in range(lists.shape[1]):
        listed = jnp.where(lane == s, lists[0, s].astype(F32), listed)
    side_ref[WINDOW : WINDOW + 1, :] = listed
    side_ref[WINDOW + 1 : WINDOW + 2, :] = w_ref[...]
    part = nt_dot(own_ref[...], full_ref[...]) * scale + side_ref[0:1, :]
    s_ref[...] = part
    ml_ref[...] = jnp.zeros_like(ml_ref)
    ml_ref[0:1, :], ml_ref[1:2, :] = fold(part, None, None)

def score_parts(full_ref, side_ref, before_ref, p_refs, s_ref, first):
    rows, width = p_refs[0].shape
    scale = 1.0 / math.sqrt(width)
    before, total = before_ref[0:1, :], before_ref[1:2, :]
    top = before
    for n, p_ref in enumerate(p_refs):
        part = nt_dot(p_ref[...], full_ref[...]) * scale + side_ref[first + n : first + n + 1, :]
        s_ref[n * rows : (n + 1) * rows, :] = part
        top = jnp.maximum(top, jnp.max(part, axis=0, keepdims=True))
    total = total * jnp.exp(before - top)
    for n in range(len(p_refs)):
        total += jnp.sum(jnp.exp(s_ref[n * rows : (n + 1) * rows, :] - top), axis=0, keepdims=True)
    return top, total

def middle_kernel(full_ref, side_ref, before_ref, *refs):
    p_refs, (s_ref, ml_ref) = refs[:-2], refs[-2:]
    ml_ref[...] = jnp.zeros_like(ml_ref)
    ml_ref[0:1, :], ml_ref[1:2, :] = score_parts(full_ref, side_ref, before_ref, p_refs, s_ref, 1)

def last_kernel(pb, full_ref, side_ref, before_ref, p_ref, s_ref, stat_ref):
    top, total = score_parts(full_ref, side_ref, before_ref, [p_ref], s_ref, LAST)
    rows = p_ref.shape[0]
    pieces = []
    for value in (top, total, side_ref[WINDOW + 1 : WINDOW + 2, :]):
        pieces += [value[:, c * rows : (c + 1) * rows] for c in range(pb)]
    pieces.append(side_ref[WINDOW : WINDOW + 1, 0:rows])
    stat_ref[...] = jnp.zeros_like(stat_ref)
    stat_ref[0 : len(pieces), :] = jnp.concatenate(pieces, axis=0)

def log_totals(stats, pb):
    return joined([(stat[0:pb, :], stat[pb : 2 * pb, :]) for stat in stats])

def query_kernel(pb, so_ref, sm_ref, sl_ref, side_ref, pos_ref, *refs):
    stat_refs, p_refs, outs, coeff = refs[:pb], refs[pb : pb + WINDOW], refs[pb + WINDOW : -1], refs[-1]
    rows, width = p_refs[0].shape
    scale = 1.0 / math.sqrt(width)
    me = lax.axis_index("pb")
    lse_rows = log_totals([ref[0] for ref in stat_refs], pb)
    lse = jnp.concatenate([lse_rows[c : c + 1, :] for c in range(pb)], axis=1)
    w = side_ref[WINDOW + 1 : WINDOW + 2, :]
    row = lax.broadcasted_iota(jnp.int32, (rows, w.shape[1]), 0)
    for t in range(WINDOW):
        if t == 0:
            prob = jnp.exp(so_ref[...] - lse) - (row == pos_ref[...] - me * rows).astype(F32)
        elif t == LAST:
            prob = jnp.exp(sl_ref[...] - lse)
        else:
            prob = jnp.exp(sm_ref[(t - 1) * rows : t * rows, :] - lse)
        coeff[t * rows : (t + 1) * rows, :] = (w * prob * scale).astype(BF16)
    for r in range(pb):
        lanes = member_slice((me + r) % pb, rows)
        total = None
        for t in range(WINDOW):
            part = tn_dot(coeff[t * rows : (t + 1) * rows, lanes], p_refs[t][...])
            total = part if total is None else total + part
        outs[r][...] = total.astype(outs[r].dtype)

def add_blocks(pb, stats, scores, pieces, orders, keep, corrections, total):
    lse_ref, weight_ref = keep
    home = lax.axis_index("pa").astype(F32)
    rows, width = pieces[0].shape
    scale = 1.0 / math.sqrt(width)
    for t, mine in enumerate(stats):
        lse_ref[t] = log_totals(mine, pb)
        weight_ref[t] = mine[0][2 * pb : 3 * pb, :]
        hit = jnp.max(jnp.where(mine[0][3 * pb : 3 * pb + 1, :] == home, 1.0, 0.0), axis=1, keepdims=True) > 0.5
        for r in range(pb):
            n = t * pb + r
            member = pl.ds(orders[n], 1)
            prob = jnp.exp(scores(n) - lse_ref[t, member, :])
            if n in corrections:
                prob = prob - corrections[n]
            value = jnp.where(hit, weight_ref[t, member, :] * prob * scale, 0.0).astype(BF16)
            part = jnp.dot(value, pieces[n][...], preferred_element_type=F32)
            total = part if total is None else total + part
    return total

def near_kernel(pb, p_ref, pos_ref, *refs):
    stat_refs, q_refs = refs[:pb], refs[pb : -4]
    out_ref, s_ref, keep = refs[-4], refs[-3], refs[-2:]
    rows, width = p_ref.shape
    scale = 1.0 / math.sqrt(width)
    me = lax.axis_index("pb")
    row = lax.broadcasted_iota(jnp.int32, (rows, rows), 0)
    full_ref = q_refs[0]
    pieces = [full_ref.at[r * rows : (r + 1) * rows, :] for r in range(pb)] + list(q_refs[1:])
    orders = list(range(pb)) + [(me - r + pb) % pb for _ in range(3) for r in range(pb)]
    corrections = {
        r: (row == pos_ref[:, r * rows : (r + 1) * rows] - me * rows).astype(F32) for r in range(pb)
    }
    for n, piece in enumerate(pieces):
        s_ref[:, n * rows : (n + 1) * rows] = nt_dot(p_ref[...], piece[...]) * scale
    stats = [[ref[t] for ref in stat_refs] for t in range(4)]
    out_ref[...] = add_blocks(
        pb, stats, lambda n: s_ref[:, n * rows : (n + 1) * rows], pieces, orders, keep, corrections, None
    )

def cross_kernel(p_ref, *refs):
    q_refs, s_ref = refs[:-1], refs[-1]
    rows, width = p_ref.shape
    scale = 1.0 / math.sqrt(width)
    for n, q_ref in enumerate(q_refs):
        s_ref[:, n * rows : (n + 1) * rows] = nt_dot(p_ref[...], q_ref[...]) * scale

def far_kernel(pb, s_ref, near_ref, *refs):
    grad_refs, up, down = refs[:pb], refs[pb : 2 * pb], refs[2 * pb : 3 * pb]
    q_refs, (out_ref, query_ref), keep = refs[3 * pb : 6 * pb], refs[6 * pb : 6 * pb + 2], refs[6 * pb + 2 :]
    rows = out_ref.shape[0]
    home, me = lax.axis_index("pa"), lax.axis_index("pb")
    y_low, x_low = (home & 2) == 0, (home & 1) == 0
    stats = []
    for k, low in ((2, y_low), (1, x_low), (3, y_low)):
        stats.append([jnp.where(low, up[c][k], down[c][k]) for c in range(pb)])
    orders = [(me - r + pb) % pb for _ in range(3) for r in range(pb)]
    out_ref[...] = add_blocks(
        pb, stats, lambda n: s_ref[:, n * rows : (n + 1) * rows], q_refs, orders, keep, {}, near_ref[...]
    )
    grad = grad_refs[0][...]
    for ref in grad_refs[1:]:
        grad = grad + ref[...].astype(F32)
    query_ref[...] = grad

VMEM = pl.BlockSpec(memory_space=pltpu.VMEM)
SMEM = pl.BlockSpec(memory_space=pltpu.SMEM)

def call(kernel, outs, args, flops, smem=0, scratch=()):
    return pl.pallas_call(
        kernel,
        out_shape=outs,
        in_specs=[SMEM] * smem + [VMEM] * (len(args) - smem),
        out_specs=[VMEM] * len(outs),
        scratch_shapes=list(scratch),
        cost_estimate=pl.CostEstimate(flops=0, bytes_accessed=0, transcendentals=0),
        compiler_params=pltpu.CompilerParams(vmem_limit_bytes=24 * 1024 * 1024),
    )(*args)

def shape(dims, dtype):
    return jax.ShapeDtypeStruct(dims, dtype)

def after(value, *others):
    return lax.optimization_barrier((value, *others))[0]

def body(queries, passages, neighbor_lists, positives, weights):
    pb, count = lax.axis_size("pb"), lax.axis_size("pa")
    rows, width = passages.shape[1:]
    q_rows = rows * pb
    tables = relay_tables(count)
    flops = 2 * rows * q_rows * width

    def move(value, name):
        return lax.ppermute(value, "pa", tables[name])

    def from_member(value, r):
        return lax.ppermute(value, "pb", [(i, (i + r) % pb) for i in range(pb)])

    def others(value):
        return [from_member(value, r) for r in range(1, pb)]

    yp, xp = move(passages[0], "y"), move(passages[0], "x")
    yq, xq = move(queries[0], "y"), move(queries[0], "x")
    own_score, own_ml, full_q, own_p, side, where = call(
        lambda *refs: own_kernel(count, pb, *refs),
        [
            shape((rows, q_rows), F32),
            shape((8, q_rows), F32),
            shape((q_rows, width), BF16),
            shape((rows, width), BF16),
            shape((16, q_rows), F32),
            shape((1, q_rows), jnp.int32),
        ],
        [neighbor_lists, weights, positives, passages[0], queries[0], *others(queries[0])],
        flops,
        smem=1,
    )
    xqs, yqs = [xq, *others(xq)], [yq, *others(yq)]
    zap, zbp, dp = move(yp, "za"), move(xp, "zb"), move(xp, "y")
    xzp = move(after(zap, xq, yq, own_ml), "x")
    middle, middle_ml = call(
        middle_kernel,
        [shape(((LAST - 1) * rows, q_rows), F32), shape((8, q_rows), F32)],
        [full_q, side, after(own_ml, *xqs, *yqs), xp, yp, dp, zap, zbp],
        (LAST - 1) * flops,
    )
    zaq, zbq = move(after(yq, zbp), "za"), move(after(xq, zbp), "zb")
    stat_rows = -(-(3 * pb + 1) // 8) * 8
    last, stat = call(
        lambda *refs: last_kernel(pb, *refs),
        [shape((rows, q_rows), F32), shape((stat_rows, rows), F32)],
        [full_q, side, middle_ml, xzp],
        flops,
    )
    stat_x, stat_y, stat_d = move(stat, "x"), move(stat, "y"), move(stat, "d")
    four = jnp.stack([stat, stat_x, stat_y, stat_d])
    dq = move(after(xq, four), "y")
    xzq = move(after(zaq, four), "x")
    up, down = move(four, "up"), move(four, "down")
    fours = [four, *others(four)]
    parts = call(
        lambda *refs: query_kernel(pb, *refs),
        [shape((rows, width), F32)] + [shape((rows, width), BF16)] * (pb - 1),
        [own_score, middle, last, side, where, *fours, own_p, xp, yp, dp, zap, zbp, xzp],
        WINDOW * flops,
        scratch=[pltpu.VMEM((WINDOW * rows, q_rows), BF16)],
    )
    arrived = [from_member(parts[r], r) for r in range(1, pb)]

    def keep(blocks):
        return [pltpu.VMEM((blocks, pb, rows), F32)] * 2

    (near,) = call(
        lambda *refs: near_kernel(pb, *refs),
        [shape((rows, width), F32)],
        [own_p, where, *fours, full_q, *xqs, *yqs, dq, *others(dq)],
        8 * flops,
        scratch=[pltpu.VMEM((rows, 4 * q_rows), F32), *keep(4)],
    )
    far_q = [zaq, *others(after(zaq, dq)), zbq, *others(after(zbq, dq)), xzq, *others(xzq)]
    (cross,) = call(cross_kernel, [shape((rows, 3 * q_rows), F32)], [own_p, *far_q], 3 * flops)
    passage_grad, query_grad = call(
        lambda *refs: far_kernel(pb, *refs),
        [shape((rows, width), F32)] * 2,
        [cross, near, parts[0], *arrived, up, *others(up), down, *others(down), *far_q],
        3 * flops,
        scratch=keep(3),
    )
    return (query_grad[None], passage_grad[None])

def solution(mesh):
    return jax.shard_map(
        body,
        mesh=mesh,
        in_specs=(
            P("pa", "pb", None),
            P("pa", "pb", None),
            P("pa", None),
            P("pa", None),
            P("pa", None),
        ),
        out_specs=(P("pa", "pb", None), P("pa", "pb", None)),
        check_vma=False,
    )
```

time: 54 us -> 51.4 us (0.952)
  starting transfers between devices: 25 us -> 23.4 us
  waiting for transfers between devices: 19 us -> 17.9 us
    ppermute x17, starting transfers between devices: 22.7 us -> 21.3 us  [move(): return lax.ppermute(value, 'pa', tables[name])]
    ppermute x17, waiting for transfers between devices: 18.9 us -> 17.9 us  [move(): return lax.ppermute(value, 'pa', tables[name])]
    ppermute x12 -> x11, starting transfers between devices: 2.35 us -> 2.11 us  [from_member(): return lax.ppermute(value, 'pb', [(i, (i + r) % pb) for i in range(pb)])]
  transfers between devices with their start and end apart: 29 -> 28, of which waited for: 9 -> 11; matrix products, arithmetic and copies ran while one was open for 0% -> 0% of each run, Pallas kernels for 9% -> 11%
where the time goes in v3:
time: 51.4 us; the launch traced here: 51.1 us
  starting transfers between devices  23.4 us (46%)
  waiting for transfers between devices  17.9 us (35%)
  Pallas kernels  7.13 us (14%)
  local copies, waits for them, and re-layouts  1.91 us (4%)
  between operations  0.78 us (2%)
    ppermute x17, starting transfers between devices, move(): return lax.ppermute(value, 'pa', tables[name])  21.3 us
    ppermute x17, waiting for transfers between devices, move(): return lax.ppermute(value, 'pa', tables[name])  17.9 us
    pallas_call x7, Pallas kernels, call(): pl.pallas_call(kernel, out_shape=outs, in_specs=[SMEM] * smem + [VMEM] *...  7.13 us
    ppermute x11, starting transfers between devices, from_member(): return lax.ppermute(value, 'pb', [(i, (i + r) % pb) for i in range(pb)])  2.11 us
    unnamed x10, local copies, waits for them, and re-layouts  1.91 us
  transfers between devices with their start and end apart: 28, of which 11 were waited for; matrix products, arithmetic and copies ran while one was open for 0% of the time, Pallas kernels for 11%

profile of v3, /device:TPU:0, one launch (start us, length us, event | category | flops | bytes accessed | tf_op | source)
XLA Modules:
  0.0 51.1 jit_solution(14624009094704803815)
XLA Ops:
  0.7 3.0 %collective-permute-start.8 = (bf16[128,1024]{1,0:T(8,128)(2,1)}, bf16[128,1024]{1,0:T(8,128)(2,1)S(1)}, u32[]{:S(2)}, u32[]{:S(2)}) collective-permute-start(bf16[128,1024]{1,0:T(8,128)(2,1)} %bitcast.8), channel_id=1, source_target_pairs={{0,2},{1,3},{2,0},{3,1},{4,6},{5,7},{6,4},{7,5},{8,10},{9,11},{10,... | collective-permute-start | bytes 786440 | tf_op jit(solution)/shard_map/ppermute | solution.py:246
  3.7 1.5 %collective-permute-start.2 = (bf16[128,1024]{1,0:T(8,128)(2,1)}, bf16[128,1024]{1,0:T(8,128)(2,1)S(1)}, u32[]{:S(2)}, u32[]{:S(2)}) collective-permute-start(bf16[128,1024]{1,0:T(8,128)(2,1)} %bitcast.9), channel_id=1, source_target_pairs={{0,1},{1,0},{2,3},{3,2},{4,5},{5,4},{6,7},{7,6},{8,9},{9,8},{10,11... | collective-permute-start | bytes 786440 | tf_op jit(solution)/shard_map/ppermute | solution.py:246
  5.2 0.5 %collective-permute-start.5 = (bf16[128,1024]{1,0:T(8,128)(2,1)}, bf16[128,1024]{1,0:T(8,128)(2,1)S(1)}, u32[]{:S(2)}, u32[]{:S(2)}) collective-permute-start(bf16[128,1024]{1,0:T(8,128)(2,1)} %bitcast.12), channel_id=1, source_target_pairs={{0,1},{1,0},{2,3},{3,2},{4,5},{5,4},{6,7},{7,6},{8,9},{9,8},{10,11... | collective-permute-start | bytes 786440 | tf_op jit(solution)/shard_map/ppermute | solution.py:246
  5.7 0.1 collective-permute-start.1
  5.8 5.2 %collective-permute-done.8.refs_1_.refs_9_ = bf16[128,1024]{1,0:T(8,128)(2,1)S(1)} collective-permute-done((bf16[128,1024]{1,0:T(8,128)(2,1)}, bf16[128,1024]{1,0:T(8,128)(2,1)S(1)}, u32[]{:S(2)}, u32[]{:S(2)}) %collective-permute-start.8) | collective-permute-done | bytes 262176 | tf_op jit(solution)/shard_map/ppermute | solution.py:246
  11.0 2.1 %collective-permute-start.10 = (bf16[128,1024]{1,0:T(8,128)(2,1)S(1)}, bf16[128,1024]{1,0:T(8,128)(2,1)S(1)}, u32[]{:S(2)}, u32[]{:S(2)}) collective-permute-start(bf16[128,1024]{1,0:T(8,128)(2,1)S(1)} %collective-permute-done.8.refs_1_.refs_9_), channel_id=1, source_target_pairs={{0,4},{1,5},{2,14},{3,15},{4,8},{5,9},{6,2},{7,3},{8,12},{9,13},{1... | collective-permute-start | bytes 786440 | tf_op jit(solution)/shard_map/ppermute | solution.py:246
  13.2 1.6 %collective-permute-start.3 = (bf16[128,1024]{1,0:T(8,128)(2,1)S(1)}, bf16[128,1024]{1,0:T(8,128)(2,1)S(1)}, u32[]{:S(2)}, u32[]{:S(2)}) collective-permute-start(bf16[128,1024]{1,0:T(8,128)(2,1)S(1)} %collective-permute-done.2.refs_0_.refs_8_), channel_id=1, source_target_pairs={{0,4},{1,13},{2,6},{3,15},{4,8},{5,1},{6,10},{7,3},{8,12},{9,5},{1... | collective-permute-start | bytes 786440 | tf_op jit(solution)/shard_map/ppermute | solution.py:246
  14.7 0.0 collective-permute-done.refs_5_
  14.7 2.0 %collective-permute-start.9 = (bf16[128,1024]{1,0:T(8,128)(2,1)S(1)}, bf16[128,1024]{1,0:T(8,128)(2,1)S(1)}, u32[]{:S(2)}, u32[]{:S(2)}) collective-permute-start(bf16[128,1024]{1,0:T(8,128)(2,1)S(1)} %collective-permute-done.2.refs_0_.refs_8_), channel_id=1, source_target_pairs={{0,2},{1,3},{2,0},{3,1},{4,6},{5,7},{6,4},{7,5},{8,10},{9,11},{10,... | collective-permute-start | bytes 786440 | tf_op jit(solution)/shard_map/ppermute | solution.py:246
  16.8 0.5 %collective-permute-done.5.refs_5_ = bf16[128,1024]{1,0:T(8,128)(2,1)S(1)} collective-permute-done((bf16[128,1024]{1,0:T(8,128)(2,1)}, bf16[128,1024]{1,0:T(8,128)(2,1)S(1)}, u32[]{:S(2)}, u32[]{:S(2)}) %collective-permute-start.5) | collective-permute-done | bytes 262176 | tf_op jit(solution)/shard_map/ppermute | solution.py:246
  17.3 0.0 collective-permute-start.6
  17.3 0.0 collective-permute-done.1.refs_7_
  17.3 0.5 collective-permute-start.7
  17.8 0.9 %copy-done = bf16[1,128,1024]{2,1,0:T(8,128)(2,1)S(1)} copy-done((bf16[1,128,1024]{2,1,0:T(8,128)(2,1)S(1)}, bf16[1,128,1024]{2,1,0:T(8,128)(2,1)}, u32[]{:S(2)}) %copy-start) | copy-done | bytes 262168
  18.8 0.9 %copy-done.1 = bf16[1,128,1024]{2,1,0:T(8,128)(2,1)S(1)} copy-done((bf16[1,128,1024]{2,1,0:T(8,128)(2,1)S(1)}, bf16[1,128,1024]{2,1,0:T(8,128)(2,1)}, u32[]{:S(2)}) %copy-start.1) | copy-done | bytes 262168
  19.7 1.0 %shard_map.68 = (f32[128,256]{1,0:T(8,128)S(1)}, f32[8,256]{1,0:T(8,128)S(1)}, bf16[256,1024]{1,0:T(8,128)(2,1)S(1)}, bf16[128,1024]{1,0:T(8,128)(2,1)S(1)}, f32...) custom-call(s32[1,7]{1,0:T(1,128)S(1)} %copy-done.4, f32[1,256]{1,0:T(1,128)S(1)} %copy-done.2, s32[1,256]{1,0:T(1,128)S(1)} %copy-done.3, ...), custom_call_target="tpu_custom_call" | custom-call | tf_op jit(solution)/shard_map/pallas_call | solution.py:222
  20.7 1.6 %collective-permute-done.10.refs_3_.refs_11_ = bf16[128,1024]{1,0:T(8,128)(2,1)S(1)} collective-permute-done((bf16[128,1024]{1,0:T(8,128)(2,1)S(1)}, bf16[128,1024]{1,0:T(8,128)(2,1)S(1)}, u32[]{:S(2)}, u32[]{:S(2)}) %collective-permute-start.10) | collective-permute-done | bytes 262176 | tf_op jit(solution)/shard_map/ppermute | solution.py:246
  22.3 1.5 %collective-permute-start.11 = (bf16[128,1024]{1,0:T(8,128)(2,1)S(1)}, bf16[128,1024]{1,0:T(8,128)(2,1)S(1)}, u32[]{:S(2)}, u32[]{:S(2)}) collective-permute-start(bf16[128,1024]{1,0:T(8,128)(2,1)S(1)} %collective-permute-done.10.refs_3_.refs_11_), channel_id=1, source_target_pairs={{0,1},{1,0},{2,3},{3,2},{4,5},{5,4},{6,7},{7,6},{8,9},{9,8},{10,11... | collective-permute-start | bytes 786440 | tf_op jit(solution)/shard_map/ppermute | solution.py:246
  23.8 1.3 %collective-permute-done.3.refs_4_.refs_12_ = bf16[128,1024]{1,0:T(8,128)(2,1)S(1)} collective-permute-done((bf16[128,1024]{1,0:T(8,128)(2,1)S(1)}, bf16[128,1024]{1,0:T(8,128)(2,1)S(1)}, u32[]{:S(2)}, u32[]{:S(2)}) %collective-permute-start.3) | collective-permute-done | bytes 262176 | tf_op jit(solution)/shard_map/ppermute | solution.py:246
  25.1 0.0 collective-permute-start.4
  25.1 0.0 collective-permute-done.6.refs_6_
  25.1 0.0 collective-permute-done.7.refs_8_
  25.1 0.0 collective-permute-done.9.refs_2_.refs_10_
  25.1 1.1 %shard_map.69 = (f32[640,256]{1,0:T(8,128)S(1)}, f32[8,256]{1,0:T(8,128)S(1)}) custom-call(bf16[256,1024]{1,0:T(8,128)(2,1)S(1)} %get-tuple-element.26.full_ref.refs_0_.refs_4_, f32[16,256]{1,0:T(8,128)S(1)} %get-tuple-element.27.side_ref.refs_1_.refs_3_, f32[8,256]{1,0:T(8,128)S(1)} %get-tuple-element.29.before_ref, ...), custom_call_target="tpu_custom_call" | custom-call | tf_op jit(solution)/shard_map/pallas_call | solution.py:222
  26.3 2.7 %collective-permute-done.11.refs_3_.refs_13_ = bf16[128,1024]{1,0:T(8,128)(2,1)S(1)} collective-permute-done((bf16[128,1024]{1,0:T(8,128)(2,1)S(1)}, bf16[128,1024]{1,0:T(8,128)(2,1)S(1)}, u32[]{:S(2)}, u32[]{:S(2)}) %collective-permute-start.11) | collective-permute-done | bytes 262176 | tf_op jit(solution)/shard_map/ppermute | solution.py:246
  29.0 0.4 shard_map.70
  29.3 1.6 %collective-permute-start.12 = (f32[8,128]{1,0:T(8,128)S(1)}, f32[8,128]{1,0:T(8,128)S(1)}, u32[]{:S(2)}, u32[]{:S(2)}) collective-permute-start(f32[8,128]{1,0:T(8,128)S(1)} %get-tuple-element.32), channel_id=1, source_target_pairs={{0,1},{1,0},{2,3},{3,2},{4,5},{5,4},{6,7},{7,6},{8,9},{9,8},{10,11... | collective-permute-start | bytes 12296 | tf_op jit(solution)/shard_map/ppermute | solution.py:246
  30.9 2.3 %collective-permute-start.13 = (f32[8,128]{1,0:T(8,128)S(1)}, f32[8,128]{1,0:T(8,128)S(1)}, u32[]{:S(2)}, u32[]{:S(2)}) collective-permute-start(f32[8,128]{1,0:T(8,128)S(1)} %get-tuple-element.32), channel_id=1, source_target_pairs={{0,2},{1,3},{2,0},{3,1},{4,6},{5,7},{6,4},{7,5},{8,10},{9,11},{10,... | collective-permute-start | bytes 12296 | tf_op jit(solution)/shard_map/ppermute | solution.py:246
  33.2 1.3 %collective-permute-start.17 = (bf16[128,1024]{1,0:T(8,128)(2,1)S(1)}, bf16[128,1024]{1,0:T(8,128)(2,1)S(1)}, u32[]{:S(2)}, u32[]{:S(2)}) collective-permute-start(bf16[128,1024]{1,0:T(8,128)(2,1)S(1)} %collective-permute-done.5.refs_5_), channel_id=1, source_target_pairs={{0,4},{1,13},{2,6},{3,15},{4,8},{5,1},{6,10},{7,3},{8,12},{9,5},{1... | collective-permute-start | bytes 786440 | tf_op jit(solution)/shard_map/ppermute | solution.py:246
  34.5 0.3 collective-permute-done.13
  34.8 3.0 %collective-permute-done.14 = f32[8,128]{1,0:T(8,128)S(1)} collective-permute-done((f32[8,128]{1,0:T(8,128)S(1)}, f32[8,128]{1,0:T(8,128)S(1)}, u32[]{:S(2)}, u32[]{:S(2)}) %collective-permute-start.14) | collective-permute-done | bytes 4128 | tf_op jit(solution)/shard_map/ppermute | solution.py:246
  37.8 0.1 collective-permute-start.15
  37.8 1.7 %collective-permute-start.19 = (bf16[128,1024]{1,0:T(8,128)(2,1)S(1)}, bf16[128,1024]{1,0:T(8,128)(2,1)S(1)}, u32[]{:S(2)}, u32[]{:S(2)}) collective-permute-start(bf16[128,1024]{1,0:T(8,128)(2,1)S(1)} %collective-permute-done.4.refs_0_.refs_8_), channel_id=1, source_target_pairs={{0,1},{1,0},{2,3},{3,2},{4,5},{5,4},{6,7},{7,6},{8,9},{9,8},{10,11... | collective-permute-start | bytes 786440 | tf_op jit(solution)/shard_map/ppermute | solution.py:246
  39.5 0.1 collective-permute-start.24
  39.5 1.8 %collective-permute-done.17.refs_2_.refs_10_ = bf16[128,1024]{1,0:T(8,128)(2,1)S(1)} collective-permute-done((bf16[128,1024]{1,0:T(8,128)(2,1)S(1)}, bf16[128,1024]{1,0:T(8,128)(2,1)S(1)}, u32[]{:S(2)}, u32[]{:S(2)}) %collective-permute-start.17) | collective-permute-done | bytes 262176 | tf_op jit(solution)/shard_map/ppermute | solution.py:246
  41.4 1.9 %collective-permute-start.26 = (f32[4,8,128]{2,1,0:T(8,128)S(1)}, f32[4,8,128]{2,1,0:T(8,128)S(1)}, u32[]{:S(2)}, u32[]{:S(2)}) collective-permute-start(f32[4,8,128]{2,1,0:T(8,128)S(1)} %pad_maximum_fusion.refs_2_.refs_5_), channel_id=1, source_target_pairs={{0,12},{1,13},{2,14},{3,15},{4,0},{5,1},{6,2},{7,3},{8,4},{9,5},{1... | collective-permute-start | bytes 49160 | tf_op jit(solution)/shard_map/ppermute | solution.py:246
  43.3 0.8 %collective-permute-done.15.refs_9_ = bf16[128,1024]{1,0:T(8,128)(2,1)S(1)} collective-permute-done((bf16[128,1024]{1,0:T(8,128)(2,1)S(1)}, bf16[128,1024]{1,0:T(8,128)(2,1)S(1)}, u32[]{:S(2)}, u32[]{:S(2)}) %collective-permute-start.15) | collective-permute-done | bytes 262176 | tf_op jit(solution)/shard_map/ppermute | solution.py:246
  44.1 0.1 collective-permute-done.19.refs_4_.refs_12_
  44.2 0.4 collective-permute-start.20
  44.6 0.1 collective-permute-start.18
  44.7 0.5 collective-permute-done.24.refs_4_
  45.2 1.2 %shard_map.73 = (f32[128,1024]{1,0:T(8,128)S(1)}, bf16[128,1024]{1,0:T(8,128)(2,1)S(1)}) custom-call(f32[128,256]{1,0:T(8,128)S(1)} %get-tuple-element.39.refs_0_, f32[640,256]{1,0:T(8,128)S(1)} %get-tuple-element.40.refs_1_, f32[128,256]{1,0:T(8,128)S(1)} %get-tuple-element.41.refs_2_, f32[16,256]{1,0:T(8,128)S(1)} %get-tuple-element.27.side_ref.refs_1_.refs_3_, ...), custom_call_target="tpu_custom_call" | custom-call | tf_op jit(solution)/shard_map/pallas_call | solution.py:222
  46.5 0.6 %collective-permute-start.23 = (bf16[128,1024]{1,0:T(8,128)(2,1)S(1)}, bf16[128,1024]{1,0:T(8,128)(2,1)S(1)}, u32[]{:S(2)}, u32[]{:S(2)}) collective-permute-start(bf16[128,1024]{1,0:T(8,128)(2,1)S(1)} %get-tuple-element.43), channel_id=1, source_target_pairs={{0,16},{16,0},{1,17},{17,1},{2,18},{18,2},{3,19},{19,3},{4,20},{20... | collective-permute-start | bytes 786440 | tf_op jit(solution)/shard_map/ppermute | solution.py:249
  47.0 0.1 collective-permute-start.25
  47.1 0.4 collective-permute-start.27
  47.5 1.3 %shard_map.72.refs_1_ = f32[128,1024]{1,0:T(8,128)S(1)} custom-call(bf16[128,1024]{1,0:T(8,128)(2,1)S(1)} %get-tuple-element.24.p_ref.refs_0_.refs_7_, s32[1,256]{1,0:T(1,128)S(1)} %get-tuple-element.38.refs_1_.refs_4_, f32[4,8,128]{2,1,0:T(8,128)S(1)} %pad_maximum_fusion.refs_2_.refs_5_, f32[4,8,128]{2,1,0:T(8,128)S(1)} %collective-permute-done.21.refs_3_.refs_6_, ...), custom_call_target="tpu_custom_call" | custom-call | tf_op jit(solution)/shard_map/pallas_call | solution.py:222
  48.8 0.6 %shard_map.71.refs_0_ = f32[128,768]{1,0:T(8,128)S(1)} custom-call(bf16[128,1024]{1,0:T(8,128)(2,1)S(1)} %get-tuple-element.24.p_ref.refs_0_.refs_7_, bf16[128,1024]{1,0:T(8,128)(2,1)S(1)} %collective-permute-done.4.refs_0_.refs_8_, bf16[128,1024]{1,0:T(8,128)(2,1)S(1)} %collective-permute-done.16.refs_1_.refs_9_, ...), custom_call_target="tpu_custom_call" | custom-call | tf_op jit(solution)/shard_map/pallas_call | solution.py:222
  49.4 1.6 %shard_map.74 = (f32[128,1024]{1,0:T(8,128)}, f32[128,1024]{1,0:T(8,128)}) custom-call(f32[128,768]{1,0:T(8,128)S(1)} %shard_map.71.refs_0_, f32[128,1024]{1,0:T(8,128)S(1)} %shard_map.72.refs_1_, f32[128,1024]{1,0:T(8,128)S(1)} %get-tuple-element.42.refs_2_, bf16[128,1024]{1,0:T(8,128)(2,1)S(1)} %collective-permute-done.23.refs_3_, ...), custom_call_target="tpu_custom_call" | custom-call | tf_op jit(solution)/shard_map/pallas_call | solution.py:222
  (26 shorter events, 0.1 us)
Async XLA Ops:
  0.6 17.2 %copy-start.3 = (s32[1,256]{1,0:T(1,128)S(1)}, s32[1,256]{1,0:T(1,128)}, u32[]{:S(2)}) copy-start(s32[1,256]{1,0:T(1,128)} %refs_2_.1) | copy-start | bytes 3076
  0.6 17.2 %copy-start.2 = (f32[1,256]{1,0:T(1,128)S(1)}, f32[1,256]{1,0:T(1,128)}, u32[]{:S(2)}) copy-start(f32[1,256]{1,0:T(1,128)} %refs_1_.1) | copy-start | bytes 3076
  0.7 17.2 %copy-start.4 = (s32[1,7]{1,0:T(1,128)S(1)}, s32[1,7]{1,0:T(1,128)}, u32[]{:S(2)}) copy-start(s32[1,7]{1,0:T(1,128)} %refs_0_.1) | copy-start | bytes 88
  0.7 10.4 %collective-permute-start.8 = (bf16[128,1024]{1,0:T(8,128)(2,1)}, bf16[128,1024]{1,0:T(8,128)(2,1)S(1)}, u32[]{:S(2)}, u32[]{:S(2)}) collective-permute-start(bf16[128,1024]{1,0:T(8,128)(2,1)} %bitcast.8), channel_id=1, source_target_pairs={{0,2},{1,3},{2,0},{3,1},{4,6},{5,7},{6,4},{7,5},{8,10},{9,11},{10,... | collective-permute-start | bytes 786440 | tf_op jit(solution)/shard_map/ppermute | solution.py:246
  3.7 9.5 %collective-permute-start.2 = (bf16[128,1024]{1,0:T(8,128)(2,1)}, bf16[128,1024]{1,0:T(8,128)(2,1)S(1)}, u32[]{:S(2)}, u32[]{:S(2)}) collective-permute-start(bf16[128,1024]{1,0:T(8,128)(2,1)} %bitcast.9), channel_id=1, source_target_pairs={{0,1},{1,0},{2,3},{3,2},{4,5},{5,4},{6,7},{7,6},{8,9},{9,8},{10,11... | collective-permute-start | bytes 786440 | tf_op jit(solution)/shard_map/ppermute | solution.py:246
  5.2 9.6 %collective-permute-start = (bf16[128,1024]{1,0:T(8,128)(2,1)}, bf16[128,1024]{1,0:T(8,128)(2,1)S(1)}, u32[]{:S(2)}, u32[]{:S(2)}) collective-permute-start(bf16[128,1024]{1,0:T(8,128)(2,1)} %bitcast.11), channel_id=1, source_target_pairs={{0,16},{16,0},{1,17},{17,1},{2,18},{18,2},{3,19},{19,3},{4,20},{20... | collective-permute-start | bytes 786440 | tf_op jit(solution)/shard_map/ppermute | solution.py:249
  5.2 12.1 %collective-permute-start.5 = (bf16[128,1024]{1,0:T(8,128)(2,1)}, bf16[128,1024]{1,0:T(8,128)(2,1)S(1)}, u32[]{:S(2)}, u32[]{:S(2)}) collective-permute-start(bf16[128,1024]{1,0:T(8,128)(2,1)} %bitcast.12), channel_id=1, source_target_pairs={{0,1},{1,0},{2,3},{3,2},{4,5},{5,4},{6,7},{7,6},{8,9},{9,8},{10,11... | collective-permute-start | bytes 786440 | tf_op jit(solution)/shard_map/ppermute | solution.py:246
  5.7 11.6 %collective-permute-start.1 = (bf16[128,1024]{1,0:T(8,128)(2,1)}, bf16[128,1024]{1,0:T(8,128)(2,1)S(1)}, u32[]{:S(2)}, u32[]{:S(2)}) collective-permute-start(bf16[128,1024]{1,0:T(8,128)(2,1)} %bitcast.13), channel_id=1, source_target_pairs={{0,2},{1,3},{2,0},{3,1},{4,6},{5,7},{6,4},{7,5},{8,10},{9,11},{10,... | collective-permute-start | bytes 786440 | tf_op jit(solution)/shard_map/ppermute | solution.py:246
  11.0 11.3 %collective-permute-start.10 = (bf16[128,1024]{1,0:T(8,128)(2,1)S(1)}, bf16[128,1024]{1,0:T(8,128)(2,1)S(1)}, u32[]{:S(2)}, u32[]{:S(2)}) collective-permute-start(bf16[128,1024]{1,0:T(8,128)(2,1)S(1)} %collective-permute-done.8.refs_1_.refs_9_), channel_id=1, source_target_pairs={{0,4},{1,5},{2,14},{3,15},{4,8},{5,9},{6,2},{7,3},{8,12},{9,13},{1... | collective-permute-start | bytes 786440 | tf_op jit(solution)/shard_map/ppermute | solution.py:246
  13.2 12.0 %collective-permute-start.3 = (bf16[128,1024]{1,0:T(8,128)(2,1)S(1)}, bf16[128,1024]{1,0:T(8,128)(2,1)S(1)}, u32[]{:S(2)}, u32[]{:S(2)}) collective-permute-start(bf16[128,1024]{1,0:T(8,128)(2,1)S(1)} %collective-permute-done.2.refs_0_.refs_8_), channel_id=1, source_target_pairs={{0,4},{1,13},{2,6},{3,15},{4,8},{5,1},{6,10},{7,3},{8,12},{9,5},{1... | collective-permute-start | bytes 786440 | tf_op jit(solution)/shard_map/ppermute | solution.py:246
  14.7 10.4 %collective-permute-start.9 = (bf16[128,1024]{1,0:T(8,128)(2,1)S(1)}, bf16[128,1024]{1,0:T(8,128)(2,1)S(1)}, u32[]{:S(2)}, u32[]{:S(2)}) collective-permute-start(bf16[128,1024]{1,0:T(8,128)(2,1)S(1)} %collective-permute-done.2.refs_0_.refs_8_), channel_id=1, source_target_pairs={{0,2},{1,3},{2,0},{3,1},{4,6},{5,7},{6,4},{7,5},{8,10},{9,11},{10,... | collective-permute-start | bytes 786440 | tf_op jit(solution)/shard_map/ppermute | solution.py:246
  17.3 7.8 %collective-permute-start.6 = (bf16[128,1024]{1,0:T(8,128)(2,1)S(1)}, bf16[128,1024]{1,0:T(8,128)(2,1)S(1)}, u32[]{:S(2)}, u32[]{:S(2)}) collective-permute-start(bf16[128,1024]{1,0:T(8,128)(2,1)S(1)} %collective-permute-done.5.refs_5_), channel_id=1, source_target_pairs={{0,16},{16,0},{1,17},{17,1},{2,18},{18,2},{3,19},{19,3},{4,20},{20... | collective-permute-start | bytes 786440 | tf_op jit(solution)/shard_map/ppermute | solution.py:249
  17.3 7.8 %collective-permute-start.7 = (bf16[128,1024]{1,0:T(8,128)(2,1)S(1)}, bf16[128,1024]{1,0:T(8,128)(2,1)S(1)}, u32[]{:S(2)}, u32[]{:S(2)}) collective-permute-start(bf16[128,1024]{1,0:T(8,128)(2,1)S(1)} %collective-permute-done.1.refs_7_), channel_id=1, source_target_pairs={{0,16},{16,0},{1,17},{17,1},{2,18},{18,2},{3,19},{19,3},{4,20},{20... | collective-permute-start | bytes 786440 | tf_op jit(solution)/shard_map/ppermute | solution.py:249
  17.8 1.0 %copy-start = (bf16[1,128,1024]{2,1,0:T(8,128)(2,1)S(1)}, bf16[1,128,1024]{2,1,0:T(8,128)(2,1)}, u32[]{:S(2)}) copy-start(bf16[1,128,1024]{2,1,0:T(8,128)(2,1)} %param.6) | copy-start | bytes 786436
  18.8 0.9 %copy-start.1 = (bf16[1,128,1024]{2,1,0:T(8,128)(2,1)S(1)}, bf16[1,128,1024]{2,1,0:T(8,128)(2,1)}, u32[]{:S(2)}) copy-start(bf16[1,128,1024]{2,1,0:T(8,128)(2,1)} %param.5) | copy-start | bytes 786436
  22.3 6.7 %collective-permute-start.11 = (bf16[128,1024]{1,0:T(8,128)(2,1)S(1)}, bf16[128,1024]{1,0:T(8,128)(2,1)S(1)}, u32[]{:S(2)}, u32[]{:S(2)}) collective-permute-start(bf16[128,1024]{1,0:T(8,128)(2,1)S(1)} %collective-permute-done.10.refs_3_.refs_11_), channel_id=1, source_target_pairs={{0,1},{1,0},{2,3},{3,2},{4,5},{5,4},{6,7},{7,6},{8,9},{9,8},{10,11... | collective-permute-start | bytes 786440 | tf_op jit(solution)/shard_map/ppermute | solution.py:246
  25.1 12.7 %collective-permute-start.4 = (bf16[128,1024]{1,0:T(8,128)(2,1)S(1)}, bf16[128,1024]{1,0:T(8,128)(2,1)S(1)}, u32[]{:S(2)}, u32[]{:S(2)}) collective-permute-start(bf16[128,1024]{1,0:T(8,128)(2,1)S(1)} %collective-permute-done.1.refs_7_), channel_id=1, source_target_pairs={{0,4},{1,5},{2,14},{3,15},{4,8},{5,9},{6,2},{7,3},{8,12},{9,13},{1... | collective-permute-start | bytes 786440 | tf_op jit(solution)/shard_map/ppermute | solution.py:246
  29.3 5.1 %collective-permute-start.12 = (f32[8,128]{1,0:T(8,128)S(1)}, f32[8,128]{1,0:T(8,128)S(1)}, u32[]{:S(2)}, u32[]{:S(2)}) collective-permute-start(f32[8,128]{1,0:T(8,128)S(1)} %get-tuple-element.32), channel_id=1, source_target_pairs={{0,1},{1,0},{2,3},{3,2},{4,5},{5,4},{6,7},{7,6},{8,9},{9,8},{10,11... | collective-permute-start | bytes 12296 | tf_op jit(solution)/shard_map/ppermute | solution.py:246
  30.9 3.9 %collective-permute-start.13 = (f32[8,128]{1,0:T(8,128)S(1)}, f32[8,128]{1,0:T(8,128)S(1)}, u32[]{:S(2)}, u32[]{:S(2)}) collective-permute-start(f32[8,128]{1,0:T(8,128)S(1)} %get-tuple-element.32), channel_id=1, source_target_pairs={{0,2},{1,3},{2,0},{3,1},{4,6},{5,7},{6,4},{7,5},{8,10},{9,11},{10,... | collective-permute-start | bytes 12296 | tf_op jit(solution)/shard_map/ppermute | solution.py:246
  33.2 4.6 %collective-permute-start.14 = (f32[8,128]{1,0:T(8,128)S(1)}, f32[8,128]{1,0:T(8,128)S(1)}, u32[]{:S(2)}, u32[]{:S(2)}) collective-permute-start(f32[8,128]{1,0:T(8,128)S(1)} %get-tuple-element.32), channel_id=1, source_target_pairs={{0,3},{1,2},{2,1},{3,0},{4,7},{5,6},{6,5},{7,4},{8,11},{9,10},{10,... | collective-permute-start | bytes 12296 | tf_op jit(solution)/shard_map/ppermute | solution.py:246
  33.2 8.2 %collective-permute-start.17 = (bf16[128,1024]{1,0:T(8,128)(2,1)S(1)}, bf16[128,1024]{1,0:T(8,128)(2,1)S(1)}, u32[]{:S(2)}, u32[]{:S(2)}) collective-permute-start(bf16[128,1024]{1,0:T(8,128)(2,1)S(1)} %collective-permute-done.5.refs_5_), channel_id=1, source_target_pairs={{0,4},{1,13},{2,6},{3,15},{4,8},{5,1},{6,10},{7,3},{8,12},{9,5},{1... | collective-permute-start | bytes 786440 | tf_op jit(solution)/shard_map/ppermute | solution.py:246
  37.8 6.4 %collective-permute-start.15 = (bf16[128,1024]{1,0:T(8,128)(2,1)S(1)}, bf16[128,1024]{1,0:T(8,128)(2,1)S(1)}, u32[]{:S(2)}, u32[]{:S(2)}) collective-permute-start(bf16[128,1024]{1,0:T(8,128)(2,1)S(1)} %collective-permute-done.5.refs_5_), channel_id=1, source_target_pairs={{0,2},{1,3},{2,0},{3,1},{4,6},{5,7},{6,4},{7,5},{8,10},{9,11},{10,... | collective-permute-start | bytes 786440 | tf_op jit(solution)/shard_map/ppermute | solution.py:246
  37.8 6.4 %collective-permute-start.19 = (bf16[128,1024]{1,0:T(8,128)(2,1)S(1)}, bf16[128,1024]{1,0:T(8,128)(2,1)S(1)}, u32[]{:S(2)}, u32[]{:S(2)}) collective-permute-start(bf16[128,1024]{1,0:T(8,128)(2,1)S(1)} %collective-permute-done.4.refs_0_.refs_8_), channel_id=1, source_target_pairs={{0,1},{1,0},{2,3},{3,2},{4,5},{5,4},{6,7},{7,6},{8,9},{9,8},{10,11... | collective-permute-start | bytes 786440 | tf_op jit(solution)/shard_map/ppermute | solution.py:246
  39.5 5.2 %collective-permute-start.21 = (f32[4,8,128]{2,1,0:T(8,128)S(1)}, f32[4,8,128]{2,1,0:T(8,128)S(1)}, u32[]{:S(2)}, u32[]{:S(2)}) collective-permute-start(f32[4,8,128]{2,1,0:T(8,128)S(1)} %pad_maximum_fusion.refs_2_.refs_5_), channel_id=1, source_target_pairs={{0,16},{16,0},{1,17},{17,1},{2,18},{18,2},{3,19},{19,3},{4,20},{20... | collective-permute-start | bytes 49160 | tf_op jit(solution)/shard_map/ppermute | solution.py:249
  39.5 5.7 %collective-permute-start.24 = (f32[4,8,128]{2,1,0:T(8,128)S(1)}, f32[4,8,128]{2,1,0:T(8,128)S(1)}, u32[]{:S(2)}, u32[]{:S(2)}) collective-permute-start(f32[4,8,128]{2,1,0:T(8,128)S(1)} %pad_maximum_fusion.refs_2_.refs_5_), channel_id=1, source_target_pairs={{0,4},{1,5},{2,6},{3,7},{4,8},{5,9},{6,10},{7,11},{8,12},{9,13},{1... | collective-permute-start | bytes 49160 | tf_op jit(solution)/shard_map/ppermute | solution.py:246
  41.4 5.1 %collective-permute-start.26 = (f32[4,8,128]{2,1,0:T(8,128)S(1)}, f32[4,8,128]{2,1,0:T(8,128)S(1)}, u32[]{:S(2)}, u32[]{:S(2)}) collective-permute-start(f32[4,8,128]{2,1,0:T(8,128)S(1)} %pad_maximum_fusion.refs_2_.refs_5_), channel_id=1, source_target_pairs={{0,12},{1,13},{2,14},{3,15},{4,0},{5,1},{6,2},{7,3},{8,4},{9,5},{1... | collective-permute-start | bytes 49160 | tf_op jit(solution)/shard_map/ppermute | solution.py:246
  44.1 2.9 %collective-permute-start.22 = (bf16[128,1024]{1,0:T(8,128)(2,1)S(1)}, bf16[128,1024]{1,0:T(8,128)(2,1)S(1)}, u32[]{:S(2)}, u32[]{:S(2)}) collective-permute-start(bf16[128,1024]{1,0:T(8,128)(2,1)S(1)} %collective-permute-done.15.refs_9_), channel_id=1, source_target_pairs={{0,16},{16,0},{1,17},{17,1},{2,18},{18,2},{3,19},{19,3},{4,20},{20... | collective-permute-start | bytes 786440 | tf_op jit(solution)/shard_map/ppermute | solution.py:249
  44.2 2.9 %collective-permute-start.20 = (bf16[128,1024]{1,0:T(8,128)(2,1)S(1)}, bf16[128,1024]{1,0:T(8,128)(2,1)S(1)}, u32[]{:S(2)}, u32[]{:S(2)}) collective-permute-start(bf16[128,1024]{1,0:T(8,128)(2,1)S(1)} %collective-permute-done.19.refs_4_.refs_12_), channel_id=1, source_target_pairs={{0,16},{16,0},{1,17},{17,1},{2,18},{18,2},{3,19},{19,3},{4,20},{20... | collective-permute-start | bytes 786440 | tf_op jit(solution)/shard_map/ppermute | solution.py:249
  44.6 4.2 %collective-permute-start.18 = (bf16[128,1024]{1,0:T(8,128)(2,1)S(1)}, bf16[128,1024]{1,0:T(8,128)(2,1)S(1)}, u32[]{:S(2)}, u32[]{:S(2)}) collective-permute-start(bf16[128,1024]{1,0:T(8,128)(2,1)S(1)} %collective-permute-done.17.refs_2_.refs_10_), channel_id=1, source_target_pairs={{0,16},{16,0},{1,17},{17,1},{2,18},{18,2},{3,19},{19,3},{4,20},{20... | collective-permute-start | bytes 786440 | tf_op jit(solution)/shard_map/ppermute | solution.py:249
  45.2 3.6 %collective-permute-start.16 = (bf16[128,1024]{1,0:T(8,128)(2,1)S(1)}, bf16[128,1024]{1,0:T(8,128)(2,1)S(1)}, u32[]{:S(2)}, u32[]{:S(2)}) collective-permute-start(bf16[128,1024]{1,0:T(8,128)(2,1)S(1)} %collective-permute-done.4.refs_0_.refs_8_), channel_id=1, source_target_pairs={{0,16},{16,0},{1,17},{17,1},{2,18},{18,2},{3,19},{19,3},{4,20},{20... | collective-permute-start | bytes 786440 | tf_op jit(solution)/shard_map/ppermute | solution.py:249
  46.5 3.0 %collective-permute-start.23 = (bf16[128,1024]{1,0:T(8,128)(2,1)S(1)}, bf16[128,1024]{1,0:T(8,128)(2,1)S(1)}, u32[]{:S(2)}, u32[]{:S(2)}) collective-permute-start(bf16[128,1024]{1,0:T(8,128)(2,1)S(1)} %get-tuple-element.43), channel_id=1, source_target_pairs={{0,16},{16,0},{1,17},{17,1},{2,18},{18,2},{3,19},{19,3},{4,20},{20... | collective-permute-start | bytes 786440 | tf_op jit(solution)/shard_map/ppermute | solution.py:249
  47.0 2.4 %collective-permute-start.25 = (f32[4,8,128]{2,1,0:T(8,128)S(1)}, f32[4,8,128]{2,1,0:T(8,128)S(1)}, u32[]{:S(2)}, u32[]{:S(2)}) collective-permute-start(f32[4,8,128]{2,1,0:T(8,128)S(1)} %collective-permute-done.24.refs_4_), channel_id=1, source_target_pairs={{0,16},{16,0},{1,17},{17,1},{2,18},{18,2},{3,19},{19,3},{4,20},{20... | collective-permute-start | bytes 49160 | tf_op jit(solution)/shard_map/ppermute | solution.py:249
  47.1 2.3 %collective-permute-start.27 = (f32[4,8,128]{2,1,0:T(8,128)S(1)}, f32[4,8,128]{2,1,0:T(8,128)S(1)}, u32[]{:S(2)}, u32[]{:S(2)}) collective-permute-start(f32[4,8,128]{2,1,0:T(8,128)S(1)} %collective-permute-done.26.refs_6_), channel_id=1, source_target_pairs={{0,16},{16,0},{1,17},{17,1},{2,18},{18,2},{3,19},{19,3},{4,20},{20... | collective-permute-start | bytes 49160 | tf_op jit(solution)/shard_map/ppermute | solution.py:249

commit v4 on v3

--- a/solution.py
+++ b/solution.py
@@ -268,15 +268,18 @@
         smem=1,
     )
     xqs, yqs = [xq, *others(xq)], [yq, *others(yq)]
-    zap, zbp, dp = move(yp, "za"), move(xp, "zb"), move(xp, "y")
+    zap, dp = move(yp, "za"), move(xp, "y")
+    zbp = move(xp, "zb")
     xzp = move(after(zap, xq, yq, own_ml), "x")
     middle, middle_ml = call(
         middle_kernel,
         [shape(((LAST - 1) * rows, q_rows), F32), shape((8, q_rows), F32)],
-        [full_q, side, after(own_ml, *xqs, *yqs), xp, yp, dp, zap, zbp],
+        [full_q, side, own_ml, xp, yp, dp, zap, zbp],
         (LAST - 1) * flops,
     )
-    zaq, zbq = move(after(yq, zbp), "za"), move(after(xq, zbp), "zb")
+    zaq = move(after(yq, zbp), "za")
+    zbq = move(after(xq, zbp), "zb")
+    dq = move(after(xq, xzp), "y")
     stat_rows = -(-(3 * pb + 1) // 8) * 8
     last, stat = call(
         lambda *refs: last_kernel(pb, *refs),
@@ -284,9 +287,10 @@
         [full_q, side, middle_ml, xzp],
         flops,
     )
-    stat_x, stat_y, stat_d = move(stat, "x"), move(stat, "y"), move(stat, "d")
-    four = jnp.stack([stat, stat_x, stat_y, stat_d])
-    dq = move(after(xq, four), "y")
+    stat_x = move(stat, "x")
+    stat_y = move(stat, "y")
+    stat_d = move(stat, "d")
+    four = jnp.stack([after(stat, *xqs, *yqs), stat_x, stat_y, stat_d])
     xzq = move(after(zaq, four), "x")
     up, down = move(four, "up"), move(four, "down")
     fours = [four, *others(four)]
@@ -305,7 +309,7 @@
     (near,) = call(
         lambda *refs: near_kernel(pb, *refs),
         [shape((rows, width), F32)],
-        [own_p, where, *fours, full_q, *xqs, *yqs, dq, *others(dq)],
+        [own_p, where, *fours, full_q, *xqs, *yqs, dq, *others(after(dq, parts[0]))],
         8 * flops,
         scratch=[pltpu.VMEM((rows, 4 * q_rows), F32), *keep(4)],
     )

time: 51.4 us -> 50.2 us (0.977)
  waiting for transfers between devices: 17.9 us -> 16 us
  starting transfers between devices: 23.4 us -> 24.2 us
    ppermute x17, waiting for transfers between devices: 17.9 us -> 14.1 us  [move(): return lax.ppermute(value, 'pa', tables[name])]
    ppermute x11, waiting for transfers between devices: 0.03 us -> 1.85 us  [from_member(): return lax.ppermute(value, 'pb', [(i, (i + r) % pb) for i in range(pb)])]
    ppermute x17, starting transfers between devices: 21.3 us -> 22.2 us  [move(): return lax.ppermute(value, 'pa', tables[name])]
  transfers between devices with their start and end apart: 28 -> 28, of which waited for: 11 -> 8; matrix products, arithmetic and copies ran while one was open for 0% -> 0% of each run, Pallas kernels for 11% -> 11%
where the time goes in v4:
time: 50.2 us; the launch traced here: 50 us
  starting transfers between devices  24.2 us (48%)
  waiting for transfers between devices  16 us (32%)
  Pallas kernels  7.13 us (14%)
  local copies, waits for them, and re-layouts  1.91 us (4%)
  between operations  0.82 us (2%)
    ppermute x17, starting transfers between devices, move(): return lax.ppermute(value, 'pa', tables[name])  22.2 us
    ppermute x17, waiting for transfers between devices, move(): return lax.ppermute(value, 'pa', tables[name])  14.1 us
    pallas_call x7, Pallas kernels, call(): pl.pallas_call(kernel, out_shape=outs, in_specs=[SMEM] * smem + [VMEM] *...  7.13 us
    ppermute x11, starting transfers between devices, from_member(): return lax.ppermute(value, 'pb', [(i, (i + r) % pb) for i in range(pb)])  1.95 us
    unnamed x10, local copies, waits for them, and re-layouts  1.91 us
    ppermute x11, waiting for transfers between devices, from_member(): return lax.ppermute(value, 'pb', [(i, (i + r) % pb) for i in range(pb)])  1.85 us
  transfers between devices with their start and end apart: 28, of which 8 were waited for; matrix products, arithmetic and copies ran while one was open for 0% of the time, Pallas kernels for 11%

profile of v4, /device:TPU:0, one launch (start us, length us, event | category | flops | bytes accessed | tf_op | source)
XLA Modules:
  0.0 50.0 jit_solution(18368553946358269463)
XLA Ops:
  0.7 3.0 %collective-permute-start.6 = (bf16[128,1024]{1,0:T(8,128)(2,1)}, bf16[128,1024]{1,0:T(8,128)(2,1)S(1)}, u32[]{:S(2)}, u32[]{:S(2)}) collective-permute-start(bf16[128,1024]{1,0:T(8,128)(2,1)} %bitcast.8), channel_id=1, source_target_pairs={{0,2},{1,3},{2,0},{3,1},{4,6},{5,7},{6,4},{7,5},{8,10},{9,11},{10,... | collective-permute-start | bytes 786440 | tf_op jit(solution)/shard_map/ppermute | solution.py:246
  3.7 1.5 %collective-permute-start.2 = (bf16[128,1024]{1,0:T(8,128)(2,1)}, bf16[128,1024]{1,0:T(8,128)(2,1)S(1)}, u32[]{:S(2)}, u32[]{:S(2)}) collective-permute-start(bf16[128,1024]{1,0:T(8,128)(2,1)} %bitcast.9), channel_id=1, source_target_pairs={{0,1},{1,0},{2,3},{3,2},{4,5},{5,4},{6,7},{7,6},{8,9},{9,8},{10,11... | collective-permute-start | bytes 786440 | tf_op jit(solution)/shard_map/ppermute | solution.py:246
  5.2 0.5 %collective-permute-start.5 = (bf16[128,1024]{1,0:T(8,128)(2,1)}, bf16[128,1024]{1,0:T(8,128)(2,1)S(1)}, u32[]{:S(2)}, u32[]{:S(2)}) collective-permute-start(bf16[128,1024]{1,0:T(8,128)(2,1)} %bitcast.12), channel_id=1, source_target_pairs={{0,1},{1,0},{2,3},{3,2},{4,5},{5,4},{6,7},{7,6},{8,9},{9,8},{10,11... | collective-permute-start | bytes 786440 | tf_op jit(solution)/shard_map/ppermute | solution.py:246
  5.7 0.1 collective-permute-start.1
  5.8 5.2 %collective-permute-done.6.refs_1_.refs_9_ = bf16[128,1024]{1,0:T(8,128)(2,1)S(1)} collective-permute-done((bf16[128,1024]{1,0:T(8,128)(2,1)}, bf16[128,1024]{1,0:T(8,128)(2,1)S(1)}, u32[]{:S(2)}, u32[]{:S(2)}) %collective-permute-start.6) | collective-permute-done | bytes 262176 | tf_op jit(solution)/shard_map/ppermute | solution.py:246
  11.0 2.1 %collective-permute-start.7 = (bf16[128,1024]{1,0:T(8,128)(2,1)S(1)}, bf16[128,1024]{1,0:T(8,128)(2,1)S(1)}, u32[]{:S(2)}, u32[]{:S(2)}) collective-permute-start(bf16[128,1024]{1,0:T(8,128)(2,1)S(1)} %collective-permute-done.6.refs_1_.refs_9_), channel_id=1, source_target_pairs={{0,4},{1,5},{2,14},{3,15},{4,8},{5,9},{6,2},{7,3},{8,12},{9,13},{1... | collective-permute-start | bytes 786440 | tf_op jit(solution)/shard_map/ppermute | solution.py:246
  13.2 0.0 collective-permute-done.2.refs_0_.refs_8_
  13.2 1.6 %collective-permute-start.3 = (bf16[128,1024]{1,0:T(8,128)(2,1)S(1)}, bf16[128,1024]{1,0:T(8,128)(2,1)S(1)}, u32[]{:S(2)}, u32[]{:S(2)}) collective-permute-start(bf16[128,1024]{1,0:T(8,128)(2,1)S(1)} %collective-permute-done.2.refs_0_.refs_8_), channel_id=1, source_target_pairs={{0,4},{1,13},{2,6},{3,15},{4,8},{5,1},{6,10},{7,3},{8,12},{9,5},{1... | collective-permute-start | bytes 786440 | tf_op jit(solution)/shard_map/ppermute | solution.py:246
  14.7 0.0 collective-permute-done.refs_5_
  14.7 2.0 %collective-permute-start.13 = (bf16[128,1024]{1,0:T(8,128)(2,1)S(1)}, bf16[128,1024]{1,0:T(8,128)(2,1)S(1)}, u32[]{:S(2)}, u32[]{:S(2)}) collective-permute-start(bf16[128,1024]{1,0:T(8,128)(2,1)S(1)} %collective-permute-done.2.refs_0_.refs_8_), channel_id=1, source_target_pairs={{0,2},{1,3},{2,0},{3,1},{4,6},{5,7},{6,4},{7,5},{8,10},{9,11},{10,... | collective-permute-start | bytes 786440 | tf_op jit(solution)/shard_map/ppermute | solution.py:246
  16.8 0.9 %copy-done = bf16[1,128,1024]{2,1,0:T(8,128)(2,1)S(1)} copy-done((bf16[1,128,1024]{2,1,0:T(8,128)(2,1)S(1)}, bf16[1,128,1024]{2,1,0:T(8,128)(2,1)}, u32[]{:S(2)}) %copy-start) | copy-done | bytes 262168
  17.7 0.9 %copy-done.1 = bf16[1,128,1024]{2,1,0:T(8,128)(2,1)S(1)} copy-done((bf16[1,128,1024]{2,1,0:T(8,128)(2,1)S(1)}, bf16[1,128,1024]{2,1,0:T(8,128)(2,1)}, u32[]{:S(2)}) %copy-start.1) | copy-done | bytes 262168
  18.7 1.0 %shard_map.68 = (f32[128,256]{1,0:T(8,128)S(1)}, f32[8,256]{1,0:T(8,128)S(1)}, bf16[256,1024]{1,0:T(8,128)(2,1)S(1)}, bf16[128,1024]{1,0:T(8,128)(2,1)S(1)}, f32...) custom-call(s32[1,7]{1,0:T(1,128)S(1)} %copy-done.4, f32[1,256]{1,0:T(1,128)S(1)} %copy-done.2, s32[1,256]{1,0:T(1,128)S(1)} %copy-done.3, ...), custom_call_target="tpu_custom_call" | custom-call | tf_op jit(solution)/shard_map/pallas_call | solution.py:222
  19.6 0.0 collective-permute-done.1.refs_7_
  19.7 2.6 %collective-permute-done.7.refs_3_.refs_11_ = bf16[128,1024]{1,0:T(8,128)(2,1)S(1)} collective-permute-done((bf16[128,1024]{1,0:T(8,128)(2,1)S(1)}, bf16[128,1024]{1,0:T(8,128)(2,1)S(1)}, u32[]{:S(2)}, u32[]{:S(2)}) %collective-permute-start.7) | collective-permute-done | bytes 262176 | tf_op jit(solution)/shard_map/ppermute | solution.py:246
  22.3 1.5 %collective-permute-start.8 = (bf16[128,1024]{1,0:T(8,128)(2,1)S(1)}, bf16[128,1024]{1,0:T(8,128)(2,1)S(1)}, u32[]{:S(2)}, u32[]{:S(2)}) collective-permute-start(bf16[128,1024]{1,0:T(8,128)(2,1)S(1)} %collective-permute-done.7.refs_3_.refs_11_), channel_id=1, source_target_pairs={{0,1},{1,0},{2,3},{3,2},{4,5},{5,4},{6,7},{7,6},{8,9},{9,8},{10,11... | collective-permute-start | bytes 786440 | tf_op jit(solution)/shard_map/ppermute | solution.py:246
  23.8 0.0 collective-permute-start.14
  23.8 0.5 %collective-permute-start.15 = (bf16[128,1024]{1,0:T(8,128)(2,1)S(1)}, bf16[128,1024]{1,0:T(8,128)(2,1)S(1)}, u32[]{:S(2)}, u32[]{:S(2)}) collective-permute-start(bf16[128,1024]{1,0:T(8,128)(2,1)S(1)} %collective-permute-done.1.refs_7_), channel_id=1, source_target_pairs={{0,16},{16,0},{1,17},{17,1},{2,18},{18,2},{3,19},{19,3},{4,20},{20... | collective-permute-start | bytes 786440 | tf_op jit(solution)/shard_map/ppermute | solution.py:249
  24.4 0.8 %collective-permute-done.3.refs_4_.refs_12_ = bf16[128,1024]{1,0:T(8,128)(2,1)S(1)} collective-permute-done((bf16[128,1024]{1,0:T(8,128)(2,1)S(1)}, bf16[128,1024]{1,0:T(8,128)(2,1)S(1)}, u32[]{:S(2)}, u32[]{:S(2)}) %collective-permute-start.3) | collective-permute-done | bytes 262176 | tf_op jit(solution)/shard_map/ppermute | solution.py:246
  25.1 1.1 %shard_map.69 = (f32[640,256]{1,0:T(8,128)S(1)}, f32[8,256]{1,0:T(8,128)S(1)}) custom-call(bf16[256,1024]{1,0:T(8,128)(2,1)S(1)} %get-tuple-element.33.full_ref.refs_0_.refs_4_, f32[16,256]{1,0:T(8,128)S(1)} %get-tuple-element.34.side_ref.refs_1_.refs_3_, f32[8,256]{1,0:T(8,128)S(1)} %get-tuple-element.27.before_ref, ...), custom_call_target="tpu_custom_call" | custom-call | tf_op jit(solution)/shard_map/pallas_call | solution.py:222
  26.2 2.5 %collective-permute-done.8.refs_3_.refs_13_ = bf16[128,1024]{1,0:T(8,128)(2,1)S(1)} collective-permute-done((bf16[128,1024]{1,0:T(8,128)(2,1)S(1)}, bf16[128,1024]{1,0:T(8,128)(2,1)S(1)}, u32[]{:S(2)}, u32[]{:S(2)}) %collective-permute-start.8) | collective-permute-done | bytes 262176 | tf_op jit(solution)/shard_map/ppermute | solution.py:246
  28.7 0.4 shard_map.70
  29.1 1.6 %collective-permute-start.16 = (f32[8,128]{1,0:T(8,128)S(1)}, f32[8,128]{1,0:T(8,128)S(1)}, u32[]{:S(2)}, u32[]{:S(2)}) collective-permute-start(f32[8,128]{1,0:T(8,128)S(1)} %get-tuple-element.37), channel_id=1, source_target_pairs={{0,1},{1,0},{2,3},{3,2},{4,5},{5,4},{6,7},{7,6},{8,9},{9,8},{10,11... | collective-permute-start | bytes 12296 | tf_op jit(solution)/shard_map/ppermute | solution.py:246
  30.6 2.5 %collective-permute-start.17 = (f32[8,128]{1,0:T(8,128)S(1)}, f32[8,128]{1,0:T(8,128)S(1)}, u32[]{:S(2)}, u32[]{:S(2)}) collective-permute-start(f32[8,128]{1,0:T(8,128)S(1)} %get-tuple-element.37), channel_id=1, source_target_pairs={{0,2},{1,3},{2,0},{3,1},{4,6},{5,7},{6,4},{7,5},{8,10},{9,11},{10,... | collective-permute-start | bytes 12296 | tf_op jit(solution)/shard_map/ppermute | solution.py:246
  33.2 0.1 collective-permute-start.11
  33.3 0.0 collective-permute-done.16
  33.3 1.5 %collective-permute-start.9 = (bf16[128,1024]{1,0:T(8,128)(2,1)S(1)}, bf16[128,1024]{1,0:T(8,128)(2,1)S(1)}, u32[]{:S(2)}, u32[]{:S(2)}) collective-permute-start(bf16[128,1024]{1,0:T(8,128)(2,1)S(1)} %collective-permute-done.5.refs_5_), channel_id=1, source_target_pairs={{0,2},{1,3},{2,0},{3,1},{4,6},{5,7},{6,4},{7,5},{8,10},{9,11},{10,... | collective-permute-start | bytes 786440 | tf_op jit(solution)/shard_map/ppermute | solution.py:246
  34.8 0.0 collective-permute-done.17
  34.8 3.0 %collective-permute-done.18 = f32[8,128]{1,0:T(8,128)S(1)} collective-permute-done((f32[8,128]{1,0:T(8,128)S(1)}, f32[8,128]{1,0:T(8,128)S(1)}, u32[]{:S(2)}, u32[]{:S(2)}) %collective-permute-start.18) | collective-permute-done | bytes 4128 | tf_op jit(solution)/shard_map/ppermute | solution.py:246
  37.8 0.0 collective-permute-done.4.refs_0_.refs_8_
  37.8 1.5 %collective-permute-start.19 = (bf16[128,1024]{1,0:T(8,128)(2,1)S(1)}, bf16[128,1024]{1,0:T(8,128)(2,1)S(1)}, u32[]{:S(2)}, u32[]{:S(2)}) collective-permute-start(bf16[128,1024]{1,0:T(8,128)(2,1)S(1)} %collective-permute-done.4.refs_0_.refs_8_), channel_id=1, source_target_pairs={{0,1},{1,0},{2,3},{3,2},{4,5},{5,4},{6,7},{7,6},{8,9},{9,8},{10,11... | collective-permute-start | bytes 786440 | tf_op jit(solution)/shard_map/ppermute | solution.py:246
  39.3 0.0 collective-permute-start.21
  39.3 0.0 collective-permute-start.24
  39.3 1.2 %collective-permute-done.21.refs_6_.refs_3_ = f32[4,8,128]{2,1,0:T(8,128)S(1)} collective-permute-done((f32[4,8,128]{2,1,0:T(8,128)S(1)}, f32[4,8,128]{2,1,0:T(8,128)S(1)}, u32[]{:S(2)}, u32[]{:S(2)}) %collective-permute-start.21) | collective-permute-done | bytes 16416 | tf_op jit(solution)/shard_map/ppermute | solution.py:249
  40.5 2.6 %collective-permute-start.26 = (f32[4,8,128]{2,1,0:T(8,128)S(1)}, f32[4,8,128]{2,1,0:T(8,128)S(1)}, u32[]{:S(2)}, u32[]{:S(2)}) collective-permute-start(f32[4,8,128]{2,1,0:T(8,128)S(1)} %pad_maximum_fusion.refs_5_.refs_2_), channel_id=1, source_target_pairs={{0,12},{1,13},{2,14},{3,15},{4,0},{5,1},{6,2},{7,3},{8,4},{9,5},{1... | collective-permute-start | bytes 49160 | tf_op jit(solution)/shard_map/ppermute | solution.py:246
  43.1 1.2 %shard_map.72 = (f32[128,1024]{1,0:T(8,128)S(1)}, bf16[128,1024]{1,0:T(8,128)(2,1)S(1)}) custom-call(f32[128,256]{1,0:T(8,128)S(1)} %get-tuple-element.40.refs_0_, f32[640,256]{1,0:T(8,128)S(1)} %get-tuple-element.41.refs_1_, f32[128,256]{1,0:T(8,128)S(1)} %get-tuple-element.42.refs_2_, f32[16,256]{1,0:T(8,128)S(1)} %get-tuple-element.34.side_ref.refs_1_.refs_3_, ...), custom_call_target="tpu_custom_call" | custom-call | tf_op jit(solution)/shard_map/pallas_call | solution.py:222
  44.4 0.1 collective-permute-start.22
  44.4 0.5 collective-permute-start.12
  44.9 0.1 collective-permute-start.10
  45.0 0.4 collective-permute-start.20
  45.5 0.1 collective-permute-start.23
  45.5 0.4 collective-permute-done.22.refs_10_
  46.0 0.1 collective-permute-start.25
  46.1 0.2 collective-permute-done.12.refs_3_.refs_11_
  46.3 0.1 collective-permute-start.27
  46.5 1.3 %shard_map.73.refs_1_ = f32[128,1024]{1,0:T(8,128)S(1)} custom-call(bf16[128,1024]{1,0:T(8,128)(2,1)S(1)} %get-tuple-element.25.p_ref.refs_7_.refs_0_, s32[1,256]{1,0:T(1,128)S(1)} %get-tuple-element.39.refs_4_.refs_1_, f32[4,8,128]{2,1,0:T(8,128)S(1)} %pad_maximum_fusion.refs_5_.refs_2_, f32[4,8,128]{2,1,0:T(8,128)S(1)} %collective-permute-done.21.refs_6_.refs_3_, ...), custom_call_target="tpu_custom_call" | custom-call | tf_op jit(solution)/shard_map/pallas_call | solution.py:222
  47.8 0.6 %shard_map.71.refs_0_ = f32[128,768]{1,0:T(8,128)S(1)} custom-call(bf16[128,1024]{1,0:T(8,128)(2,1)S(1)} %get-tuple-element.25.p_ref.refs_7_.refs_0_, bf16[128,1024]{1,0:T(8,128)(2,1)S(1)} %collective-permute-done.4.refs_0_.refs_8_, bf16[128,1024]{1,0:T(8,128)(2,1)S(1)} %collective-permute-done.10.refs_1_.refs_9_, ...), custom_call_target="tpu_custom_call" | custom-call | tf_op jit(solution)/shard_map/pallas_call | solution.py:222
  48.4 1.6 %shard_map.74 = (f32[128,1024]{1,0:T(8,128)}, f32[128,1024]{1,0:T(8,128)}) custom-call(f32[128,768]{1,0:T(8,128)S(1)} %shard_map.71.refs_0_, f32[128,1024]{1,0:T(8,128)S(1)} %shard_map.73.refs_1_, f32[128,1024]{1,0:T(8,128)S(1)} %get-tuple-element.43.refs_2_, bf16[128,1024]{1,0:T(8,128)(2,1)S(1)} %collective-permute-done.23.refs_3_, ...), custom_call_target="tpu_custom_call" | custom-call | tf_op jit(solution)/shard_map/pallas_call | solution.py:222
  (26 shorter events, 0.1 us)
Async XLA Ops:
  0.6 16.1 %copy-start.3 = (s32[1,256]{1,0:T(1,128)S(1)}, s32[1,256]{1,0:T(1,128)}, u32[]{:S(2)}) copy-start(s32[1,256]{1,0:T(1,128)} %refs_2_.1) | copy-start | bytes 3076
  0.6 16.1 %copy-start.2 = (f32[1,256]{1,0:T(1,128)S(1)}, f32[1,256]{1,0:T(1,128)}, u32[]{:S(2)}) copy-start(f32[1,256]{1,0:T(1,128)} %refs_1_.1) | copy-start | bytes 3076
  0.7 16.1 %copy-start.4 = (s32[1,7]{1,0:T(1,128)S(1)}, s32[1,7]{1,0:T(1,128)}, u32[]{:S(2)}) copy-start(s32[1,7]{1,0:T(1,128)} %refs_0_.1) | copy-start | bytes 88
  0.7 10.4 %collective-permute-start.6 = (bf16[128,1024]{1,0:T(8,128)(2,1)}, bf16[128,1024]{1,0:T(8,128)(2,1)S(1)}, u32[]{:S(2)}, u32[]{:S(2)}) collective-permute-start(bf16[128,1024]{1,0:T(8,128)(2,1)} %bitcast.8), channel_id=1, source_target_pairs={{0,2},{1,3},{2,0},{3,1},{4,6},{5,7},{6,4},{7,5},{8,10},{9,11},{10,... | collective-permute-start | bytes 786440 | tf_op jit(solution)/shard_map/ppermute | solution.py:246
  3.7 9.5 %collective-permute-start.2 = (bf16[128,1024]{1,0:T(8,128)(2,1)}, bf16[128,1024]{1,0:T(8,128)(2,1)S(1)}, u32[]{:S(2)}, u32[]{:S(2)}) collective-permute-start(bf16[128,1024]{1,0:T(8,128)(2,1)} %bitcast.9), channel_id=1, source_target_pairs={{0,1},{1,0},{2,3},{3,2},{4,5},{5,4},{6,7},{7,6},{8,9},{9,8},{10,11... | collective-permute-start | bytes 786440 | tf_op jit(solution)/shard_map/ppermute | solution.py:246
  5.2 9.6 %collective-permute-start = (bf16[128,1024]{1,0:T(8,128)(2,1)}, bf16[128,1024]{1,0:T(8,128)(2,1)S(1)}, u32[]{:S(2)}, u32[]{:S(2)}) collective-permute-start(bf16[128,1024]{1,0:T(8,128)(2,1)} %bitcast.11), channel_id=1, source_target_pairs={{0,16},{16,0},{1,17},{17,1},{2,18},{18,2},{3,19},{19,3},{4,20},{20... | collective-permute-start | bytes 786440 | tf_op jit(solution)/shard_map/ppermute | solution.py:249
  5.2 14.5 %collective-permute-start.5 = (bf16[128,1024]{1,0:T(8,128)(2,1)}, bf16[128,1024]{1,0:T(8,128)(2,1)S(1)}, u32[]{:S(2)}, u32[]{:S(2)}) collective-permute-start(bf16[128,1024]{1,0:T(8,128)(2,1)} %bitcast.12), channel_id=1, source_target_pairs={{0,1},{1,0},{2,3},{3,2},{4,5},{5,4},{6,7},{7,6},{8,9},{9,8},{10,11... | collective-permute-start | bytes 786440 | tf_op jit(solution)/shard_map/ppermute | solution.py:246
  5.7 13.9 %collective-permute-start.1 = (bf16[128,1024]{1,0:T(8,128)(2,1)}, bf16[128,1024]{1,0:T(8,128)(2,1)S(1)}, u32[]{:S(2)}, u32[]{:S(2)}) collective-permute-start(bf16[128,1024]{1,0:T(8,128)(2,1)} %bitcast.13), channel_id=1, source_target_pairs={{0,2},{1,3},{2,0},{3,1},{4,6},{5,7},{6,4},{7,5},{8,10},{9,11},{10,... | collective-permute-start | bytes 786440 | tf_op jit(solution)/shard_map/ppermute | solution.py:246
  11.0 11.3 %collective-permute-start.7 = (bf16[128,1024]{1,0:T(8,128)(2,1)S(1)}, bf16[128,1024]{1,0:T(8,128)(2,1)S(1)}, u32[]{:S(2)}, u32[]{:S(2)}) collective-permute-start(bf16[128,1024]{1,0:T(8,128)(2,1)S(1)} %collective-permute-done.6.refs_1_.refs_9_), channel_id=1, source_target_pairs={{0,4},{1,5},{2,14},{3,15},{4,8},{5,9},{6,2},{7,3},{8,12},{9,13},{1... | collective-permute-start | bytes 786440 | tf_op jit(solution)/shard_map/ppermute | solution.py:246
  13.2 12.0 %collective-permute-start.3 = (bf16[128,1024]{1,0:T(8,128)(2,1)S(1)}, bf16[128,1024]{1,0:T(8,128)(2,1)S(1)}, u32[]{:S(2)}, u32[]{:S(2)}) collective-permute-start(bf16[128,1024]{1,0:T(8,128)(2,1)S(1)} %collective-permute-done.2.refs_0_.refs_8_), channel_id=1, source_target_pairs={{0,4},{1,13},{2,6},{3,15},{4,8},{5,1},{6,10},{7,3},{8,12},{9,5},{1... | collective-permute-start | bytes 786440 | tf_op jit(solution)/shard_map/ppermute | solution.py:246
  14.7 10.4 %collective-permute-start.13 = (bf16[128,1024]{1,0:T(8,128)(2,1)S(1)}, bf16[128,1024]{1,0:T(8,128)(2,1)S(1)}, u32[]{:S(2)}, u32[]{:S(2)}) collective-permute-start(bf16[128,1024]{1,0:T(8,128)(2,1)S(1)} %collective-permute-done.2.refs_0_.refs_8_), channel_id=1, source_target_pairs={{0,2},{1,3},{2,0},{3,1},{4,6},{5,7},{6,4},{7,5},{8,10},{9,11},{10,... | collective-permute-start | bytes 786440 | tf_op jit(solution)/shard_map/ppermute | solution.py:246
  16.8 1.0 %copy-start = (bf16[1,128,1024]{2,1,0:T(8,128)(2,1)S(1)}, bf16[1,128,1024]{2,1,0:T(8,128)(2,1)}, u32[]{:S(2)}) copy-start(bf16[1,128,1024]{2,1,0:T(8,128)(2,1)} %param.6) | copy-start | bytes 786436
  17.7 0.9 %copy-start.1 = (bf16[1,128,1024]{2,1,0:T(8,128)(2,1)S(1)}, bf16[1,128,1024]{2,1,0:T(8,128)(2,1)}, u32[]{:S(2)}) copy-start(bf16[1,128,1024]{2,1,0:T(8,128)(2,1)} %param.5) | copy-start | bytes 786436
  22.3 6.4 %collective-permute-start.8 = (bf16[128,1024]{1,0:T(8,128)(2,1)S(1)}, bf16[128,1024]{1,0:T(8,128)(2,1)S(1)}, u32[]{:S(2)}, u32[]{:S(2)}) collective-permute-start(bf16[128,1024]{1,0:T(8,128)(2,1)S(1)} %collective-permute-done.7.refs_3_.refs_11_), channel_id=1, source_target_pairs={{0,1},{1,0},{2,3},{3,2},{4,5},{5,4},{6,7},{7,6},{8,9},{9,8},{10,11... | collective-permute-start | bytes 786440 | tf_op jit(solution)/shard_map/ppermute | solution.py:246
  23.8 9.3 %collective-permute-start.14 = (bf16[128,1024]{1,0:T(8,128)(2,1)S(1)}, bf16[128,1024]{1,0:T(8,128)(2,1)S(1)}, u32[]{:S(2)}, u32[]{:S(2)}) collective-permute-start(bf16[128,1024]{1,0:T(8,128)(2,1)S(1)} %collective-permute-done.5.refs_5_), channel_id=1, source_target_pairs={{0,16},{16,0},{1,17},{17,1},{2,18},{18,2},{3,19},{19,3},{4,20},{20... | collective-permute-start | bytes 786440 | tf_op jit(solution)/shard_map/ppermute | solution.py:249
  23.8 9.3 %collective-permute-start.15 = (bf16[128,1024]{1,0:T(8,128)(2,1)S(1)}, bf16[128,1024]{1,0:T(8,128)(2,1)S(1)}, u32[]{:S(2)}, u32[]{:S(2)}) collective-permute-start(bf16[128,1024]{1,0:T(8,128)(2,1)S(1)} %collective-permute-done.1.refs_7_), channel_id=1, source_target_pairs={{0,16},{16,0},{1,17},{17,1},{2,18},{18,2},{3,19},{19,3},{4,20},{20... | collective-permute-start | bytes 786440 | tf_op jit(solution)/shard_map/ppermute | solution.py:249
  25.1 12.7 %collective-permute-start.4 = (bf16[128,1024]{1,0:T(8,128)(2,1)S(1)}, bf16[128,1024]{1,0:T(8,128)(2,1)S(1)}, u32[]{:S(2)}, u32[]{:S(2)}) collective-permute-start(bf16[128,1024]{1,0:T(8,128)(2,1)S(1)} %collective-permute-done.1.refs_7_), channel_id=1, source_target_pairs={{0,4},{1,5},{2,14},{3,15},{4,8},{5,9},{6,2},{7,3},{8,12},{9,13},{1... | collective-permute-start | bytes 786440 | tf_op jit(solution)/shard_map/ppermute | solution.py:246
  29.1 4.2 %collective-permute-start.16 = (f32[8,128]{1,0:T(8,128)S(1)}, f32[8,128]{1,0:T(8,128)S(1)}, u32[]{:S(2)}, u32[]{:S(2)}) collective-permute-start(f32[8,128]{1,0:T(8,128)S(1)} %get-tuple-element.37), channel_id=1, source_target_pairs={{0,1},{1,0},{2,3},{3,2},{4,5},{5,4},{6,7},{7,6},{8,9},{9,8},{10,11... | collective-permute-start | bytes 12296 | tf_op jit(solution)/shard_map/ppermute | solution.py:246
  30.6 4.2 %collective-permute-start.17 = (f32[8,128]{1,0:T(8,128)S(1)}, f32[8,128]{1,0:T(8,128)S(1)}, u32[]{:S(2)}, u32[]{:S(2)}) collective-permute-start(f32[8,128]{1,0:T(8,128)S(1)} %get-tuple-element.37), channel_id=1, source_target_pairs={{0,2},{1,3},{2,0},{3,1},{4,6},{5,7},{6,4},{7,5},{8,10},{9,11},{10,... | collective-permute-start | bytes 12296 | tf_op jit(solution)/shard_map/ppermute | solution.py:246
  33.2 4.6 %collective-permute-start.18 = (f32[8,128]{1,0:T(8,128)S(1)}, f32[8,128]{1,0:T(8,128)S(1)}, u32[]{:S(2)}, u32[]{:S(2)}) collective-permute-start(f32[8,128]{1,0:T(8,128)S(1)} %get-tuple-element.37), channel_id=1, source_target_pairs={{0,3},{1,2},{2,1},{3,0},{4,7},{5,6},{6,5},{7,4},{8,11},{9,10},{10,... | collective-permute-start | bytes 12296 | tf_op jit(solution)/shard_map/ppermute | solution.py:246
  33.2 11.2 %collective-permute-start.11 = (bf16[128,1024]{1,0:T(8,128)(2,1)S(1)}, bf16[128,1024]{1,0:T(8,128)(2,1)S(1)}, u32[]{:S(2)}, u32[]{:S(2)}) collective-permute-start(bf16[128,1024]{1,0:T(8,128)(2,1)S(1)} %collective-permute-done.5.refs_5_), channel_id=1, source_target_pairs={{0,4},{1,13},{2,6},{3,15},{4,8},{5,1},{6,10},{7,3},{8,12},{9,5},{1... | collective-permute-start | bytes 786440 | tf_op jit(solution)/shard_map/ppermute | solution.py:246
  33.3 11.1 %collective-permute-start.9 = (bf16[128,1024]{1,0:T(8,128)(2,1)S(1)}, bf16[128,1024]{1,0:T(8,128)(2,1)S(1)}, u32[]{:S(2)}, u32[]{:S(2)}) collective-permute-start(bf16[128,1024]{1,0:T(8,128)(2,1)S(1)} %collective-permute-done.5.refs_5_), channel_id=1, source_target_pairs={{0,2},{1,3},{2,0},{3,1},{4,6},{5,7},{6,4},{7,5},{8,10},{9,11},{10,... | collective-permute-start | bytes 786440 | tf_op jit(solution)/shard_map/ppermute | solution.py:246
  37.8 7.2 %collective-permute-start.19 = (bf16[128,1024]{1,0:T(8,128)(2,1)S(1)}, bf16[128,1024]{1,0:T(8,128)(2,1)S(1)}, u32[]{:S(2)}, u32[]{:S(2)}) collective-permute-start(bf16[128,1024]{1,0:T(8,128)(2,1)S(1)} %collective-permute-done.4.refs_0_.refs_8_), channel_id=1, source_target_pairs={{0,1},{1,0},{2,3},{3,2},{4,5},{5,4},{6,7},{7,6},{8,9},{9,8},{10,11... | collective-permute-start | bytes 786440 | tf_op jit(solution)/shard_map/ppermute | solution.py:246
  39.3 1.2 %collective-permute-start.21 = (f32[4,8,128]{2,1,0:T(8,128)S(1)}, f32[4,8,128]{2,1,0:T(8,128)S(1)}, u32[]{:S(2)}, u32[]{:S(2)}) collective-permute-start(f32[4,8,128]{2,1,0:T(8,128)S(1)} %pad_maximum_fusion.refs_5_.refs_2_), channel_id=1, source_target_pairs={{0,16},{16,0},{1,17},{17,1},{2,18},{18,2},{3,19},{19,3},{4,20},{20... | collective-permute-start | bytes 49160 | tf_op jit(solution)/shard_map/ppermute | solution.py:249
  39.3 5.7 %collective-permute-start.24 = (f32[4,8,128]{2,1,0:T(8,128)S(1)}, f32[4,8,128]{2,1,0:T(8,128)S(1)}, u32[]{:S(2)}, u32[]{:S(2)}) collective-permute-start(f32[4,8,128]{2,1,0:T(8,128)S(1)} %pad_maximum_fusion.refs_5_.refs_2_), channel_id=1, source_target_pairs={{0,4},{1,5},{2,6},{3,7},{4,8},{5,9},{6,10},{7,11},{8,12},{9,13},{1... | collective-permute-start | bytes 49160 | tf_op jit(solution)/shard_map/ppermute | solution.py:246
  40.5 5.0 %collective-permute-start.26 = (f32[4,8,128]{2,1,0:T(8,128)S(1)}, f32[4,8,128]{2,1,0:T(8,128)S(1)}, u32[]{:S(2)}, u32[]{:S(2)}) collective-permute-start(f32[4,8,128]{2,1,0:T(8,128)S(1)} %pad_maximum_fusion.refs_5_.refs_2_), channel_id=1, source_target_pairs={{0,12},{1,13},{2,14},{3,15},{4,0},{5,1},{6,2},{7,3},{8,4},{9,5},{1... | collective-permute-start | bytes 49160 | tf_op jit(solution)/shard_map/ppermute | solution.py:246
  44.4 1.6 %collective-permute-start.22 = (bf16[128,1024]{1,0:T(8,128)(2,1)S(1)}, bf16[128,1024]{1,0:T(8,128)(2,1)S(1)}, u32[]{:S(2)}, u32[]{:S(2)}) collective-permute-start(bf16[128,1024]{1,0:T(8,128)(2,1)S(1)} %collective-permute-done.9.refs_9_), channel_id=1, source_target_pairs={{0,16},{16,0},{1,17},{17,1},{2,18},{18,2},{3,19},{19,3},{4,20},{20... | collective-permute-start | bytes 786440 | tf_op jit(solution)/shard_map/ppermute | solution.py:249
  44.4 1.9 %collective-permute-start.12 = (bf16[128,1024]{1,0:T(8,128)(2,1)S(1)}, bf16[128,1024]{1,0:T(8,128)(2,1)S(1)}, u32[]{:S(2)}, u32[]{:S(2)}) collective-permute-start(bf16[128,1024]{1,0:T(8,128)(2,1)S(1)} %collective-permute-done.11.refs_2_.refs_10_), channel_id=1, source_target_pairs={{0,16},{16,0},{1,17},{17,1},{2,18},{18,2},{3,19},{19,3},{4,20},{20... | collective-permute-start | bytes 786440 | tf_op jit(solution)/shard_map/ppermute | solution.py:249
  44.9 2.8 %collective-permute-start.10 = (bf16[128,1024]{1,0:T(8,128)(2,1)S(1)}, bf16[128,1024]{1,0:T(8,128)(2,1)S(1)}, u32[]{:S(2)}, u32[]{:S(2)}) collective-permute-start(bf16[128,1024]{1,0:T(8,128)(2,1)S(1)} %collective-permute-done.4.refs_0_.refs_8_), channel_id=1, source_target_pairs={{0,16},{16,0},{1,17},{17,1},{2,18},{18,2},{3,19},{19,3},{4,20},{20... | collective-permute-start | bytes 786440 | tf_op jit(solution)/shard_map/ppermute | solution.py:249
  45.0 2.7 %collective-permute-start.20 = (bf16[128,1024]{1,0:T(8,128)(2,1)S(1)}, bf16[128,1024]{1,0:T(8,128)(2,1)S(1)}, u32[]{:S(2)}, u32[]{:S(2)}) collective-permute-start(bf16[128,1024]{1,0:T(8,128)(2,1)S(1)} %collective-permute-done.19.refs_4_.refs_12_), channel_id=1, source_target_pairs={{0,16},{16,0},{1,17},{17,1},{2,18},{18,2},{3,19},{19,3},{4,20},{20... | collective-permute-start | bytes 786440 | tf_op jit(solution)/shard_map/ppermute | solution.py:249
  45.5 2.9 %collective-permute-start.23 = (bf16[128,1024]{1,0:T(8,128)(2,1)S(1)}, bf16[128,1024]{1,0:T(8,128)(2,1)S(1)}, u32[]{:S(2)}, u32[]{:S(2)}) collective-permute-start(bf16[128,1024]{1,0:T(8,128)(2,1)S(1)} %get-tuple-element.45), channel_id=1, source_target_pairs={{0,16},{16,0},{1,17},{17,1},{2,18},{18,2},{3,19},{19,3},{4,20},{20... | collective-permute-start | bytes 786440 | tf_op jit(solution)/shard_map/ppermute | solution.py:249
  46.0 2.4 %collective-permute-start.25 = (f32[4,8,128]{2,1,0:T(8,128)S(1)}, f32[4,8,128]{2,1,0:T(8,128)S(1)}, u32[]{:S(2)}, u32[]{:S(2)}) collective-permute-start(f32[4,8,128]{2,1,0:T(8,128)S(1)} %collective-permute-done.24.refs_4_), channel_id=1, source_target_pairs={{0,16},{16,0},{1,17},{17,1},{2,18},{18,2},{3,19},{19,3},{4,20},{20... | collective-permute-start | bytes 49160 | tf_op jit(solution)/shard_map/ppermute | solution.py:249
  46.3 2.0 %collective-permute-start.27 = (f32[4,8,128]{2,1,0:T(8,128)S(1)}, f32[4,8,128]{2,1,0:T(8,128)S(1)}, u32[]{:S(2)}, u32[]{:S(2)}) collective-permute-start(f32[4,8,128]{2,1,0:T(8,128)S(1)} %collective-permute-done.26.refs_6_), channel_id=1, source_target_pairs={{0,16},{16,0},{1,17},{17,1},{2,18},{18,2},{3,19},{19,3},{4,20},{20... | collective-permute-start | bytes 49160 | tf_op jit(solution)/shard_map/ppermute | solution.py:249

commit v5 on v4

--- a/solution.py
+++ b/solution.py
@@ -274,7 +274,7 @@
     middle, middle_ml = call(
         middle_kernel,
         [shape(((LAST - 1) * rows, q_rows), F32), shape((8, q_rows), F32)],
-        [full_q, side, own_ml, xp, yp, dp, zap, zbp],
+        [full_q, side, after(own_ml, *xqs, *yqs), xp, yp, dp, zap, zbp],
         (LAST - 1) * flops,
     )
     zaq = move(after(yq, zbp), "za")
@@ -289,9 +289,9 @@
     )
     stat_x = move(stat, "x")
     stat_y = move(stat, "y")
-    stat_d = move(stat, "d")
-    four = jnp.stack([after(stat, *xqs, *yqs), stat_x, stat_y, stat_d])
-    xzq = move(after(zaq, four), "x")
+    stat_d = move(stat_y, "x")
+    four = jnp.stack([stat, stat_x, stat_y, stat_d])
+    xzq = move(after(zaq, four, zbq), "x")
     up, down = move(four, "up"), move(four, "down")
     fours = [four, *others(four)]
     parts = call(

time: 50.2 us -> 50.1 us (level)
  starting transfers between devices: 24.2 us -> 24.9 us
  waiting for transfers between devices: 16 us -> 15.3 us
    ppermute x11, waiting for transfers between devices: 1.85 us -> 0.68 us  [from_member(): return lax.ppermute(value, 'pb', [(i, (i + r) % pb) for i in range(pb)])]
    ppermute x17, starting transfers between devices: 22.2 us -> 23.2 us  [move(): return lax.ppermute(value, 'pa', tables[name])]
  transfers between devices with their start and end apart: 28 -> 28, of which waited for: 8 -> 10; matrix products, arithmetic and copies ran while one was open for 0% -> 0% of each run, Pallas kernels for 11% -> 11%
where the time goes in v5:
time: 50.1 us; the launch traced here: 49.9 us
  starting transfers between devices  24.9 us (50%)
  waiting for transfers between devices  15.3 us (31%)
  Pallas kernels  7.13 us (14%)
  local copies, waits for them, and re-layouts  1.91 us (4%)
  between operations  0.78 us (2%)
    ppermute x17, starting transfers between devices, move(): return lax.ppermute(value, 'pa', tables[name])  23.2 us
    ppermute x17, waiting for transfers between devices, move(): return lax.ppermute(value, 'pa', tables[name])  14.6 us
    pallas_call x7, Pallas kernels, call(): pl.pallas_call(kernel, out_shape=outs, in_specs=[SMEM] * smem + [VMEM] *...  7.13 us
    unnamed x10, local copies, waits for them, and re-layouts  1.91 us
    ppermute x11, starting transfers between devices, from_member(): return lax.ppermute(value, 'pb', [(i, (i + r) % pb) for i in range(pb)])  1.67 us
  transfers between devices with their start and end apart: 28, of which 10 were waited for; matrix products, arithmetic and copies ran while one was open for 0% of the time, Pallas kernels for 11%

profile of v5, /device:TPU:0, one launch (start us, length us, event | category | flops | bytes accessed | tf_op | source)
XLA Modules:
  0.0 49.9 jit_solution(2553187255036659205)
XLA Ops:
  0.7 3.0 %collective-permute-start.6 = (bf16[128,1024]{1,0:T(8,128)(2,1)}, bf16[128,1024]{1,0:T(8,128)(2,1)S(1)}, u32[]{:S(2)}, u32[]{:S(2)}) collective-permute-start(bf16[128,1024]{1,0:T(8,128)(2,1)} %bitcast.8), channel_id=1, source_target_pairs={{0,2},{1,3},{2,0},{3,1},{4,6},{5,7},{6,4},{7,5},{8,10},{9,11},{10,... | collective-permute-start | bytes 786440 | tf_op jit(solution)/shard_map/ppermute | solution.py:246
  3.7 1.5 %collective-permute-start.2 = (bf16[128,1024]{1,0:T(8,128)(2,1)}, bf16[128,1024]{1,0:T(8,128)(2,1)S(1)}, u32[]{:S(2)}, u32[]{:S(2)}) collective-permute-start(bf16[128,1024]{1,0:T(8,128)(2,1)} %bitcast.9), channel_id=1, source_target_pairs={{0,1},{1,0},{2,3},{3,2},{4,5},{5,4},{6,7},{7,6},{8,9},{9,8},{10,11... | collective-permute-start | bytes 786440 | tf_op jit(solution)/shard_map/ppermute | solution.py:246
  5.2 0.5 %collective-permute-start.5 = (bf16[128,1024]{1,0:T(8,128)(2,1)}, bf16[128,1024]{1,0:T(8,128)(2,1)S(1)}, u32[]{:S(2)}, u32[]{:S(2)}) collective-permute-start(bf16[128,1024]{1,0:T(8,128)(2,1)} %bitcast.11), channel_id=1, source_target_pairs={{0,1},{1,0},{2,3},{3,2},{4,5},{5,4},{6,7},{7,6},{8,9},{9,8},{10,11... | collective-permute-start | bytes 786440 | tf_op jit(solution)/shard_map/ppermute | solution.py:246
  5.7 0.1 collective-permute-start.1
  5.8 5.2 %collective-permute-done.6.refs_1_.refs_9_ = bf16[128,1024]{1,0:T(8,128)(2,1)S(1)} collective-permute-done((bf16[128,1024]{1,0:T(8,128)(2,1)}, bf16[128,1024]{1,0:T(8,128)(2,1)S(1)}, u32[]{:S(2)}, u32[]{:S(2)}) %collective-permute-start.6) | collective-permute-done | bytes 262176 | tf_op jit(solution)/shard_map/ppermute | solution.py:246
  11.0 2.1 %collective-permute-start.7 = (bf16[128,1024]{1,0:T(8,128)(2,1)S(1)}, bf16[128,1024]{1,0:T(8,128)(2,1)S(1)}, u32[]{:S(2)}, u32[]{:S(2)}) collective-permute-start(bf16[128,1024]{1,0:T(8,128)(2,1)S(1)} %collective-permute-done.6.refs_1_.refs_9_), channel_id=1, source_target_pairs={{0,4},{1,5},{2,14},{3,15},{4,8},{5,9},{6,2},{7,3},{8,12},{9,13},{1... | collective-permute-start | bytes 786440 | tf_op jit(solution)/shard_map/ppermute | solution.py:246
  13.2 0.0 collective-permute-done.2.refs_0_.refs_8_
  13.2 1.6 %collective-permute-start.3 = (bf16[128,1024]{1,0:T(8,128)(2,1)S(1)}, bf16[128,1024]{1,0:T(8,128)(2,1)S(1)}, u32[]{:S(2)}, u32[]{:S(2)}) collective-permute-start(bf16[128,1024]{1,0:T(8,128)(2,1)S(1)} %collective-permute-done.2.refs_0_.refs_8_), channel_id=1, source_target_pairs={{0,4},{1,13},{2,6},{3,15},{4,8},{5,1},{6,10},{7,3},{8,12},{9,5},{1... | collective-permute-start | bytes 786440 | tf_op jit(solution)/shard_map/ppermute | solution.py:246
  14.7 2.6 %collective-permute-done.5.refs_5_ = bf16[128,1024]{1,0:T(8,128)(2,1)S(1)} collective-permute-done((bf16[128,1024]{1,0:T(8,128)(2,1)}, bf16[128,1024]{1,0:T(8,128)(2,1)S(1)}, u32[]{:S(2)}, u32[]{:S(2)}) %collective-permute-start.5) | collective-permute-done | bytes 262176 | tf_op jit(solution)/shard_map/ppermute | solution.py:246
  17.3 0.0 collective-permute-done.refs_5_
  17.3 0.4 collective-permute-start.15
  17.7 0.0 collective-permute-done.1.refs_7_
  17.7 0.2 collective-permute-start.14
  17.9 0.9 %copy-done = bf16[1,128,1024]{2,1,0:T(8,128)(2,1)S(1)} copy-done((bf16[1,128,1024]{2,1,0:T(8,128)(2,1)S(1)}, bf16[1,128,1024]{2,1,0:T(8,128)(2,1)}, u32[]{:S(2)}) %copy-start) | copy-done | bytes 262168
  18.8 0.9 %copy-done.1 = bf16[1,128,1024]{2,1,0:T(8,128)(2,1)S(1)} copy-done((bf16[1,128,1024]{2,1,0:T(8,128)(2,1)S(1)}, bf16[1,128,1024]{2,1,0:T(8,128)(2,1)}, u32[]{:S(2)}) %copy-start.1) | copy-done | bytes 262168
  19.8 0.9 %shard_map.68 = (f32[128,256]{1,0:T(8,128)S(1)}, f32[8,256]{1,0:T(8,128)S(1)}, bf16[256,1024]{1,0:T(8,128)(2,1)S(1)}, bf16[128,1024]{1,0:T(8,128)(2,1)S(1)}, f32...) custom-call(s32[1,7]{1,0:T(1,128)S(1)} %copy-done.4, f32[1,256]{1,0:T(1,128)S(1)} %copy-done.2, s32[1,256]{1,0:T(1,128)S(1)} %copy-done.3, ...), custom_call_target="tpu_custom_call" | custom-call | tf_op jit(solution)/shard_map/pallas_call | solution.py:222
  20.7 1.6 %collective-permute-done.7.refs_3_.refs_11_ = bf16[128,1024]{1,0:T(8,128)(2,1)S(1)} collective-permute-done((bf16[128,1024]{1,0:T(8,128)(2,1)S(1)}, bf16[128,1024]{1,0:T(8,128)(2,1)S(1)}, u32[]{:S(2)}, u32[]{:S(2)}) %collective-permute-start.7) | collective-permute-done | bytes 262176 | tf_op jit(solution)/shard_map/ppermute | solution.py:246
  22.3 1.5 %collective-permute-start.8 = (bf16[128,1024]{1,0:T(8,128)(2,1)S(1)}, bf16[128,1024]{1,0:T(8,128)(2,1)S(1)}, u32[]{:S(2)}, u32[]{:S(2)}) collective-permute-start(bf16[128,1024]{1,0:T(8,128)(2,1)S(1)} %collective-permute-done.7.refs_3_.refs_11_), channel_id=1, source_target_pairs={{0,1},{1,0},{2,3},{3,2},{4,5},{5,4},{6,7},{7,6},{8,9},{9,8},{10,11... | collective-permute-start | bytes 786440 | tf_op jit(solution)/shard_map/ppermute | solution.py:246
  23.8 1.3 %collective-permute-done.3.refs_4_.refs_12_ = bf16[128,1024]{1,0:T(8,128)(2,1)S(1)} collective-permute-done((bf16[128,1024]{1,0:T(8,128)(2,1)S(1)}, bf16[128,1024]{1,0:T(8,128)(2,1)S(1)}, u32[]{:S(2)}, u32[]{:S(2)}) %collective-permute-start.3) | collective-permute-done | bytes 262176 | tf_op jit(solution)/shard_map/ppermute | solution.py:246
  25.1 0.0 collective-permute-done.13.refs_6_
  25.1 1.3 %collective-permute-start.4 = (bf16[128,1024]{1,0:T(8,128)(2,1)S(1)}, bf16[128,1024]{1,0:T(8,128)(2,1)S(1)}, u32[]{:S(2)}, u32[]{:S(2)}) collective-permute-start(bf16[128,1024]{1,0:T(8,128)(2,1)S(1)} %collective-permute-done.1.refs_7_), channel_id=1, source_target_pairs={{0,4},{1,5},{2,14},{3,15},{4,8},{5,9},{6,2},{7,3},{8,12},{9,13},{1... | collective-permute-start | bytes 786440 | tf_op jit(solution)/shard_map/ppermute | solution.py:246
  26.4 1.1 %shard_map.69 = (f32[640,256]{1,0:T(8,128)S(1)}, f32[8,256]{1,0:T(8,128)S(1)}) custom-call(bf16[256,1024]{1,0:T(8,128)(2,1)S(1)} %get-tuple-element.33.full_ref.refs_0_.refs_4_, f32[16,256]{1,0:T(8,128)S(1)} %get-tuple-element.34.side_ref.refs_1_.refs_3_, f32[8,256]{1,0:T(8,128)S(1)} %get-tuple-element.35.before_ref, ...), custom_call_target="tpu_custom_call" | custom-call | tf_op jit(solution)/shard_map/pallas_call | solution.py:222
  27.5 1.8 %collective-permute-done.8.refs_3_.refs_13_ = bf16[128,1024]{1,0:T(8,128)(2,1)S(1)} collective-permute-done((bf16[128,1024]{1,0:T(8,128)(2,1)S(1)}, bf16[128,1024]{1,0:T(8,128)(2,1)S(1)}, u32[]{:S(2)}, u32[]{:S(2)}) %collective-permute-start.8) | collective-permute-done | bytes 262176 | tf_op jit(solution)/shard_map/ppermute | solution.py:246
  29.3 0.4 shard_map.70
  29.7 2.8 %collective-permute-start.17 = (f32[8,128]{1,0:T(8,128)S(1)}, f32[8,128]{1,0:T(8,128)S(1)}, u32[]{:S(2)}, u32[]{:S(2)}) collective-permute-start(f32[8,128]{1,0:T(8,128)S(1)} %get-tuple-element.37), channel_id=1, source_target_pairs={{0,2},{1,3},{2,0},{3,1},{4,6},{5,7},{6,4},{7,5},{8,10},{9,11},{10,... | collective-permute-start | bytes 12296 | tf_op jit(solution)/shard_map/ppermute | solution.py:246
  32.5 0.8 %collective-permute-start.16 = (f32[8,128]{1,0:T(8,128)S(1)}, f32[8,128]{1,0:T(8,128)S(1)}, u32[]{:S(2)}, u32[]{:S(2)}) collective-permute-start(f32[8,128]{1,0:T(8,128)S(1)} %get-tuple-element.37), channel_id=1, source_target_pairs={{0,1},{1,0},{2,3},{3,2},{4,5},{5,4},{6,7},{7,6},{8,9},{9,8},{10,11... | collective-permute-start | bytes 12296 | tf_op jit(solution)/shard_map/ppermute | solution.py:246
  33.2 0.8 %collective-permute-done.17 = f32[8,128]{1,0:T(8,128)S(1)} collective-permute-done((f32[8,128]{1,0:T(8,128)S(1)}, f32[8,128]{1,0:T(8,128)S(1)}, u32[]{:S(2)}, u32[]{:S(2)}) %collective-permute-start.17) | collective-permute-done | bytes 4128 | tf_op jit(solution)/shard_map/ppermute | solution.py:246
  34.0 1.0 %collective-permute-start.18 = (f32[8,128]{1,0:T(8,128)S(1)}, f32[8,128]{1,0:T(8,128)S(1)}, u32[]{:S(2)}, u32[]{:S(2)}) collective-permute-start(f32[8,128]{1,0:T(8,128)S(1)} %collective-permute-done.17), channel_id=1, source_target_pairs={{0,1},{1,0},{2,3},{3,2},{4,5},{5,4},{6,7},{7,6},{8,9},{9,8},{10,11... | collective-permute-start | bytes 12296 | tf_op jit(solution)/shard_map/ppermute | solution.py:246
  35.0 1.8 %collective-permute-start.9 = (bf16[128,1024]{1,0:T(8,128)(2,1)S(1)}, bf16[128,1024]{1,0:T(8,128)(2,1)S(1)}, u32[]{:S(2)}, u32[]{:S(2)}) collective-permute-start(bf16[128,1024]{1,0:T(8,128)(2,1)S(1)} %collective-permute-done.5.refs_5_), channel_id=1, source_target_pairs={{0,2},{1,3},{2,0},{3,1},{4,6},{5,7},{6,4},{7,5},{8,10},{9,11},{10,... | collective-permute-start | bytes 786440 | tf_op jit(solution)/shard_map/ppermute | solution.py:246
  36.8 0.8 %collective-permute-done.18 = f32[8,128]{1,0:T(8,128)S(1)} collective-permute-done((f32[8,128]{1,0:T(8,128)S(1)}, f32[8,128]{1,0:T(8,128)S(1)}, u32[]{:S(2)}, u32[]{:S(2)}) %collective-permute-start.18) | collective-permute-done | bytes 4128 | tf_op jit(solution)/shard_map/ppermute | solution.py:246
  37.7 0.5 collective-permute-done.4.refs_0_.refs_8_
  38.2 1.0 %collective-permute-start.19 = (bf16[128,1024]{1,0:T(8,128)(2,1)S(1)}, bf16[128,1024]{1,0:T(8,128)(2,1)S(1)}, u32[]{:S(2)}, u32[]{:S(2)}) collective-permute-start(bf16[128,1024]{1,0:T(8,128)(2,1)S(1)} %collective-permute-done.4.refs_0_.refs_8_), channel_id=1, source_target_pairs={{0,1},{1,0},{2,3},{3,2},{4,5},{5,4},{6,7},{7,6},{8,9},{9,8},{10,11... | collective-permute-start | bytes 786440 | tf_op jit(solution)/shard_map/ppermute | solution.py:246
  39.2 1.3 %collective-permute-start.24 = (f32[4,8,128]{2,1,0:T(8,128)S(1)}, f32[4,8,128]{2,1,0:T(8,128)S(1)}, u32[]{:S(2)}, u32[]{:S(2)}) collective-permute-start(f32[4,8,128]{2,1,0:T(8,128)S(1)} %pad_maximum_fusion.refs_5_.refs_2_), channel_id=1, source_target_pairs={{0,4},{1,5},{2,6},{3,7},{4,8},{5,9},{6,10},{7,11},{8,12},{9,13},{1... | collective-permute-start | bytes 49160 | tf_op jit(solution)/shard_map/ppermute | solution.py:246
  40.5 2.5 %collective-permute-start.26 = (f32[4,8,128]{2,1,0:T(8,128)S(1)}, f32[4,8,128]{2,1,0:T(8,128)S(1)}, u32[]{:S(2)}, u32[]{:S(2)}) collective-permute-start(f32[4,8,128]{2,1,0:T(8,128)S(1)} %pad_maximum_fusion.refs_5_.refs_2_), channel_id=1, source_target_pairs={{0,12},{1,13},{2,14},{3,15},{4,0},{5,1},{6,2},{7,3},{8,4},{9,5},{1... | collective-permute-start | bytes 49160 | tf_op jit(solution)/shard_map/ppermute | solution.py:246
  43.0 1.2 %shard_map.72 = (f32[128,1024]{1,0:T(8,128)S(1)}, bf16[128,1024]{1,0:T(8,128)(2,1)S(1)}) custom-call(f32[128,256]{1,0:T(8,128)S(1)} %get-tuple-element.40.refs_0_, f32[640,256]{1,0:T(8,128)S(1)} %get-tuple-element.41.refs_1_, f32[128,256]{1,0:T(8,128)S(1)} %get-tuple-element.42.refs_2_, f32[16,256]{1,0:T(8,128)S(1)} %get-tuple-element.34.side_ref.refs_1_.refs_3_, ...), custom_call_target="tpu_custom_call" | custom-call | tf_op jit(solution)/shard_map/pallas_call | solution.py:222
  44.3 0.0 collective-permute-done.9.refs_9_
  44.3 0.1 collective-permute-start.22
  44.4 0.5 collective-permute-start.12
  44.9 0.1 collective-permute-start.10
  44.9 0.4 collective-permute-start.20
  45.4 0.1 collective-permute-start.23
  45.5 0.4 collective-permute-done.22.refs_10_
  45.9 0.1 collective-permute-start.25
  46.0 0.2 collective-permute-done.12.refs_3_.refs_11_
  46.3 0.1 collective-permute-start.27
  46.4 1.3 %shard_map.73.refs_1_ = f32[128,1024]{1,0:T(8,128)S(1)} custom-call(bf16[128,1024]{1,0:T(8,128)(2,1)S(1)} %get-tuple-element.25.p_ref.refs_7_.refs_0_, s32[1,256]{1,0:T(1,128)S(1)} %get-tuple-element.39.refs_4_.refs_1_, f32[4,8,128]{2,1,0:T(8,128)S(1)} %pad_maximum_fusion.refs_5_.refs_2_, f32[4,8,128]{2,1,0:T(8,128)S(1)} %collective-permute-done.21.refs_6_.refs_3_, ...), custom_call_target="tpu_custom_call" | custom-call | tf_op jit(solution)/shard_map/pallas_call | solution.py:222
  47.7 0.6 %shard_map.71.refs_0_ = f32[128,768]{1,0:T(8,128)S(1)} custom-call(bf16[128,1024]{1,0:T(8,128)(2,1)S(1)} %get-tuple-element.25.p_ref.refs_7_.refs_0_, bf16[128,1024]{1,0:T(8,128)(2,1)S(1)} %collective-permute-done.4.refs_0_.refs_8_, bf16[128,1024]{1,0:T(8,128)(2,1)S(1)} %collective-permute-done.10.refs_1_.refs_9_, ...), custom_call_target="tpu_custom_call" | custom-call | tf_op jit(solution)/shard_map/pallas_call | solution.py:222
  48.3 1.6 %shard_map.74 = (f32[128,1024]{1,0:T(8,128)}, f32[128,1024]{1,0:T(8,128)}) custom-call(f32[128,768]{1,0:T(8,128)S(1)} %shard_map.71.refs_0_, f32[128,1024]{1,0:T(8,128)S(1)} %shard_map.73.refs_1_, f32[128,1024]{1,0:T(8,128)S(1)} %get-tuple-element.43.refs_2_, bf16[128,1024]{1,0:T(8,128)(2,1)S(1)} %collective-permute-done.23.refs_3_, ...), custom_call_target="tpu_custom_call" | custom-call | tf_op jit(solution)/shard_map/pallas_call | solution.py:222
  (26 shorter events, 0.1 us)
Async XLA Ops:
  0.6 17.3 %copy-start.3 = (s32[1,256]{1,0:T(1,128)S(1)}, s32[1,256]{1,0:T(1,128)}, u32[]{:S(2)}) copy-start(s32[1,256]{1,0:T(1,128)} %refs_2_.1) | copy-start | bytes 3076
  0.6 17.2 %copy-start.2 = (f32[1,256]{1,0:T(1,128)S(1)}, f32[1,256]{1,0:T(1,128)}, u32[]{:S(2)}) copy-start(f32[1,256]{1,0:T(1,128)} %refs_1_.1) | copy-start | bytes 3076
  0.7 17.2 %copy-start.4 = (s32[1,7]{1,0:T(1,128)S(1)}, s32[1,7]{1,0:T(1,128)}, u32[]{:S(2)}) copy-start(s32[1,7]{1,0:T(1,128)} %refs_0_.1) | copy-start | bytes 88
  0.7 10.4 %collective-permute-start.6 = (bf16[128,1024]{1,0:T(8,128)(2,1)}, bf16[128,1024]{1,0:T(8,128)(2,1)S(1)}, u32[]{:S(2)}, u32[]{:S(2)}) collective-permute-start(bf16[128,1024]{1,0:T(8,128)(2,1)} %bitcast.8), channel_id=1, source_target_pairs={{0,2},{1,3},{2,0},{3,1},{4,6},{5,7},{6,4},{7,5},{8,10},{9,11},{10,... | collective-permute-start | bytes 786440 | tf_op jit(solution)/shard_map/ppermute | solution.py:246
  3.7 9.5 %collective-permute-start.2 = (bf16[128,1024]{1,0:T(8,128)(2,1)}, bf16[128,1024]{1,0:T(8,128)(2,1)S(1)}, u32[]{:S(2)}, u32[]{:S(2)}) collective-permute-start(bf16[128,1024]{1,0:T(8,128)(2,1)} %bitcast.9), channel_id=1, source_target_pairs={{0,1},{1,0},{2,3},{3,2},{4,5},{5,4},{6,7},{7,6},{8,9},{9,8},{10,11... | collective-permute-start | bytes 786440 | tf_op jit(solution)/shard_map/ppermute | solution.py:246
  5.2 12.1 %collective-permute-start.5 = (bf16[128,1024]{1,0:T(8,128)(2,1)}, bf16[128,1024]{1,0:T(8,128)(2,1)S(1)}, u32[]{:S(2)}, u32[]{:S(2)}) collective-permute-start(bf16[128,1024]{1,0:T(8,128)(2,1)} %bitcast.11), channel_id=1, source_target_pairs={{0,1},{1,0},{2,3},{3,2},{4,5},{5,4},{6,7},{7,6},{8,9},{9,8},{10,11... | collective-permute-start | bytes 786440 | tf_op jit(solution)/shard_map/ppermute | solution.py:246
  5.7 11.6 %collective-permute-start = (bf16[128,1024]{1,0:T(8,128)(2,1)}, bf16[128,1024]{1,0:T(8,128)(2,1)S(1)}, u32[]{:S(2)}, u32[]{:S(2)}) collective-permute-start(bf16[128,1024]{1,0:T(8,128)(2,1)} %bitcast.12), channel_id=1, source_target_pairs={{0,16},{16,0},{1,17},{17,1},{2,18},{18,2},{3,19},{19,3},{4,20},{20... | collective-permute-start | bytes 786440 | tf_op jit(solution)/shard_map/ppermute | solution.py:249
  5.7 11.9 %collective-permute-start.1 = (bf16[128,1024]{1,0:T(8,128)(2,1)}, bf16[128,1024]{1,0:T(8,128)(2,1)S(1)}, u32[]{:S(2)}, u32[]{:S(2)}) collective-permute-start(bf16[128,1024]{1,0:T(8,128)(2,1)} %bitcast.13), channel_id=1, source_target_pairs={{0,2},{1,3},{2,0},{3,1},{4,6},{5,7},{6,4},{7,5},{8,10},{9,11},{10,... | collective-permute-start | bytes 786440 | tf_op jit(solution)/shard_map/ppermute | solution.py:246
  11.0 11.3 %collective-permute-start.7 = (bf16[128,1024]{1,0:T(8,128)(2,1)S(1)}, bf16[128,1024]{1,0:T(8,128)(2,1)S(1)}, u32[]{:S(2)}, u32[]{:S(2)}) collective-permute-start(bf16[128,1024]{1,0:T(8,128)(2,1)S(1)} %collective-permute-done.6.refs_1_.refs_9_), channel_id=1, source_target_pairs={{0,4},{1,5},{2,14},{3,15},{4,8},{5,9},{6,2},{7,3},{8,12},{9,13},{1... | collective-permute-start | bytes 786440 | tf_op jit(solution)/shard_map/ppermute | solution.py:246
  13.2 12.0 %collective-permute-start.3 = (bf16[128,1024]{1,0:T(8,128)(2,1)S(1)}, bf16[128,1024]{1,0:T(8,128)(2,1)S(1)}, u32[]{:S(2)}, u32[]{:S(2)}) collective-permute-start(bf16[128,1024]{1,0:T(8,128)(2,1)S(1)} %collective-permute-done.2.refs_0_.refs_8_), channel_id=1, source_target_pairs={{0,4},{1,13},{2,6},{3,15},{4,8},{5,1},{6,10},{7,3},{8,12},{9,5},{1... | collective-permute-start | bytes 786440 | tf_op jit(solution)/shard_map/ppermute | solution.py:246
  17.3 7.8 %collective-permute-start.13 = (bf16[128,1024]{1,0:T(8,128)(2,1)S(1)}, bf16[128,1024]{1,0:T(8,128)(2,1)S(1)}, u32[]{:S(2)}, u32[]{:S(2)}) collective-permute-start(bf16[128,1024]{1,0:T(8,128)(2,1)S(1)} %collective-permute-done.5.refs_5_), channel_id=1, source_target_pairs={{0,16},{16,0},{1,17},{17,1},{2,18},{18,2},{3,19},{19,3},{4,20},{20... | collective-permute-start | bytes 786440 | tf_op jit(solution)/shard_map/ppermute | solution.py:249
  17.3 9.1 %collective-permute-start.15 = (bf16[128,1024]{1,0:T(8,128)(2,1)S(1)}, bf16[128,1024]{1,0:T(8,128)(2,1)S(1)}, u32[]{:S(2)}, u32[]{:S(2)}) collective-permute-start(bf16[128,1024]{1,0:T(8,128)(2,1)S(1)} %collective-permute-done.2.refs_0_.refs_8_), channel_id=1, source_target_pairs={{0,2},{1,3},{2,0},{3,1},{4,6},{5,7},{6,4},{7,5},{8,10},{9,11},{10,... | collective-permute-start | bytes 786440 | tf_op jit(solution)/shard_map/ppermute | solution.py:246
  17.7 8.7 %collective-permute-start.14 = (bf16[128,1024]{1,0:T(8,128)(2,1)S(1)}, bf16[128,1024]{1,0:T(8,128)(2,1)S(1)}, u32[]{:S(2)}, u32[]{:S(2)}) collective-permute-start(bf16[128,1024]{1,0:T(8,128)(2,1)S(1)} %collective-permute-done.1.refs_7_), channel_id=1, source_target_pairs={{0,16},{16,0},{1,17},{17,1},{2,18},{18,2},{3,19},{19,3},{4,20},{20... | collective-permute-start | bytes 786440 | tf_op jit(solution)/shard_map/ppermute | solution.py:249
  17.9 1.0 %copy-start = (bf16[1,128,1024]{2,1,0:T(8,128)(2,1)S(1)}, bf16[1,128,1024]{2,1,0:T(8,128)(2,1)}, u32[]{:S(2)}) copy-start(bf16[1,128,1024]{2,1,0:T(8,128)(2,1)} %param.6) | copy-start | bytes 786436
  18.8 0.9 %copy-start.1 = (bf16[1,128,1024]{2,1,0:T(8,128)(2,1)S(1)}, bf16[1,128,1024]{2,1,0:T(8,128)(2,1)}, u32[]{:S(2)}) copy-start(bf16[1,128,1024]{2,1,0:T(8,128)(2,1)} %param.5) | copy-start | bytes 786436
  22.3 7.0 %collective-permute-start.8 = (bf16[128,1024]{1,0:T(8,128)(2,1)S(1)}, bf16[128,1024]{1,0:T(8,128)(2,1)S(1)}, u32[]{:S(2)}, u32[]{:S(2)}) collective-permute-start(bf16[128,1024]{1,0:T(8,128)(2,1)S(1)} %collective-permute-done.7.refs_3_.refs_11_), channel_id=1, source_target_pairs={{0,1},{1,0},{2,3},{3,2},{4,5},{5,4},{6,7},{7,6},{8,9},{9,8},{10,11... | collective-permute-start | bytes 786440 | tf_op jit(solution)/shard_map/ppermute | solution.py:246
  25.1 12.6 %collective-permute-start.11 = (bf16[128,1024]{1,0:T(8,128)(2,1)S(1)}, bf16[128,1024]{1,0:T(8,128)(2,1)S(1)}, u32[]{:S(2)}, u32[]{:S(2)}) collective-permute-start(bf16[128,1024]{1,0:T(8,128)(2,1)S(1)} %collective-permute-done.5.refs_5_), channel_id=1, source_target_pairs={{0,4},{1,13},{2,6},{3,15},{4,8},{5,1},{6,10},{7,3},{8,12},{9,5},{1... | collective-permute-start | bytes 786440 | tf_op jit(solution)/shard_map/ppermute | solution.py:246
  25.1 13.0 %collective-permute-start.4 = (bf16[128,1024]{1,0:T(8,128)(2,1)S(1)}, bf16[128,1024]{1,0:T(8,128)(2,1)S(1)}, u32[]{:S(2)}, u32[]{:S(2)}) collective-permute-start(bf16[128,1024]{1,0:T(8,128)(2,1)S(1)} %collective-permute-done.1.refs_7_), channel_id=1, source_target_pairs={{0,4},{1,5},{2,14},{3,15},{4,8},{5,9},{6,2},{7,3},{8,12},{9,13},{1... | collective-permute-start | bytes 786440 | tf_op jit(solution)/shard_map/ppermute | solution.py:246
  29.7 4.4 %collective-permute-start.17 = (f32[8,128]{1,0:T(8,128)S(1)}, f32[8,128]{1,0:T(8,128)S(1)}, u32[]{:S(2)}, u32[]{:S(2)}) collective-permute-start(f32[8,128]{1,0:T(8,128)S(1)} %get-tuple-element.37), channel_id=1, source_target_pairs={{0,2},{1,3},{2,0},{3,1},{4,6},{5,7},{6,4},{7,5},{8,10},{9,11},{10,... | collective-permute-start | bytes 12296 | tf_op jit(solution)/shard_map/ppermute | solution.py:246
  32.5 4.4 %collective-permute-start.16 = (f32[8,128]{1,0:T(8,128)S(1)}, f32[8,128]{1,0:T(8,128)S(1)}, u32[]{:S(2)}, u32[]{:S(2)}) collective-permute-start(f32[8,128]{1,0:T(8,128)S(1)} %get-tuple-element.37), channel_id=1, source_target_pairs={{0,1},{1,0},{2,3},{3,2},{4,5},{5,4},{6,7},{7,6},{8,9},{9,8},{10,11... | collective-permute-start | bytes 12296 | tf_op jit(solution)/shard_map/ppermute | solution.py:246
  34.0 3.6 %collective-permute-start.18 = (f32[8,128]{1,0:T(8,128)S(1)}, f32[8,128]{1,0:T(8,128)S(1)}, u32[]{:S(2)}, u32[]{:S(2)}) collective-permute-start(f32[8,128]{1,0:T(8,128)S(1)} %collective-permute-done.17), channel_id=1, source_target_pairs={{0,1},{1,0},{2,3},{3,2},{4,5},{5,4},{6,7},{7,6},{8,9},{9,8},{10,11... | collective-permute-start | bytes 12296 | tf_op jit(solution)/shard_map/ppermute | solution.py:246
  35.0 9.3 %collective-permute-start.9 = (bf16[128,1024]{1,0:T(8,128)(2,1)S(1)}, bf16[128,1024]{1,0:T(8,128)(2,1)S(1)}, u32[]{:S(2)}, u32[]{:S(2)}) collective-permute-start(bf16[128,1024]{1,0:T(8,128)(2,1)S(1)} %collective-permute-done.5.refs_5_), channel_id=1, source_target_pairs={{0,2},{1,3},{2,0},{3,1},{4,6},{5,7},{6,4},{7,5},{8,10},{9,11},{10,... | collective-permute-start | bytes 786440 | tf_op jit(solution)/shard_map/ppermute | solution.py:246
  38.2 6.8 %collective-permute-start.19 = (bf16[128,1024]{1,0:T(8,128)(2,1)S(1)}, bf16[128,1024]{1,0:T(8,128)(2,1)S(1)}, u32[]{:S(2)}, u32[]{:S(2)}) collective-permute-start(bf16[128,1024]{1,0:T(8,128)(2,1)S(1)} %collective-permute-done.4.refs_0_.refs_8_), channel_id=1, source_target_pairs={{0,1},{1,0},{2,3},{3,2},{4,5},{5,4},{6,7},{7,6},{8,9},{9,8},{10,11... | collective-permute-start | bytes 786440 | tf_op jit(solution)/shard_map/ppermute | solution.py:246
  39.2 3.8 %collective-permute-start.21 = (f32[4,8,128]{2,1,0:T(8,128)S(1)}, f32[4,8,128]{2,1,0:T(8,128)S(1)}, u32[]{:S(2)}, u32[]{:S(2)}) collective-permute-start(f32[4,8,128]{2,1,0:T(8,128)S(1)} %pad_maximum_fusion.refs_5_.refs_2_), channel_id=1, source_target_pairs={{0,16},{16,0},{1,17},{17,1},{2,18},{18,2},{3,19},{19,3},{4,20},{20... | collective-permute-start | bytes 49160 | tf_op jit(solution)/shard_map/ppermute | solution.py:249
  39.2 5.7 %collective-permute-start.24 = (f32[4,8,128]{2,1,0:T(8,128)S(1)}, f32[4,8,128]{2,1,0:T(8,128)S(1)}, u32[]{:S(2)}, u32[]{:S(2)}) collective-permute-start(f32[4,8,128]{2,1,0:T(8,128)S(1)} %pad_maximum_fusion.refs_5_.refs_2_), channel_id=1, source_target_pairs={{0,4},{1,5},{2,6},{3,7},{4,8},{5,9},{6,10},{7,11},{8,12},{9,13},{1... | collective-permute-start | bytes 49160 | tf_op jit(solution)/shard_map/ppermute | solution.py:246
  40.5 4.9 %collective-permute-start.26 = (f32[4,8,128]{2,1,0:T(8,128)S(1)}, f32[4,8,128]{2,1,0:T(8,128)S(1)}, u32[]{:S(2)}, u32[]{:S(2)}) collective-permute-start(f32[4,8,128]{2,1,0:T(8,128)S(1)} %pad_maximum_fusion.refs_5_.refs_2_), channel_id=1, source_target_pairs={{0,12},{1,13},{2,14},{3,15},{4,0},{5,1},{6,2},{7,3},{8,4},{9,5},{1... | collective-permute-start | bytes 49160 | tf_op jit(solution)/shard_map/ppermute | solution.py:246
  44.3 1.6 %collective-permute-start.22 = (bf16[128,1024]{1,0:T(8,128)(2,1)S(1)}, bf16[128,1024]{1,0:T(8,128)(2,1)S(1)}, u32[]{:S(2)}, u32[]{:S(2)}) collective-permute-start(bf16[128,1024]{1,0:T(8,128)(2,1)S(1)} %collective-permute-done.9.refs_9_), channel_id=1, source_target_pairs={{0,16},{16,0},{1,17},{17,1},{2,18},{18,2},{3,19},{19,3},{4,20},{20... | collective-permute-start | bytes 786440 | tf_op jit(solution)/shard_map/ppermute | solution.py:249
  44.4 1.9 %collective-permute-start.12 = (bf16[128,1024]{1,0:T(8,128)(2,1)S(1)}, bf16[128,1024]{1,0:T(8,128)(2,1)S(1)}, u32[]{:S(2)}, u32[]{:S(2)}) collective-permute-start(bf16[128,1024]{1,0:T(8,128)(2,1)S(1)} %collective-permute-done.11.refs_2_.refs_10_), channel_id=1, source_target_pairs={{0,16},{16,0},{1,17},{17,1},{2,18},{18,2},{3,19},{19,3},{4,20},{20... | collective-permute-start | bytes 786440 | tf_op jit(solution)/shard_map/ppermute | solution.py:249
  44.9 2.8 %collective-permute-start.10 = (bf16[128,1024]{1,0:T(8,128)(2,1)S(1)}, bf16[128,1024]{1,0:T(8,128)(2,1)S(1)}, u32[]{:S(2)}, u32[]{:S(2)}) collective-permute-start(bf16[128,1024]{1,0:T(8,128)(2,1)S(1)} %collective-permute-done.4.refs_0_.refs_8_), channel_id=1, source_target_pairs={{0,16},{16,0},{1,17},{17,1},{2,18},{18,2},{3,19},{19,3},{4,20},{20... | collective-permute-start | bytes 786440 | tf_op jit(solution)/shard_map/ppermute | solution.py:249
  44.9 2.7 %collective-permute-start.20 = (bf16[128,1024]{1,0:T(8,128)(2,1)S(1)}, bf16[128,1024]{1,0:T(8,128)(2,1)S(1)}, u32[]{:S(2)}, u32[]{:S(2)}) collective-permute-start(bf16[128,1024]{1,0:T(8,128)(2,1)S(1)} %collective-permute-done.19.refs_4_.refs_12_), channel_id=1, source_target_pairs={{0,16},{16,0},{1,17},{17,1},{2,18},{18,2},{3,19},{19,3},{4,20},{20... | collective-permute-start | bytes 786440 | tf_op jit(solution)/shard_map/ppermute | solution.py:249
  45.4 2.9 %collective-permute-start.23 = (bf16[128,1024]{1,0:T(8,128)(2,1)S(1)}, bf16[128,1024]{1,0:T(8,128)(2,1)S(1)}, u32[]{:S(2)}, u32[]{:S(2)}) collective-permute-start(bf16[128,1024]{1,0:T(8,128)(2,1)S(1)} %get-tuple-element.45), channel_id=1, source_target_pairs={{0,16},{16,0},{1,17},{17,1},{2,18},{18,2},{3,19},{19,3},{4,20},{20... | collective-permute-start | bytes 786440 | tf_op jit(solution)/shard_map/ppermute | solution.py:249
  45.9 2.4 %collective-permute-start.25 = (f32[4,8,128]{2,1,0:T(8,128)S(1)}, f32[4,8,128]{2,1,0:T(8,128)S(1)}, u32[]{:S(2)}, u32[]{:S(2)}) collective-permute-start(f32[4,8,128]{2,1,0:T(8,128)S(1)} %collective-permute-done.24.refs_4_), channel_id=1, source_target_pairs={{0,16},{16,0},{1,17},{17,1},{2,18},{18,2},{3,19},{19,3},{4,20},{20... | collective-permute-start | bytes 49160 | tf_op jit(solution)/shard_map/ppermute | solution.py:249
  46.3 2.0 %collective-permute-start.27 = (f32[4,8,128]{2,1,0:T(8,128)S(1)}, f32[4,8,128]{2,1,0:T(8,128)S(1)}, u32[]{:S(2)}, u32[]{:S(2)}) collective-permute-start(f32[4,8,128]{2,1,0:T(8,128)S(1)} %collective-permute-done.26.refs_6_), channel_id=1, source_target_pairs={{0,16},{16,0},{1,17},{17,1},{2,18},{18,2},{3,19},{19,3},{4,20},{20... | collective-permute-start | bytes 49160 | tf_op jit(solution)/shard_map/ppermute | solution.py:249

commit v6 on v5

--- a/solution.py
+++ b/solution.py
@@ -199,31 +199,43 @@
 
 def far_kernel(pb, s_ref, near_ref, *refs):
     grad_refs, up, down = refs[:pb], refs[pb : 2 * pb], refs[2 * pb : 3 * pb]
-    q_refs, (out_ref, query_ref), keep = refs[3 * pb : 6 * pb], refs[6 * pb : 6 * pb + 2], refs[6 * pb + 2 :]
+    q_refs, (out_hbm, query_hbm), refs = refs[3 * pb : 6 * pb], refs[6 * pb : 6 * pb + 2], refs[6 * pb + 2 :]
+    keep, (out_ref, query_ref, sems) = refs[:2], refs[2:]
     rows = out_ref.shape[0]
+    grad = grad_refs[0][...]
+    for ref in grad_refs[1:]:
+        grad = grad + ref[...].astype(F32)
+    query_ref[...] = grad
+    first = pltpu.make_async_copy(query_ref, query_hbm, sems.at[0])
+    first.start()
     home, me = lax.axis_index("pa"), lax.axis_index("pb")
     y_low, x_low = (home & 2) == 0, (home & 1) == 0
     stats = []
     for k, low in ((2, y_low), (1, x_low), (3, y_low)):
         stats.append([jnp.where(low, up[c][k], down[c][k]) for c in range(pb)])
     orders = [(me - r + pb) % pb for _ in range(3) for r in range(pb)]
-    out_ref[...] = add_blocks(
-        pb, stats, lambda n: s_ref[:, n * rows : (n + 1) * rows], q_refs, orders, keep, {}, near_ref[...]
-    )
-    grad = grad_refs[0][...]
-    for ref in grad_refs[1:]:
-        grad = grad + ref[...].astype(F32)
-    query_ref[...] = grad
+    half = rows // 2
+    copies = [first]
+    for h in range(2):
+        part = slice(h * half, (h + 1) * half)
+        out_ref[part, :] = add_blocks(
+            pb, stats, lambda n: s_ref[part, n * rows : (n + 1) * rows], q_refs, orders, keep, {}, near_ref[part, :]
+        )
+        copy = pltpu.make_async_copy(out_ref.at[part, :], out_hbm.at[part, :], sems.at[1 + h])
+        copy.start()
+        copies.append(copy)
+    for copy in copies:
+        copy.wait()
 
 VMEM = pl.BlockSpec(memory_space=pltpu.VMEM)
 SMEM = pl.BlockSpec(memory_space=pltpu.SMEM)
 
-def call(kernel, outs, args, flops, smem=0, scratch=()):
+def call(kernel, outs, args, flops, smem=0, scratch=(), placed=VMEM):
     return pl.pallas_call(
         kernel,
         out_shape=outs,
         in_specs=[SMEM] * smem + [VMEM] * (len(args) - smem),
-        out_specs=[VMEM] * len(outs),
+        out_specs=[placed] * len(outs),
         scratch_shapes=list(scratch),
         cost_estimate=pl.CostEstimate(flops=0, bytes_accessed=0, transcendentals=0),
         compiler_params=pltpu.CompilerParams(vmem_limit_bytes=24 * 1024 * 1024),
@@ -320,7 +332,13 @@
         [shape((rows, width), F32)] * 2,
         [cross, near, parts[0], *arrived, up, *others(up), down, *others(down), *far_q],
         3 * flops,
-        scratch=keep(3),
+        scratch=[
+            *keep(3),
+            pltpu.VMEM((rows, width), F32),
+            pltpu.VMEM((rows, width), F32),
+            pltpu.SemaphoreType.DMA((3,)),
+        ],
+        placed=pl.BlockSpec(memory_space=pl.ANY),
     )
     return (query_grad[None], passage_grad[None])
 

time: 50.1 us -> 50 us (level)
  no operation moved by 1% of the time
where the time goes in v6:
time: 50 us; the launch traced here: 49.9 us
  starting transfers between devices  24.9 us (50%)
  waiting for transfers between devices  15.3 us (31%)
  Pallas kernels  7.06 us (14%)
  local copies, waits for them, and re-layouts  1.91 us (4%)
  between operations  0.78 us (2%)
    ppermute x17, starting transfers between devices, move(): return lax.ppermute(value, 'pa', tables[name])  23.2 us
    ppermute x17, waiting for transfers between devices, move(): return lax.ppermute(value, 'pa', tables[name])  14.6 us
    pallas_call x7, Pallas kernels, call(): pl.pallas_call(kernel, out_shape=outs, in_specs=[SMEM] * smem + [VMEM] *...  7.06 us
    unnamed x10, local copies, waits for them, and re-layouts  1.91 us
    ppermute x11, starting transfers between devices, from_member(): return lax.ppermute(value, 'pb', [(i, (i + r) % pb) for i in range(pb)])  1.67 us
  transfers between devices with their start and end apart: 28, of which 10 were waited for; matrix products, arithmetic and copies ran while one was open for 0% of the time, Pallas kernels for 11%

profile of v6, /device:TPU:0, one launch (start us, length us, event | category | flops | bytes accessed | tf_op | source)
XLA Modules:
  0.0 49.9 jit_solution(13649323852640998054)
XLA Ops:
  0.7 3.0 %collective-permute-start.6 = (bf16[128,1024]{1,0:T(8,128)(2,1)}, bf16[128,1024]{1,0:T(8,128)(2,1)S(1)}, u32[]{:S(2)}, u32[]{:S(2)}) collective-permute-start(bf16[128,1024]{1,0:T(8,128)(2,1)} %bitcast.8), channel_id=1, source_target_pairs={{0,2},{1,3},{2,0},{3,1},{4,6},{5,7},{6,4},{7,5},{8,10},{9,11},{10,... | collective-permute-start | bytes 786440 | tf_op jit(solution)/shard_map/ppermute | solution.py:258
  3.7 1.5 %collective-permute-start.2 = (bf16[128,1024]{1,0:T(8,128)(2,1)}, bf16[128,1024]{1,0:T(8,128)(2,1)S(1)}, u32[]{:S(2)}, u32[]{:S(2)}) collective-permute-start(bf16[128,1024]{1,0:T(8,128)(2,1)} %bitcast.9), channel_id=1, source_target_pairs={{0,1},{1,0},{2,3},{3,2},{4,5},{5,4},{6,7},{7,6},{8,9},{9,8},{10,11... | collective-permute-start | bytes 786440 | tf_op jit(solution)/shard_map/ppermute | solution.py:258
  5.2 0.5 %collective-permute-start.5 = (bf16[128,1024]{1,0:T(8,128)(2,1)}, bf16[128,1024]{1,0:T(8,128)(2,1)S(1)}, u32[]{:S(2)}, u32[]{:S(2)}) collective-permute-start(bf16[128,1024]{1,0:T(8,128)(2,1)} %bitcast.11), channel_id=1, source_target_pairs={{0,1},{1,0},{2,3},{3,2},{4,5},{5,4},{6,7},{7,6},{8,9},{9,8},{10,11... | collective-permute-start | bytes 786440 | tf_op jit(solution)/shard_map/ppermute | solution.py:258
  5.7 0.0 collective-permute-start
  5.7 0.1 collective-permute-start.1
  5.8 5.2 %collective-permute-done.6.refs_1_.refs_9_ = bf16[128,1024]{1,0:T(8,128)(2,1)S(1)} collective-permute-done((bf16[128,1024]{1,0:T(8,128)(2,1)}, bf16[128,1024]{1,0:T(8,128)(2,1)S(1)}, u32[]{:S(2)}, u32[]{:S(2)}) %collective-permute-start.6) | collective-permute-done | bytes 262176 | tf_op jit(solution)/shard_map/ppermute | solution.py:258
  11.0 2.1 %collective-permute-start.7 = (bf16[128,1024]{1,0:T(8,128)(2,1)S(1)}, bf16[128,1024]{1,0:T(8,128)(2,1)S(1)}, u32[]{:S(2)}, u32[]{:S(2)}) collective-permute-start(bf16[128,1024]{1,0:T(8,128)(2,1)S(1)} %collective-permute-done.6.refs_1_.refs_9_), channel_id=1, source_target_pairs={{0,4},{1,5},{2,14},{3,15},{4,8},{5,9},{6,2},{7,3},{8,12},{9,13},{1... | collective-permute-start | bytes 786440 | tf_op jit(solution)/shard_map/ppermute | solution.py:258
  13.2 0.0 collective-permute-done.2.refs_0_.refs_8_
  13.2 1.6 %collective-permute-start.3 = (bf16[128,1024]{1,0:T(8,128)(2,1)S(1)}, bf16[128,1024]{1,0:T(8,128)(2,1)S(1)}, u32[]{:S(2)}, u32[]{:S(2)}) collective-permute-start(bf16[128,1024]{1,0:T(8,128)(2,1)S(1)} %collective-permute-done.2.refs_0_.refs_8_), channel_id=1, source_target_pairs={{0,4},{1,13},{2,6},{3,15},{4,8},{5,1},{6,10},{7,3},{8,12},{9,5},{1... | collective-permute-start | bytes 786440 | tf_op jit(solution)/shard_map/ppermute | solution.py:258
  14.7 2.6 %collective-permute-done.5.refs_5_ = bf16[128,1024]{1,0:T(8,128)(2,1)S(1)} collective-permute-done((bf16[128,1024]{1,0:T(8,128)(2,1)}, bf16[128,1024]{1,0:T(8,128)(2,1)S(1)}, u32[]{:S(2)}, u32[]{:S(2)}) %collective-permute-start.5) | collective-permute-done | bytes 262176 | tf_op jit(solution)/shard_map/ppermute | solution.py:258
  17.3 0.4 collective-permute-start.15
  17.7 0.2 collective-permute-start.14
  17.9 0.9 %copy-done = bf16[1,128,1024]{2,1,0:T(8,128)(2,1)S(1)} copy-done((bf16[1,128,1024]{2,1,0:T(8,128)(2,1)S(1)}, bf16[1,128,1024]{2,1,0:T(8,128)(2,1)}, u32[]{:S(2)}) %copy-start) | copy-done | bytes 262168
  18.8 0.9 %copy-done.1 = bf16[1,128,1024]{2,1,0:T(8,128)(2,1)S(1)} copy-done((bf16[1,128,1024]{2,1,0:T(8,128)(2,1)S(1)}, bf16[1,128,1024]{2,1,0:T(8,128)(2,1)}, u32[]{:S(2)}) %copy-start.1) | copy-done | bytes 262168
  19.8 0.9 %shard_map.68 = (f32[128,256]{1,0:T(8,128)S(1)}, f32[8,256]{1,0:T(8,128)S(1)}, bf16[256,1024]{1,0:T(8,128)(2,1)S(1)}, bf16[128,1024]{1,0:T(8,128)(2,1)S(1)}, f32...) custom-call(s32[1,7]{1,0:T(1,128)S(1)} %copy-done.4, f32[1,256]{1,0:T(1,128)S(1)} %copy-done.2, s32[1,256]{1,0:T(1,128)S(1)} %copy-done.3, ...), custom_call_target="tpu_custom_call" | custom-call | tf_op jit(solution)/shard_map/pallas_call | solution.py:234
  20.7 1.6 %collective-permute-done.7.refs_3_.refs_11_ = bf16[128,1024]{1,0:T(8,128)(2,1)S(1)} collective-permute-done((bf16[128,1024]{1,0:T(8,128)(2,1)S(1)}, bf16[128,1024]{1,0:T(8,128)(2,1)S(1)}, u32[]{:S(2)}, u32[]{:S(2)}) %collective-permute-start.7) | collective-permute-done | bytes 262176 | tf_op jit(solution)/shard_map/ppermute | solution.py:258
  22.3 1.5 %collective-permute-start.8 = (bf16[128,1024]{1,0:T(8,128)(2,1)S(1)}, bf16[128,1024]{1,0:T(8,128)(2,1)S(1)}, u32[]{:S(2)}, u32[]{:S(2)}) collective-permute-start(bf16[128,1024]{1,0:T(8,128)(2,1)S(1)} %collective-permute-done.7.refs_3_.refs_11_), channel_id=1, source_target_pairs={{0,1},{1,0},{2,3},{3,2},{4,5},{5,4},{6,7},{7,6},{8,9},{9,8},{10,11... | collective-permute-start | bytes 786440 | tf_op jit(solution)/shard_map/ppermute | solution.py:258
  23.8 1.3 %collective-permute-done.3.refs_4_.refs_12_ = bf16[128,1024]{1,0:T(8,128)(2,1)S(1)} collective-permute-done((bf16[128,1024]{1,0:T(8,128)(2,1)S(1)}, bf16[128,1024]{1,0:T(8,128)(2,1)S(1)}, u32[]{:S(2)}, u32[]{:S(2)}) %collective-permute-start.3) | collective-permute-done | bytes 262176 | tf_op jit(solution)/shard_map/ppermute | solution.py:258
  25.1 1.3 %collective-permute-start.4 = (bf16[128,1024]{1,0:T(8,128)(2,1)S(1)}, bf16[128,1024]{1,0:T(8,128)(2,1)S(1)}, u32[]{:S(2)}, u32[]{:S(2)}) collective-permute-start(bf16[128,1024]{1,0:T(8,128)(2,1)S(1)} %collective-permute-done.1.refs_7_), channel_id=1, source_target_pairs={{0,4},{1,5},{2,14},{3,15},{4,8},{5,9},{6,2},{7,3},{8,12},{9,13},{1... | collective-permute-start | bytes 786440 | tf_op jit(solution)/shard_map/ppermute | solution.py:258
  26.4 0.0 collective-permute-done.14.refs_8_
  26.4 0.0 collective-permute-done.15.refs_2_.refs_10_
  26.4 1.1 %shard_map.69 = (f32[640,256]{1,0:T(8,128)S(1)}, f32[8,256]{1,0:T(8,128)S(1)}) custom-call(bf16[256,1024]{1,0:T(8,128)(2,1)S(1)} %get-tuple-element.33.full_ref.refs_0_.refs_4_, f32[16,256]{1,0:T(8,128)S(1)} %get-tuple-element.34.side_ref.refs_1_.refs_3_, f32[8,256]{1,0:T(8,128)S(1)} %get-tuple-element.35.before_ref, ...), custom_call_target="tpu_custom_call" | custom-call | tf_op jit(solution)/shard_map/pallas_call | solution.py:234
  27.5 1.8 %collective-permute-done.8.refs_3_.refs_13_ = bf16[128,1024]{1,0:T(8,128)(2,1)S(1)} collective-permute-done((bf16[128,1024]{1,0:T(8,128)(2,1)S(1)}, bf16[128,1024]{1,0:T(8,128)(2,1)S(1)}, u32[]{:S(2)}, u32[]{:S(2)}) %collective-permute-start.8) | collective-permute-done | bytes 262176 | tf_op jit(solution)/shard_map/ppermute | solution.py:258
  29.3 0.4 shard_map.70
  29.7 2.8 %collective-permute-start.17 = (f32[8,128]{1,0:T(8,128)S(1)}, f32[8,128]{1,0:T(8,128)S(1)}, u32[]{:S(2)}, u32[]{:S(2)}) collective-permute-start(f32[8,128]{1,0:T(8,128)S(1)} %get-tuple-element.37), channel_id=1, source_target_pairs={{0,2},{1,3},{2,0},{3,1},{4,6},{5,7},{6,4},{7,5},{8,10},{9,11},{10,... | collective-permute-start | bytes 12296 | tf_op jit(solution)/shard_map/ppermute | solution.py:258
  32.5 0.8 %collective-permute-start.16 = (f32[8,128]{1,0:T(8,128)S(1)}, f32[8,128]{1,0:T(8,128)S(1)}, u32[]{:S(2)}, u32[]{:S(2)}) collective-permute-start(f32[8,128]{1,0:T(8,128)S(1)} %get-tuple-element.37), channel_id=1, source_target_pairs={{0,1},{1,0},{2,3},{3,2},{4,5},{5,4},{6,7},{7,6},{8,9},{9,8},{10,11... | collective-permute-start | bytes 12296 | tf_op jit(solution)/shard_map/ppermute | solution.py:258
  33.2 0.8 %collective-permute-done.17 = f32[8,128]{1,0:T(8,128)S(1)} collective-permute-done((f32[8,128]{1,0:T(8,128)S(1)}, f32[8,128]{1,0:T(8,128)S(1)}, u32[]{:S(2)}, u32[]{:S(2)}) %collective-permute-start.17) | collective-permute-done | bytes 4128 | tf_op jit(solution)/shard_map/ppermute | solution.py:258
  34.0 1.0 %collective-permute-start.18 = (f32[8,128]{1,0:T(8,128)S(1)}, f32[8,128]{1,0:T(8,128)S(1)}, u32[]{:S(2)}, u32[]{:S(2)}) collective-permute-start(f32[8,128]{1,0:T(8,128)S(1)} %collective-permute-done.17), channel_id=1, source_target_pairs={{0,1},{1,0},{2,3},{3,2},{4,5},{5,4},{6,7},{7,6},{8,9},{9,8},{10,11... | collective-permute-start | bytes 12296 | tf_op jit(solution)/shard_map/ppermute | solution.py:258
  35.0 1.8 %collective-permute-start.9 = (bf16[128,1024]{1,0:T(8,128)(2,1)S(1)}, bf16[128,1024]{1,0:T(8,128)(2,1)S(1)}, u32[]{:S(2)}, u32[]{:S(2)}) collective-permute-start(bf16[128,1024]{1,0:T(8,128)(2,1)S(1)} %collective-permute-done.5.refs_5_), channel_id=1, source_target_pairs={{0,2},{1,3},{2,0},{3,1},{4,6},{5,7},{6,4},{7,5},{8,10},{9,11},{10,... | collective-permute-start | bytes 786440 | tf_op jit(solution)/shard_map/ppermute | solution.py:258
  36.8 0.0 collective-permute-done.16
  36.8 0.8 %collective-permute-done.18 = f32[8,128]{1,0:T(8,128)S(1)} collective-permute-done((f32[8,128]{1,0:T(8,128)S(1)}, f32[8,128]{1,0:T(8,128)S(1)}, u32[]{:S(2)}, u32[]{:S(2)}) %collective-permute-start.18) | collective-permute-done | bytes 4128 | tf_op jit(solution)/shard_map/ppermute | solution.py:258
  37.7 0.5 collective-permute-done.4.refs_0_.refs_8_
  38.2 1.0 %collective-permute-start.19 = (bf16[128,1024]{1,0:T(8,128)(2,1)S(1)}, bf16[128,1024]{1,0:T(8,128)(2,1)S(1)}, u32[]{:S(2)}, u32[]{:S(2)}) collective-permute-start(bf16[128,1024]{1,0:T(8,128)(2,1)S(1)} %collective-permute-done.4.refs_0_.refs_8_), channel_id=1, source_target_pairs={{0,1},{1,0},{2,3},{3,2},{4,5},{5,4},{6,7},{7,6},{8,9},{9,8},{10,11... | collective-permute-start | bytes 786440 | tf_op jit(solution)/shard_map/ppermute | solution.py:258
  39.2 1.3 %collective-permute-start.24 = (f32[4,8,128]{2,1,0:T(8,128)S(1)}, f32[4,8,128]{2,1,0:T(8,128)S(1)}, u32[]{:S(2)}, u32[]{:S(2)}) collective-permute-start(f32[4,8,128]{2,1,0:T(8,128)S(1)} %pad_maximum_fusion.refs_5_.refs_2_), channel_id=1, source_target_pairs={{0,4},{1,5},{2,6},{3,7},{4,8},{5,9},{6,10},{7,11},{8,12},{9,13},{1... | collective-permute-start | bytes 49160 | tf_op jit(solution)/shard_map/ppermute | solution.py:258
  40.5 2.5 %collective-permute-start.26 = (f32[4,8,128]{2,1,0:T(8,128)S(1)}, f32[4,8,128]{2,1,0:T(8,128)S(1)}, u32[]{:S(2)}, u32[]{:S(2)}) collective-permute-start(f32[4,8,128]{2,1,0:T(8,128)S(1)} %pad_maximum_fusion.refs_5_.refs_2_), channel_id=1, source_target_pairs={{0,12},{1,13},{2,14},{3,15},{4,0},{5,1},{6,2},{7,3},{8,4},{9,5},{1... | collective-permute-start | bytes 49160 | tf_op jit(solution)/shard_map/ppermute | solution.py:258
  43.0 1.2 %shard_map.72 = (f32[128,1024]{1,0:T(8,128)S(1)}, bf16[128,1024]{1,0:T(8,128)(2,1)S(1)}) custom-call(f32[128,256]{1,0:T(8,128)S(1)} %get-tuple-element.40.refs_0_, f32[640,256]{1,0:T(8,128)S(1)} %get-tuple-element.41.refs_1_, f32[128,256]{1,0:T(8,128)S(1)} %get-tuple-element.42.refs_2_, f32[16,256]{1,0:T(8,128)S(1)} %get-tuple-element.34.side_ref.refs_1_.refs_3_, ...), custom_call_target="tpu_custom_call" | custom-call | tf_op jit(solution)/shard_map/pallas_call | solution.py:234
  44.3 0.1 collective-permute-start.22
  44.4 0.5 collective-permute-start.12
  44.9 0.1 collective-permute-start.10
  44.9 0.4 collective-permute-start.20
  45.4 0.1 collective-permute-start.23
  45.5 0.4 collective-permute-done.22.refs_10_
  45.9 0.1 collective-permute-start.25
  46.0 0.2 collective-permute-done.12.refs_3_.refs_11_
  46.3 0.1 collective-permute-start.27
  46.4 1.3 %shard_map.73.refs_1_ = f32[128,1024]{1,0:T(8,128)S(1)} custom-call(bf16[128,1024]{1,0:T(8,128)(2,1)S(1)} %get-tuple-element.25.p_ref.refs_7_.refs_0_, s32[1,256]{1,0:T(1,128)S(1)} %get-tuple-element.39.refs_4_.refs_1_, f32[4,8,128]{2,1,0:T(8,128)S(1)} %pad_maximum_fusion.refs_5_.refs_2_, f32[4,8,128]{2,1,0:T(8,128)S(1)} %collective-permute-done.21.refs_6_.refs_3_, ...), custom_call_target="tpu_custom_call" | custom-call | tf_op jit(solution)/shard_map/pallas_call | solution.py:234
  47.7 0.6 %shard_map.71.refs_0_ = f32[128,768]{1,0:T(8,128)S(1)} custom-call(bf16[128,1024]{1,0:T(8,128)(2,1)S(1)} %get-tuple-element.25.p_ref.refs_7_.refs_0_, bf16[128,1024]{1,0:T(8,128)(2,1)S(1)} %collective-permute-done.4.refs_0_.refs_8_, bf16[128,1024]{1,0:T(8,128)(2,1)S(1)} %collective-permute-done.10.refs_1_.refs_9_, ...), custom_call_target="tpu_custom_call" | custom-call | tf_op jit(solution)/shard_map/pallas_call | solution.py:234
  48.3 1.6 %shard_map.74 = (f32[128,1024]{1,0:T(8,128)}, f32[128,1024]{1,0:T(8,128)}) custom-call(f32[128,768]{1,0:T(8,128)S(1)} %shard_map.71.refs_0_, f32[128,1024]{1,0:T(8,128)S(1)} %shard_map.73.refs_1_, f32[128,1024]{1,0:T(8,128)S(1)} %get-tuple-element.43.refs_2_, bf16[128,1024]{1,0:T(8,128)(2,1)S(1)} %collective-permute-done.23.refs_3_, ...), custom_call_target="tpu_custom_call" | custom-call | tf_op jit(solution)/shard_map/pallas_call | solution.py:234
  (26 shorter events, 0.1 us)
Async XLA Ops:
  0.6 17.3 %copy-start.3 = (s32[1,256]{1,0:T(1,128)S(1)}, s32[1,256]{1,0:T(1,128)}, u32[]{:S(2)}) copy-start(s32[1,256]{1,0:T(1,128)} %refs_2_.1) | copy-start | bytes 3076
  0.6 17.2 %copy-start.2 = (f32[1,256]{1,0:T(1,128)S(1)}, f32[1,256]{1,0:T(1,128)}, u32[]{:S(2)}) copy-start(f32[1,256]{1,0:T(1,128)} %refs_1_.1) | copy-start | bytes 3076
  0.7 17.2 %copy-start.4 = (s32[1,7]{1,0:T(1,128)S(1)}, s32[1,7]{1,0:T(1,128)}, u32[]{:S(2)}) copy-start(s32[1,7]{1,0:T(1,128)} %refs_0_.1) | copy-start | bytes 88
  0.7 10.4 %collective-permute-start.6 = (bf16[128,1024]{1,0:T(8,128)(2,1)}, bf16[128,1024]{1,0:T(8,128)(2,1)S(1)}, u32[]{:S(2)}, u32[]{:S(2)}) collective-permute-start(bf16[128,1024]{1,0:T(8,128)(2,1)} %bitcast.8), channel_id=1, source_target_pairs={{0,2},{1,3},{2,0},{3,1},{4,6},{5,7},{6,4},{7,5},{8,10},{9,11},{10,... | collective-permute-start | bytes 786440 | tf_op jit(solution)/shard_map/ppermute | solution.py:258
  3.7 9.5 %collective-permute-start.2 = (bf16[128,1024]{1,0:T(8,128)(2,1)}, bf16[128,1024]{1,0:T(8,128)(2,1)S(1)}, u32[]{:S(2)}, u32[]{:S(2)}) collective-permute-start(bf16[128,1024]{1,0:T(8,128)(2,1)} %bitcast.9), channel_id=1, source_target_pairs={{0,1},{1,0},{2,3},{3,2},{4,5},{5,4},{6,7},{7,6},{8,9},{9,8},{10,11... | collective-permute-start | bytes 786440 | tf_op jit(solution)/shard_map/ppermute | solution.py:258
  5.2 12.1 %collective-permute-start.5 = (bf16[128,1024]{1,0:T(8,128)(2,1)}, bf16[128,1024]{1,0:T(8,128)(2,1)S(1)}, u32[]{:S(2)}, u32[]{:S(2)}) collective-permute-start(bf16[128,1024]{1,0:T(8,128)(2,1)} %bitcast.11), channel_id=1, source_target_pairs={{0,1},{1,0},{2,3},{3,2},{4,5},{5,4},{6,7},{7,6},{8,9},{9,8},{10,11... | collective-permute-start | bytes 786440 | tf_op jit(solution)/shard_map/ppermute | solution.py:258
  5.7 11.6 %collective-permute-start = (bf16[128,1024]{1,0:T(8,128)(2,1)}, bf16[128,1024]{1,0:T(8,128)(2,1)S(1)}, u32[]{:S(2)}, u32[]{:S(2)}) collective-permute-start(bf16[128,1024]{1,0:T(8,128)(2,1)} %bitcast.12), channel_id=1, source_target_pairs={{0,16},{16,0},{1,17},{17,1},{2,18},{18,2},{3,19},{19,3},{4,20},{20... | collective-permute-start | bytes 786440 | tf_op jit(solution)/shard_map/ppermute | solution.py:261
  5.7 11.9 %collective-permute-start.1 = (bf16[128,1024]{1,0:T(8,128)(2,1)}, bf16[128,1024]{1,0:T(8,128)(2,1)S(1)}, u32[]{:S(2)}, u32[]{:S(2)}) collective-permute-start(bf16[128,1024]{1,0:T(8,128)(2,1)} %bitcast.13), channel_id=1, source_target_pairs={{0,2},{1,3},{2,0},{3,1},{4,6},{5,7},{6,4},{7,5},{8,10},{9,11},{10,... | collective-permute-start | bytes 786440 | tf_op jit(solution)/shard_map/ppermute | solution.py:258
  11.0 11.3 %collective-permute-start.7 = (bf16[128,1024]{1,0:T(8,128)(2,1)S(1)}, bf16[128,1024]{1,0:T(8,128)(2,1)S(1)}, u32[]{:S(2)}, u32[]{:S(2)}) collective-permute-start(bf16[128,1024]{1,0:T(8,128)(2,1)S(1)} %collective-permute-done.6.refs_1_.refs_9_), channel_id=1, source_target_pairs={{0,4},{1,5},{2,14},{3,15},{4,8},{5,9},{6,2},{7,3},{8,12},{9,13},{1... | collective-permute-start | bytes 786440 | tf_op jit(solution)/shard_map/ppermute | solution.py:258
  13.2 12.0 %collective-permute-start.3 = (bf16[128,1024]{1,0:T(8,128)(2,1)S(1)}, bf16[128,1024]{1,0:T(8,128)(2,1)S(1)}, u32[]{:S(2)}, u32[]{:S(2)}) collective-permute-start(bf16[128,1024]{1,0:T(8,128)(2,1)S(1)} %collective-permute-done.2.refs_0_.refs_8_), channel_id=1, source_target_pairs={{0,4},{1,13},{2,6},{3,15},{4,8},{5,1},{6,10},{7,3},{8,12},{9,5},{1... | collective-permute-start | bytes 786440 | tf_op jit(solution)/shard_map/ppermute | solution.py:258
  17.3 7.8 %collective-permute-start.13 = (bf16[128,1024]{1,0:T(8,128)(2,1)S(1)}, bf16[128,1024]{1,0:T(8,128)(2,1)S(1)}, u32[]{:S(2)}, u32[]{:S(2)}) collective-permute-start(bf16[128,1024]{1,0:T(8,128)(2,1)S(1)} %collective-permute-done.5.refs_5_), channel_id=1, source_target_pairs={{0,16},{16,0},{1,17},{17,1},{2,18},{18,2},{3,19},{19,3},{4,20},{20... | collective-permute-start | bytes 786440 | tf_op jit(solution)/shard_map/ppermute | solution.py:261
  17.3 9.1 %collective-permute-start.15 = (bf16[128,1024]{1,0:T(8,128)(2,1)S(1)}, bf16[128,1024]{1,0:T(8,128)(2,1)S(1)}, u32[]{:S(2)}, u32[]{:S(2)}) collective-permute-start(bf16[128,1024]{1,0:T(8,128)(2,1)S(1)} %collective-permute-done.2.refs_0_.refs_8_), channel_id=1, source_target_pairs={{0,2},{1,3},{2,0},{3,1},{4,6},{5,7},{6,4},{7,5},{8,10},{9,11},{10,... | collective-permute-start | bytes 786440 | tf_op jit(solution)/shard_map/ppermute | solution.py:258
  17.7 8.7 %collective-permute-start.14 = (bf16[128,1024]{1,0:T(8,128)(2,1)S(1)}, bf16[128,1024]{1,0:T(8,128)(2,1)S(1)}, u32[]{:S(2)}, u32[]{:S(2)}) collective-permute-start(bf16[128,1024]{1,0:T(8,128)(2,1)S(1)} %collective-permute-done.1.refs_7_), channel_id=1, source_target_pairs={{0,16},{16,0},{1,17},{17,1},{2,18},{18,2},{3,19},{19,3},{4,20},{20... | collective-permute-start | bytes 786440 | tf_op jit(solution)/shard_map/ppermute | solution.py:261
  17.9 1.0 %copy-start = (bf16[1,128,1024]{2,1,0:T(8,128)(2,1)S(1)}, bf16[1,128,1024]{2,1,0:T(8,128)(2,1)}, u32[]{:S(2)}) copy-start(bf16[1,128,1024]{2,1,0:T(8,128)(2,1)} %param.6) | copy-start | bytes 786436
  18.8 0.9 %copy-start.1 = (bf16[1,128,1024]{2,1,0:T(8,128)(2,1)S(1)}, bf16[1,128,1024]{2,1,0:T(8,128)(2,1)}, u32[]{:S(2)}) copy-start(bf16[1,128,1024]{2,1,0:T(8,128)(2,1)} %param.5) | copy-start | bytes 786436
  22.3 7.0 %collective-permute-start.8 = (bf16[128,1024]{1,0:T(8,128)(2,1)S(1)}, bf16[128,1024]{1,0:T(8,128)(2,1)S(1)}, u32[]{:S(2)}, u32[]{:S(2)}) collective-permute-start(bf16[128,1024]{1,0:T(8,128)(2,1)S(1)} %collective-permute-done.7.refs_3_.refs_11_), channel_id=1, source_target_pairs={{0,1},{1,0},{2,3},{3,2},{4,5},{5,4},{6,7},{7,6},{8,9},{9,8},{10,11... | collective-permute-start | bytes 786440 | tf_op jit(solution)/shard_map/ppermute | solution.py:258
  25.1 12.6 %collective-permute-start.11 = (bf16[128,1024]{1,0:T(8,128)(2,1)S(1)}, bf16[128,1024]{1,0:T(8,128)(2,1)S(1)}, u32[]{:S(2)}, u32[]{:S(2)}) collective-permute-start(bf16[128,1024]{1,0:T(8,128)(2,1)S(1)} %collective-permute-done.5.refs_5_), channel_id=1, source_target_pairs={{0,4},{1,13},{2,6},{3,15},{4,8},{5,1},{6,10},{7,3},{8,12},{9,5},{1... | collective-permute-start | bytes 786440 | tf_op jit(solution)/shard_map/ppermute | solution.py:258
  25.1 13.0 %collective-permute-start.4 = (bf16[128,1024]{1,0:T(8,128)(2,1)S(1)}, bf16[128,1024]{1,0:T(8,128)(2,1)S(1)}, u32[]{:S(2)}, u32[]{:S(2)}) collective-permute-start(bf16[128,1024]{1,0:T(8,128)(2,1)S(1)} %collective-permute-done.1.refs_7_), channel_id=1, source_target_pairs={{0,4},{1,5},{2,14},{3,15},{4,8},{5,9},{6,2},{7,3},{8,12},{9,13},{1... | collective-permute-start | bytes 786440 | tf_op jit(solution)/shard_map/ppermute | solution.py:258
  29.7 4.4 %collective-permute-start.17 = (f32[8,128]{1,0:T(8,128)S(1)}, f32[8,128]{1,0:T(8,128)S(1)}, u32[]{:S(2)}, u32[]{:S(2)}) collective-permute-start(f32[8,128]{1,0:T(8,128)S(1)} %get-tuple-element.37), channel_id=1, source_target_pairs={{0,2},{1,3},{2,0},{3,1},{4,6},{5,7},{6,4},{7,5},{8,10},{9,11},{10,... | collective-permute-start | bytes 12296 | tf_op jit(solution)/shard_map/ppermute | solution.py:258
  32.5 4.4 %collective-permute-start.16 = (f32[8,128]{1,0:T(8,128)S(1)}, f32[8,128]{1,0:T(8,128)S(1)}, u32[]{:S(2)}, u32[]{:S(2)}) collective-permute-start(f32[8,128]{1,0:T(8,128)S(1)} %get-tuple-element.37), channel_id=1, source_target_pairs={{0,1},{1,0},{2,3},{3,2},{4,5},{5,4},{6,7},{7,6},{8,9},{9,8},{10,11... | collective-permute-start | bytes 12296 | tf_op jit(solution)/shard_map/ppermute | solution.py:258
  34.0 3.6 %collective-permute-start.18 = (f32[8,128]{1,0:T(8,128)S(1)}, f32[8,128]{1,0:T(8,128)S(1)}, u32[]{:S(2)}, u32[]{:S(2)}) collective-permute-start(f32[8,128]{1,0:T(8,128)S(1)} %collective-permute-done.17), channel_id=1, source_target_pairs={{0,1},{1,0},{2,3},{3,2},{4,5},{5,4},{6,7},{7,6},{8,9},{9,8},{10,11... | collective-permute-start | bytes 12296 | tf_op jit(solution)/shard_map/ppermute | solution.py:258
  35.0 9.3 %collective-permute-start.9 = (bf16[128,1024]{1,0:T(8,128)(2,1)S(1)}, bf16[128,1024]{1,0:T(8,128)(2,1)S(1)}, u32[]{:S(2)}, u32[]{:S(2)}) collective-permute-start(bf16[128,1024]{1,0:T(8,128)(2,1)S(1)} %collective-permute-done.5.refs_5_), channel_id=1, source_target_pairs={{0,2},{1,3},{2,0},{3,1},{4,6},{5,7},{6,4},{7,5},{8,10},{9,11},{10,... | collective-permute-start | bytes 786440 | tf_op jit(solution)/shard_map/ppermute | solution.py:258
  38.2 6.8 %collective-permute-start.19 = (bf16[128,1024]{1,0:T(8,128)(2,1)S(1)}, bf16[128,1024]{1,0:T(8,128)(2,1)S(1)}, u32[]{:S(2)}, u32[]{:S(2)}) collective-permute-start(bf16[128,1024]{1,0:T(8,128)(2,1)S(1)} %collective-permute-done.4.refs_0_.refs_8_), channel_id=1, source_target_pairs={{0,1},{1,0},{2,3},{3,2},{4,5},{5,4},{6,7},{7,6},{8,9},{9,8},{10,11... | collective-permute-start | bytes 786440 | tf_op jit(solution)/shard_map/ppermute | solution.py:258
  39.2 3.8 %collective-permute-start.21 = (f32[4,8,128]{2,1,0:T(8,128)S(1)}, f32[4,8,128]{2,1,0:T(8,128)S(1)}, u32[]{:S(2)}, u32[]{:S(2)}) collective-permute-start(f32[4,8,128]{2,1,0:T(8,128)S(1)} %pad_maximum_fusion.refs_5_.refs_2_), channel_id=1, source_target_pairs={{0,16},{16,0},{1,17},{17,1},{2,18},{18,2},{3,19},{19,3},{4,20},{20... | collective-permute-start | bytes 49160 | tf_op jit(solution)/shard_map/ppermute | solution.py:261
  39.2 5.7 %collective-permute-start.24 = (f32[4,8,128]{2,1,0:T(8,128)S(1)}, f32[4,8,128]{2,1,0:T(8,128)S(1)}, u32[]{:S(2)}, u32[]{:S(2)}) collective-permute-start(f32[4,8,128]{2,1,0:T(8,128)S(1)} %pad_maximum_fusion.refs_5_.refs_2_), channel_id=1, source_target_pairs={{0,4},{1,5},{2,6},{3,7},{4,8},{5,9},{6,10},{7,11},{8,12},{9,13},{1... | collective-permute-start | bytes 49160 | tf_op jit(solution)/shard_map/ppermute | solution.py:258
  40.5 4.9 %collective-permute-start.26 = (f32[4,8,128]{2,1,0:T(8,128)S(1)}, f32[4,8,128]{2,1,0:T(8,128)S(1)}, u32[]{:S(2)}, u32[]{:S(2)}) collective-permute-start(f32[4,8,128]{2,1,0:T(8,128)S(1)} %pad_maximum_fusion.refs_5_.refs_2_), channel_id=1, source_target_pairs={{0,12},{1,13},{2,14},{3,15},{4,0},{5,1},{6,2},{7,3},{8,4},{9,5},{1... | collective-permute-start | bytes 49160 | tf_op jit(solution)/shard_map/ppermute | solution.py:258
  44.3 1.6 %collective-permute-start.22 = (bf16[128,1024]{1,0:T(8,128)(2,1)S(1)}, bf16[128,1024]{1,0:T(8,128)(2,1)S(1)}, u32[]{:S(2)}, u32[]{:S(2)}) collective-permute-start(bf16[128,1024]{1,0:T(8,128)(2,1)S(1)} %collective-permute-done.9.refs_9_), channel_id=1, source_target_pairs={{0,16},{16,0},{1,17},{17,1},{2,18},{18,2},{3,19},{19,3},{4,20},{20... | collective-permute-start | bytes 786440 | tf_op jit(solution)/shard_map/ppermute | solution.py:261
  44.4 1.9 %collective-permute-start.12 = (bf16[128,1024]{1,0:T(8,128)(2,1)S(1)}, bf16[128,1024]{1,0:T(8,128)(2,1)S(1)}, u32[]{:S(2)}, u32[]{:S(2)}) collective-permute-start(bf16[128,1024]{1,0:T(8,128)(2,1)S(1)} %collective-permute-done.11.refs_2_.refs_10_), channel_id=1, source_target_pairs={{0,16},{16,0},{1,17},{17,1},{2,18},{18,2},{3,19},{19,3},{4,20},{20... | collective-permute-start | bytes 786440 | tf_op jit(solution)/shard_map/ppermute | solution.py:261
  44.9 2.8 %collective-permute-start.10 = (bf16[128,1024]{1,0:T(8,128)(2,1)S(1)}, bf16[128,1024]{1,0:T(8,128)(2,1)S(1)}, u32[]{:S(2)}, u32[]{:S(2)}) collective-permute-start(bf16[128,1024]{1,0:T(8,128)(2,1)S(1)} %collective-permute-done.4.refs_0_.refs_8_), channel_id=1, source_target_pairs={{0,16},{16,0},{1,17},{17,1},{2,18},{18,2},{3,19},{19,3},{4,20},{20... | collective-permute-start | bytes 786440 | tf_op jit(solution)/shard_map/ppermute | solution.py:261
  44.9 2.7 %collective-permute-start.20 = (bf16[128,1024]{1,0:T(8,128)(2,1)S(1)}, bf16[128,1024]{1,0:T(8,128)(2,1)S(1)}, u32[]{:S(2)}, u32[]{:S(2)}) collective-permute-start(bf16[128,1024]{1,0:T(8,128)(2,1)S(1)} %collective-permute-done.19.refs_4_.refs_12_), channel_id=1, source_target_pairs={{0,16},{16,0},{1,17},{17,1},{2,18},{18,2},{3,19},{19,3},{4,20},{20... | collective-permute-start | bytes 786440 | tf_op jit(solution)/shard_map/ppermute | solution.py:261
  45.4 2.9 %collective-permute-start.23 = (bf16[128,1024]{1,0:T(8,128)(2,1)S(1)}, bf16[128,1024]{1,0:T(8,128)(2,1)S(1)}, u32[]{:S(2)}, u32[]{:S(2)}) collective-permute-start(bf16[128,1024]{1,0:T(8,128)(2,1)S(1)} %get-tuple-element.45), channel_id=1, source_target_pairs={{0,16},{16,0},{1,17},{17,1},{2,18},{18,2},{3,19},{19,3},{4,20},{20... | collective-permute-start | bytes 786440 | tf_op jit(solution)/shard_map/ppermute | solution.py:261
  45.9 2.4 %collective-permute-start.25 = (f32[4,8,128]{2,1,0:T(8,128)S(1)}, f32[4,8,128]{2,1,0:T(8,128)S(1)}, u32[]{:S(2)}, u32[]{:S(2)}) collective-permute-start(f32[4,8,128]{2,1,0:T(8,128)S(1)} %collective-permute-done.24.refs_4_), channel_id=1, source_target_pairs={{0,16},{16,0},{1,17},{17,1},{2,18},{18,2},{3,19},{19,3},{4,20},{20... | collective-permute-start | bytes 49160 | tf_op jit(solution)/shard_map/ppermute | solution.py:261
  46.3 2.0 %collective-permute-start.27 = (f32[4,8,128]{2,1,0:T(8,128)S(1)}, f32[4,8,128]{2,1,0:T(8,128)S(1)}, u32[]{:S(2)}, u32[]{:S(2)}) collective-permute-start(f32[4,8,128]{2,1,0:T(8,128)S(1)} %collective-permute-done.26.refs_6_), channel_id=1, source_target_pairs={{0,16},{16,0},{1,17},{17,1},{2,18},{18,2},{3,19},{19,3},{4,20},{20... | collective-permute-start | bytes 49160 | tf_op jit(solution)/shard_map/ppermute | solution.py:261
